TPU v7x, 256 devices: a whole 4x4x8 slice. The times are simulated.
256 devices in a mesh: slab: 64 (over z, x, core), dom: 4 (over y).
Axes of the slice: x: 4, y: 4, z: 8, core: 2. Of those that a mesh axis runs over, the one named last changes fastest.
Arguments:
- elem_grad: float32 [3, 8, 1376256], P(None, None, ('slab', 'dom')), may hold values from -3 to 3
- elem_stress: float32 [6, 1376256], P(None, ('slab', 'dom')), may hold values from -6 to 6
- elem_grade: int32 [1376256], P(('slab', 'dom')), may hold values from 0 to 15
- grade_scale: float32 [16], replicated, may hold values from 0.5 to 2
- part_counts: int32 [64, 4], P('slab'), may hold values from 1 to 5376, as said below
- node_lists: int32 [4, 128, 8, 512], P(None, 'slab', None, 'dom'), may hold values from -1 to 7167, as said below
- stiff_diag: float32 [3, 128, 8, 512], P(None, 'slab', None, 'dom'), may hold values from 1 to 4
- start_block: float32 [3, 32, 128, 8, 512], P(None, None, 'slab', None, 'dom'), may hold values from -600 to 600
Outputs:
- next_block: float32 [3, 32, 128, 8, 512], P(None, None, 'slab', None, 'dom')
- diag_blocks: float32 [2, 32, 32], replicated
- offdiag_blocks: float32 [3, 32, 32], replicated
Inputs may be any that keep to these rules, and one draw needn't show every extreme that they name: `part_counts`: each row sums to 7168, the elements of one slab; in every slab one partition holds exactly 5376. node_lists[j, f, x, y] is the pool number, within the slab of floor f, of the element of layer f whose in-plane base corner is (x - j mod 2, (y - j // 2) mod 512); it is -1 exactly where x - j mod 2 lies outside 0 to 6. Every element of a slab appears at its four in-plane corners.
All inputs are finite; a program needn't handle non-finite values.
Results may differ from a plain program's by a relative error of at most 0.0003.
Values sent between devices are 32-bit elements; how exact they have to be, the bound alone decides.
No kernel may reach another device: no remote copies, remote signals or barrier semaphores. Data moves between devices by JAX's collectives and lax.ppermute only.
A program may use at most 128 MiB of HBM per device.

v0:
```python
import jax
import jax.numpy as jnp
import numpy as np
from jax import lax
from jax.sharding import PartitionSpec as P

highest = lax.Precision.HIGHEST


def extended_2(cells, sides, width):
    for axis, dim in sides:
        count = lax.axis_size(axis)
        ends = count - 1
        head = lax.slice_in_dim(cells, 0, width, axis=dim)
        tail = lax.slice_in_dim(cells, cells.shape[dim] - width, cells.shape[dim], axis=dim)
        cells = jnp.concatenate(
            [
                lax.ppermute(tail, axis, [(i, (i + 1) % count) for i in range(ends)]),
                cells,
                lax.ppermute(head, axis, [((i + 1) % count, i) for i in range(ends)]),
            ],
            axis=dim,
        )
    return cells


def from_behind(value, axis, steps):
    count = lax.axis_size(axis)
    pairs = [(source, (source + steps) % count) for source in range(count)]
    return lax.ppermute(value, axis, pairs)


def passed_along(block, axis, distance):
    devices = range(lax.axis_size(axis))
    route = [(i - distance, i) for i in devices if i - distance in devices]
    return lax.ppermute(block, axis, route)


def offset_table(quad_slot, layer_side):
    table = np.zeros((8, 27))
    shift_x = quad_slot % 2
    shift_y = quad_slot // 2
    for corner in range(8):
        corner_x = corner % 2
        corner_y = corner // 2 % 2
        corner_z = corner // 4
        target = (
            corner_x - shift_x + 1 + 3 * (corner_y - shift_y + 1) + 9 * (corner_z - layer_side + 1)
        )
        table[corner, target] = 1.0
    return jnp.asarray(table, dtype=jnp.float32)


def stress_matrix(stress):
    return jnp.stack(
        [
            jnp.stack([stress[0], stress[5], stress[4]]),
            jnp.stack([stress[5], stress[1], stress[3]]),
            jnp.stack([stress[4], stress[3], stress[2]]),
        ]
    )


def grade_lookup(grades, table):
    levels = jnp.arange(table.shape[0], dtype=jnp.int32)[:, None]
    onehot = (grades[None, :] == levels).astype(jnp.float32)
    return jnp.dot(table, onehot, precision=highest)


def element_matrices(gradients, stress, scales):
    pushed = jnp.einsum("ik...,kb...->ib...", stress_matrix(stress), gradients, precision=highest)
    return jnp.einsum("ia...,ib...->ab...", gradients, pushed, precision=highest) * scales


def pool_columns(slot_lists, counts, capacity):
    offsets = jnp.cumsum(counts) - counts
    shaped = offsets.reshape((-1,) + (1,) * slot_lists.ndim)
    pool_ids = jnp.maximum(slot_lists, 0)
    partition = jnp.sum((pool_ids[None] >= shaped[1:]).astype(jnp.int32), axis=0)
    levels = jnp.arange(counts.shape[0], dtype=jnp.int32).reshape(shaped.shape)
    starts = jnp.sum(jnp.where(partition[None] == levels, shaped, 0), axis=0)
    columns = partition * capacity + pool_ids - starts
    return (columns, (slot_lists >= 0).astype(jnp.float32))


def accumulate(getter, present):
    sides = []
    for layer_side in range(2):
        summed = None
        for quad_slot in range(4):
            row_values = getter(quad_slot, layer_side) * present[quad_slot]
            contribution = jnp.einsum(
                "bfxy,bo->ofxy", row_values, offset_table(quad_slot, layer_side), precision=highest
            )
            summed = contribution if summed is None else summed + contribution
        sides.append(summed)
    return (sides[0], sides[1])


def apply_operator(block, stencil, diagonal):
    extended = extended_2(block, (("slab", 2),), 1)
    edge_shape = extended.shape[:4]
    first_column = extended[..., 0].reshape(-1)
    last_column = extended[..., -1].reshape(-1)
    from_left = from_behind(last_column, "dom", 1).reshape(edge_shape + (1,))
    from_right = from_behind(first_column, "dom", -1).reshape(edge_shape + (1,))
    extended = jnp.concatenate([from_left, extended, from_right], axis=4)
    padded = jnp.pad(extended, ((0, 0), (0, 0), (0, 0), (1, 1), (0, 0)))
    floors, across, beside_all = (block.shape[2], block.shape[3], block.shape[4])
    result = diagonal[:, None] * block
    for offset in range(27):
        step_x = offset % 3
        step_y = offset // 3 % 3
        step_z = offset // 9
        result = (
            result
            + stencil[offset]
            * padded[
                :,
                :,
                step_z : step_z + floors,
                step_x : step_x + across,
                step_y : step_y + beside_all,
            ]
        )
    return result


def local_inner(first_block, second_block):
    return jnp.einsum("cvfxy,cwfxy->vw", first_block, second_block, precision=highest)


def mix(block, matrix):
    return jnp.einsum("cvfxy,vw->cwfxy", block, matrix, precision=highest)


def normalize(block, gram_matrix):
    factor = jnp.linalg.cholesky(gram_matrix)
    identity = jnp.eye(gram_matrix.shape[0], dtype=jnp.float32)
    inverse = lax.linalg.triangular_solve(factor, identity, left_side=True, lower=True)
    return (jnp.einsum("cvfxy,wv->cwfxy", block, inverse, precision=highest), factor.T)


def advance(basis_block, image_block, dof_count):
    projection = lax.psum(local_inner(basis_block, image_block), ("slab", "dom")) / dof_count
    residual = image_block - mix(basis_block, projection)
    gram_matrix = lax.psum(local_inner(residual, residual), ("slab", "dom")) / dof_count
    following, upper_factor = normalize(residual, gram_matrix)
    return (following, projection, upper_factor)


def per_device(
    elem_grad,
    elem_stress,
    elem_grade,
    grade_scale,
    part_counts,
    node_lists,
    stiff_diag,
    start_block,
):
    capacity = elem_grad.shape[2]
    counts = part_counts[0]
    columns, present = pool_columns(node_lists, counts, capacity)
    flat_columns = columns.reshape(-1)
    slot_shape = node_lists.shape
    scales = grade_lookup(elem_grade, grade_scale)
    matrices = element_matrices(elem_grad, elem_stress, scales).reshape(64, capacity)
    shard_piece = lax.all_gather(matrices, "dom", axis=1, tiled=True)
    inside = (flat_columns >= 0) & (flat_columns < shard_piece.shape[1])
    selected = jnp.take(shard_piece, jnp.clip(flat_columns, 0, shard_piece.shape[1] - 1), axis=1)
    picked = jnp.where(inside[None, :], selected, 0.0)
    picked = picked.reshape((8, 8) + slot_shape)

    def getter(quad_slot, layer_side):
        return picked[quad_slot + 4 * layer_side, :, quad_slot]

    bottom, top_side = accumulate(getter, present)
    below = passed_along(bottom[:, 0], "slab", -1)
    stencil = top_side + jnp.concatenate([bottom[:, 1:], below[:, None]], axis=1)
    dof_count = (
        3
        * start_block.shape[2]
        * start_block.shape[3]
        * start_block.shape[4]
        * lax.axis_size("slab")
        * lax.axis_size("dom")
    )
    start_gram = lax.psum(local_inner(start_block, start_block), ("slab", "dom")) / dof_count
    first, start_factor = normalize(start_block, start_gram)
    image_block = apply_operator(first, stencil, stiff_diag)
    second, alpha_one, beta_one = advance(first, image_block, dof_count)
    image_block = apply_operator(second, stencil, stiff_diag) - mix(first, beta_one.T)
    third, alpha_two, beta_two = advance(second, image_block, dof_count)
    return (third, jnp.stack([alpha_one, alpha_two]), jnp.stack([start_factor, beta_one, beta_two]))


def solution(mesh):
    in_specs = (
        P(None, None, ("slab", "dom")),
        P(None, ("slab", "dom")),
        P(("slab", "dom")),
        P(),
        P("slab", None),
        P(None, "slab", None, "dom"),
        P(None, "slab", None, "dom"),
        P(None, None, "slab", None, "dom"),
    )
    out_specs = (P(None, None, "slab", None, "dom"), P(), P())
    return jax.shard_map(
        per_device, mesh=mesh, in_specs=in_specs, out_specs=out_specs, check_vma=False
    )
```

profile of v0, /device:TPU:8, one launch (start us, length us, event | category | flops | bytes accessed | tf_op | source)
XLA Modules:
  0.0 704.1 jit_solution(14707492040384633531)
XLA Ops:
  7.2 1.7 fusion.143
  9.1 7.5 %copy.136 = f32[3,3,5376]{1,0,2:T(4,128)} copy(f32[3,3,5376]{2,1,0:T(4,128)S(1)} %pad_maximum_fusion.18) | data formatting | bytes 387072 | tf_op jit(solution)/shard_map/stack | solution.py:55
  16.6 7.2 %copy.137 = f32[3,8,5376]{1,0,2:T(4,128)} copy(f32[3,8,5376]{2,1,0:T(8,128)S(1)} %copy-done.12) | data formatting | bytes 1032192 | tf_op args[0]
  23.9 39.3 %fusion.144 = f32[5376,3,8]{2,1,0:T(4,128)S(1)} fusion(f32[3,3,5376]{1,0,2:T(4,128)} %copy.136, f32[3,8,5376]{1,0,2:T(4,128)} %copy.137), kind=kOutput, calls=%fused_computation.282 | convolution fusion | flops 4644864 | bytes 1225728 | tf_op jit(solution)/shard_map/ik...,kb...->ib.../dot_general | solution.py:71
  63.5 57.7 %multiply_bitcast_fusion = f32[8,8,5376]{0,1,2:T(8,128)} fusion(f32[5376]{0:T(1024)S(1)} %convolution_reduce_fusion, f32[3,8,5376]{1,0,2:T(4,128)S(1)} %copy-done.2, f32[5376,3,8]{2,1,0:T(4,128)S(1)} %fusion.144), kind=kOutput, calls=%fused_computation.1 | convolution fusion | flops 12730368 | bytes 2429952 | tf_op jit(solution)/shard_map/ia...,ib...->ab.../dot_general | solution.py:72
  121.2 12.2 %copy.139 = f32[8,8,5376]{2,1,0:T(8,128)S(1)} copy(f32[8,8,5376]{0,1,2:T(8,128)} %multiply_bitcast_fusion) | data formatting | bytes 2752512 | tf_op jit(solution)/shard_map/mul | solution.py:72
  133.4 2.1 copy.140
  136.5 78.8 %psum.35 = f32[32,32]{0,1:T(8,128)S(1)} all-reduce(f32[32,32]{0,1:T(8,128)S(1)} %convolution_bitcast_fusion.10), channel_id=1, replica_groups=mesh['slab'=64,'dom'=4] {'slab','dom'}, use_global_device_ids=true, to_apply=%region_0.0 | all-reduce | flops 1024 | bytes 8192 | tf_op jit(solution)/shard_map/psum | solution.py:189
  215.4 2.9 cholesky.59
  220.3 2.4 custom-call.7
  224.0 1.8 collective-permute-start.1
  225.8 1.5 collective-permute-start.2
  229.0 1.7 collective-permute-done.2
  230.8 1.7 fusion.137
  232.6 3.8 copy.154
  237.3 2.4 copy.155
  242.1 2.3 copy.156
  244.7 3.5 copy.157
  248.2 4.5 select_maximum_fusion.4
  252.7 31.8 %gather_fusion = f32[8192,64]{1,0:T(8,128)} fusion(f32[64,21504]{0,1:T(8,128)} %all-gather.2.cloned.1.call-done, s32[8192]{0:T(1024)S(1)} %copy-done.13), kind=kCustom, calls=%fused_computation | custom fusion | bytes 4227072 | tf_op jit(solution)/shard_map/jit(_take)/gather | solution.py:171
  284.6 3.8 copy.141
  288.4 2.0 copy.205
  292.6 1.5 collective-permute-start
  295.4 5.8 collective-permute-done
  302.1 5.3 fusion.41
  308.5 86.8 %psum.36 = f32[32,32]{0,1:T(8,128)S(1)} all-reduce(f32[32,32]{0,1:T(8,128)S(1)} %convolution_bitcast_fusion.9), channel_id=1, replica_groups=mesh['slab'=64,'dom'=4] {'slab','dom'}, use_global_device_ids=true, to_apply=%region_6.9 | all-reduce | flops 1024 | bytes 8192 | tf_op jit(solution)/shard_map/psum | solution.py:145
  396.9 73.4 %psum.37 = f32[32,32]{0,1:T(8,128)S(1)} all-reduce(f32[32,32]{0,1:T(8,128)S(1)} %convolution_bitcast_fusion.8), channel_id=1, replica_groups=mesh['slab'=64,'dom'=4] {'slab','dom'}, use_global_device_ids=true, to_apply=%region_7.10 | all-reduce | flops 1024 | bytes 8192 | tf_op jit(solution)/shard_map/psum | solution.py:147
  470.4 2.9 cholesky.70
  475.4 2.4 custom-call.8
  478.9 1.8 collective-permute-start.5
  482.1 2.3 collective-permute-done.6
  485.2 1.7 fusion.136
  487.0 4.4 copy.163
  491.4 1.7 reshape_squeeze.14
  493.1 1.9 collective-permute-start.7
  494.9 3.0 copy.164
  497.9 1.7 reshape_squeeze.15
  500.8 1.6 reshape.147
  502.4 3.2 copy.165
  505.7 1.6 reshape.148
  507.3 4.4 copy.166
  512.0 3.4 select_maximum_fusion
  515.7 7.2 %fusion.10 = f32[3,32,2,8,128]{4,1,3,2,0:T(8,128)S(1)} fusion(f32[3,32,4,10,130]{4,1,3,2,0:T(8,128)S(1)} %select_maximum_fusion, f32[3,32,4,8,1]{4,1,3,2,0:T(8,128)S(1)} %copy-done.5, f32[3,32,1,8,128]{4,1,3,2,0:T(8,128)S(1)} %copy-done.11, f32[3,32,2,8,128]{4,1,3,2,0:T(8,128)S(1)} %convolution_bitcast_fusion.3, ...), kind=kOutput, calls=%fused_computation.45 | convolution fusion | flops 90442752 | bytes 17575936 | tf_op jit(solution)/shard_map/cvfxy,vw->cwfxy/dot_general | solution.py:134
  524.5 85.6 %psum.38 = f32[32,32]{0,1:T(8,128)S(1)} all-reduce(f32[32,32]{0,1:T(8,128)S(1)} %convolution_bitcast_fusion.7), channel_id=1, replica_groups=mesh['slab'=64,'dom'=4] {'slab','dom'}, use_global_device_ids=true, to_apply=%region_8.11 | all-reduce | flops 1024 | bytes 8192 | tf_op jit(solution)/shard_map/psum | solution.py:145
  610.1 1.9 fusion.5
  612.9 73.6 %psum.39 = f32[32,32]{0,1:T(8,128)S(1)} all-reduce(f32[32,32]{0,1:T(8,128)S(1)} %convolution_bitcast_fusion.6), channel_id=1, replica_groups=mesh['slab'=64,'dom'=4] {'slab','dom'}, use_global_device_ids=true, to_apply=%region_9.12 | all-reduce | flops 1024 | bytes 8192 | tf_op jit(solution)/shard_map/psum | solution.py:147
  686.6 2.9 cholesky.81
  692.3 2.4 custom-call.9
  (268 shorter events, 30.8 us)
Async XLA Ops:
  7.2 56.1 %copy-start = (f32[16]{0:T(128)S(1)}, f32[16]{0:T(128)}, u32[]{:S(2)}) copy-start(f32[16]{0:T(128)} %param.22) | copy-start | bytes 196
  7.2 245.5 %all-gather.2.cloned.1.call-start = ((), (), s32[]{:S(2)}) async-start(), calls=%async_computation | async-start | bytes 13762560 | tf_op jit(solution)/shard_map/all_gather | solution.py:169
  9.1 7.5 %copy-start.12 = (f32[3,8,5376]{2,1,0:T(8,128)S(1)}, f32[3,8,5376]{2,1,0:T(8,128)}, u32[]{:S(2)}) copy-start(f32[3,8,5376]{2,1,0:T(8,128)} %param.19) | copy-start | bytes 1548292
  23.9 39.4 %copy-start.89 = (s32[5376]{0:T(1024)S(1)}, s32[5376]{0:T(1024)}, u32[]{:S(2)}) copy-start(s32[5376]{0:T(1024)} %param.21) | copy-start | bytes 64516
  23.9 39.6 %copy-start.2 = (f32[3,8,5376]{1,0,2:T(4,128)S(1)}, f32[3,8,5376]{1,0,2:T(4,128)}, u32[]{:S(2)}) copy-start(f32[3,8,5376]{1,0,2:T(4,128)} %copy.137) | copy-start | bytes 1548292
  135.6 91.7 %copy-start.90 = (s32[1,4]{1,0:T(1,128)S(1)}, s32[1,4]{1,0:T(1,128)}, u32[]{:S(2)}) copy-start(s32[1,4]{1,0:T(1,128)} %param.23) | copy-start | bytes 52
  135.6 92.0 %copy-start.14 = (s32[4,2,8,128]{3,2,1,0:T(8,128)S(1)}, s32[4,2,8,128]{3,2,1,0:T(8,128)}, u32[]{:S(2)}) copy-start(s32[4,2,8,128]{3,2,1,0:T(8,128)} %param.24) | copy-start | bytes 98308
  224.0 5.1 collective-permute-start.1
  225.8 4.9 collective-permute-start.2
  230.7 17.5 %copy-start.6 = (f32[3,32,1,8,128]{4,1,3,2,0:T(8,128)}, f32[3,32,1,8,128]{4,1,3,2,0:T(8,128)S(1)}, u32[]{:S(2)}) copy-start(f32[3,32,1,8,128]{4,1,3,2,0:T(8,128)S(1)} %collective-permute-done.2) | copy-start | bytes 1179652
  230.8 10.4 %copy-start.15 = (f32[4,2,8,128]{3,2,1,0:T(8,128)S(1)}, f32[4,2,8,128]{3,2,1,0:T(8,128)}, u32[]{:S(2)}) copy-start(f32[4,2,8,128]{3,2,1,0:T(8,128)} %get-tuple-element.80) | copy-start | bytes 98308
  236.5 5.3 collective-permute-start.3
  239.9 4.6 collective-permute-start.4
  284.5 5.9 copy-start.78
  290.5 10.7 %copy-start.81 = (f32[8,27,1,1]{1,0,3,2:T(8,128)S(1)}, f32[8,27,1,1]{1,0,3,2:T(8,128)}, u32[]{:S(2)}) copy-start(f32[8,27,1,1]{1,0,3,2:T(8,128)} %constant.100) | copy-start | bytes 2596
  290.8 11.3 %copy-start.3 = (f32[3,32,4,10,130]{4,1,3,2,0:T(8,128)S(1)}, f32[3,32,4,10,130]{4,1,3,2,0:T(8,128)}, u32[]{:S(2)}) copy-start(f32[3,32,4,10,130]{4,1,3,2,0:T(8,128)} %select_maximum_fusion.4) | copy-start | bytes 5990404
  290.8 11.3 %copy-start.4 = (f32[3,32,4,8,1]{4,1,3,2,0:T(8,128)S(1)}, f32[3,32,4,8,1]{4,1,3,2,0:T(8,128)}, u32[]{:S(2)}) copy-start(f32[3,32,4,8,1]{4,1,3,2,0:T(8,128)} %copy.157) | copy-start | bytes 36868
  290.8 11.3 %copy-start.7 = (f32[3,32,1,8,128]{4,1,3,2,0:T(8,128)S(1)}, f32[3,32,1,8,128]{4,1,3,2,0:T(8,128)}, u32[]{:S(2)}) copy-start(f32[3,32,1,8,128]{4,1,3,2,0:T(8,128)} %copy-done.6) | copy-start | bytes 1179652
  290.8 11.3 %copy-start.79 = (f32[3,2,8,128]{3,2,1,0:T(8,128)S(1)}, f32[3,2,8,128]{3,2,1,0:T(8,128)}, u32[]{:S(2)}) copy-start(f32[3,2,8,128]{3,2,1,0:T(8,128)} %param.25) | copy-start | bytes 73732
  292.6 8.6 %collective-permute-start = (f32[27,8,128]{2,0,1:T(8,128)S(1)}, f32[27,8,128]{2,0,1:T(8,128)S(1)}, u32[]{:S(2)}, u32[]{:S(2)}) collective-permute-start(f32[27,8,128]{2,0,1:T(8,128)S(1)} %get-tuple-element.69), channel_id=1, source_target_pairs={{4,0},{8,4},{12,8},{16,12},{20,16},{24,20},{28,24},{32,28},{36,32}... | collective-permute-start | bytes 331784 | tf_op jit(solution)/shard_map/ppermute | solution.py:36
  301.7 5.7 copy-start.21
  301.7 5.7 copy-start.23
  301.7 5.7 copy-start.25
  301.7 5.7 copy-start.27
  301.7 5.7 copy-start.29
  301.7 5.7 copy-start.31
  301.8 5.7 copy-start.33
  301.8 5.7 copy-start.35
  301.8 5.7 copy-start.37
  301.8 5.7 copy-start.39
  301.8 5.7 copy-start.41
  301.8 5.7 copy-start.43
  301.8 5.7 copy-start.45
  301.8 5.7 copy-start.47
  301.8 5.7 copy-start.49
  301.8 5.7 copy-start.51
  301.9 5.7 copy-start.53
  301.9 5.7 copy-start.55
  301.9 5.7 copy-start.57
  301.9 5.7 copy-start.59
  478.9 3.1 collective-permute-start.5
  480.7 3.6 collective-permute-start.6
  493.1 7.7 %collective-permute-start.7 = (f32[3072]{0:T(1024)}, f32[3072]{0:T(1024)}, u32[]{:S(2)}, u32[]{:S(2)}) collective-permute-start(f32[3072]{0:T(1024)} %reshape_squeeze.14), channel_id=1, source_target_pairs={{0,1},{1,2},{2,3},{3,0},{4,5},{5,6},{6,7},{7,4},{8,9},{9,10},{10,1... | collective-permute-start | bytes 36872 | tf_op jit(solution)/shard_map/ppermute | solution.py:30
  499.7 6.0 collective-permute-start.8
  523.7 167.1 %copy-start.18 = (f32[1,32,32]{1,2,0:T(8,128)S(1)}, f32[1,32,32]{1,2,0:T(8,128)}, u32[]{:S(2)}) copy-start(f32[1,32,32]{1,2,0:T(8,128)} %get-tuple-element.84) | copy-start | bytes 12292
  523.8 167.1 %copy-start.19 = (f32[1,32,32]{1,2,0:T(8,128)S(1)}, f32[1,32,32]{1,2,0:T(8,128)}, u32[]{:S(2)}) copy-start(f32[1,32,32]{1,2,0:T(8,128)} %get-tuple-element.86) | copy-start | bytes 12292
  523.8 167.8 %copy-start.20 = (f32[1,32,32]{1,2,0:T(8,128)S(1)}, f32[1,32,32]{1,2,0:T(8,128)}, u32[]{:S(2)}) copy-start(f32[1,32,32]{1,2,0:T(8,128)} %multiply_bitcast_fusion.2) | copy-start | bytes 12292
  523.8 173.3 %copy-start.1 = (f32[16]{0:T(128)S(1)}, f32[16]{0:T(128)}, u32[]{:S(2)}) copy-start(f32[16]{0:T(128)} %param.22) | copy-start | bytes 196
  (53 other events, 194.6 us)
Sparse Core Ops, SparseCore 0:
  135.7 111.6 all-gather.1
where the time goes:
time: 713 us; the launch traced here: 704 us
  blocking collectives  398 us (56%)
  matrix products  118 us (17%)
  local copies, waits for them, and re-layouts  112 us (16%)
  other arithmetic  37.7 us (5%)
  between operations  15.9 us (2%)
  starting transfers between devices  12.5 us (2%)
  waiting for transfers between devices  9.83 us (1%)
    psum x2, blocking collectives, advance(): lax.psum(local_inner(basis_block, image_block), ('slab', 'dom')) / dof_count  172 us
    psum x2, blocking collectives, advance(): lax.psum(local_inner(residual, residual), ('slab', 'dom')) / dof_count  147 us
    psum x1, blocking collectives, per_device(): lax.psum(local_inner(start_block, start_block), ('slab', 'dom')) / dof_count  78.8 us
    dot_general x1, matrix products, element_matrices(): jnp.einsum('ia...,ib...->ab...', gradients, pushed, precision=highest)  57.7 us
    dot_general x1, matrix products, element_matrices(): jnp.einsum('ik...,kb...->ib...', stress_matrix(stress), gradients, precis...  39.3 us
    gather x2, local copies, waits for them, and re-layouts, per_device(): jnp.take(shard_piece, jnp.clip(flat_columns, 0, shard_piece.shape[1] - 1)...  35.7 us
  transfers between devices with their start and end apart: 10, of which 3 were waited for; matrix products, arithmetic and copies ran while one was open for 6% of the time, Pallas kernels for 0%

commit v1 on v0

v1 whole, which is shorter than its diff:
```python
import jax
import jax.numpy as jnp
from jax import lax
from jax.experimental import pallas as pl
from jax.experimental.pallas import tpu as pltpu
from jax.sharding import PartitionSpec as P

highest = lax.Precision.HIGHEST
SUB, LANE = 8, 128
ROWS = 31


def lane_pick(values, index):
    return jnp.take_along_axis(values, index, axis=1, mode="promise_in_bounds")


def stencil_kernel(ranges_ref, table_ref, lists_ref, *refs):
    sources, (low_ref, top_ref, below_ref, picked_ref) = refs[:-4], refs[-4:]
    sub = lax.broadcasted_iota(jnp.int32, (SUB, LANE), 0)
    lane = lax.broadcasted_iota(jnp.int32, (SUB, LANE), 1)
    inner = sub < SUB - 1
    ids = []
    for layer in range(2):
        behind = jnp.broadcast_to(lists_ref[2, layer, :, 0:1], (SUB, LANE))
        behind = jnp.max(jnp.where(lane == sub, behind, -1), axis=0, keepdims=True)
        behind = jnp.broadcast_to(behind, (SUB, LANE))
        behind = jnp.where(lane < SUB - 1, behind, -1)
        ids.append(jnp.where(inner, lists_ref[0, layer], behind))
    picked_ref[...] = jnp.zeros(picked_ref.shape, jnp.float32)
    for part in range(len(sources) // 2):
        start, count = ranges_ref[part, 0], ranges_ref[part, 1]
        group_of, lane_of = [], []
        for layer in range(2):
            place = ids[layer] - start
            held = (place >= 0) & (place < count)
            group_of.append(jnp.where(held, place >> 7, -1))
            lane_of.append(jnp.where(held, place & (LANE - 1), 0))
        halves = sources[2 * part : 2 * part + 2]

        def pick_groups(step, carry):
            for unit in range(2):
                group = step * 2 + unit
                span = pl.ds(pl.multiple_of(group * LANE, LANE), LANE)
                here = [group_of[layer] == group for layer in range(2)]
                for row in range(ROWS):
                    half, line = divmod(row, 16)
                    line = jnp.broadcast_to(halves[half][line : line + 1, span], (SUB, LANE))
                    for layer in range(2):
                        got = lane_pick(line, lane_of[layer])
                        picked_ref[layer, row] = jnp.where(here[layer], got, picked_ref[layer, row])
            return carry

        lax.fori_loop(0, (count + 2 * LANE - 1) // (2 * LANE), pick_groups, 0)
    low_ref[...] = jnp.zeros(low_ref.shape, jnp.float32)
    top_ref[...] = jnp.zeros(top_ref.shape, jnp.float32)
    below_ref[...] = jnp.zeros(below_ref.shape, jnp.float32)
    first_lane = lane == 0

    def from_behind(rows):
        edge = lane_pick(jnp.broadcast_to(rows[SUB - 1 : SUB], (SUB, LANE)), sub)
        return jnp.where(first_lane, edge, pltpu.roll(rows, 1, axis=1))

    for layer in range(2):
        grade = picked_ref[layer, 30]
        scale = jnp.zeros((SUB, LANE), jnp.float32)
        for level in range(table_ref.shape[0]):
            scale = jnp.where(grade == float(level), table_ref[level], scale)
        own = [picked_ref[layer, row] for row in range(24)]
        own += [picked_ref[layer, 24 + row] * scale for row in range(6)]
        behind = [from_behind(rows) for rows in own]
        for slot in range(4):
            data = own if slot < 2 else behind
            stress = [jnp.where(inner, data[24 + row], 0.0) for row in range(6)]
            grad = data[:24]
            if slot % 2 == 1:
                stress = [pltpu.roll(rows, 1, axis=0) for rows in stress]
                grad = [pltpu.roll(rows, 1, axis=0) for rows in grad]
            order = ((0, 5, 4), (5, 1, 3), (4, 3, 2))
            for corner in range(8):
                pushed = [
                    stress[order[i][0]] * grad[corner]
                    + stress[order[i][1]] * grad[8 + corner]
                    + stress[order[i][2]] * grad[16 + corner]
                    for i in range(3)
                ]
                offset = (corner % 2 - slot % 2 + 1) + 3 * (corner // 2 % 2 - slot // 2 + 1)
                offset += 9 * (corner // 4)
                upper = sum(grad[8 * i + slot + 4] * pushed[i] for i in range(3))
                lower = sum(grad[8 * i + slot] * pushed[i] for i in range(3))
                if layer == 0:
                    low_ref[offset] += upper
                    below_ref[offset] += lower
                else:
                    top_ref[offset] += upper
                    low_ref[offset + 9] += lower
    for ref in (low_ref, top_ref, below_ref):
        for offset in range(ref.shape[0]):
            if offset % 3 != 1:
                ref[offset] = pltpu.roll(ref[offset], (offset % 3 - 1) % SUB, axis=0)


def local_stencils(ranges, table, lists, sources):
    vmem = pl.BlockSpec(memory_space=pltpu.VMEM)
    smem = pl.BlockSpec(memory_space=pltpu.SMEM)
    return pl.pallas_call(
        stencil_kernel,
        out_shape=[
            jax.ShapeDtypeStruct((27, SUB, LANE), jnp.float32),
            jax.ShapeDtypeStruct((18, SUB, LANE), jnp.float32),
            jax.ShapeDtypeStruct((18, SUB, LANE), jnp.float32),
        ],
        in_specs=[smem, smem] + [vmem] * (1 + len(sources)),
        out_specs=[vmem, vmem, vmem],
        scratch_shapes=[pltpu.VMEM((2, ROWS, SUB, LANE), jnp.float32)],
        compiler_params=pltpu.CompilerParams(vmem_limit_bytes=24 * 1024 * 1024),
    )(ranges, table, lists, *sources)


def edges_kernel(first_ref, second_ref, left_ref, right_ref):
    collect_edges((first_ref, second_ref), left_ref, right_ref)


def collect_edges(floors, left_ref, right_ref):
    lane = lax.broadcasted_iota(jnp.int32, (SUB, LANE), 1)
    vecs = floors[0].shape[0]

    def step(vec, carry):
        out = []
        for floor in range(2):
            rows = floors[floor][vec]
            left, right = carry[2 * floor : 2 * floor + 2]
            out.append(jnp.where(lane == vec, pltpu.roll(rows, vec, axis=1), left))
            out.append(jnp.where(lane == vec, pltpu.roll(rows, vec + 1, axis=1), right))
        return tuple(out)

    zero = jnp.zeros((SUB, LANE), jnp.float32)
    done = lax.fori_loop(0, vecs, step, (zero,) * 4, unroll=4)
    for floor in range(2):
        left_ref[floor] = done[2 * floor]
        right_ref[floor] = done[2 * floor + 1]


def edge_columns(first, second):
    vmem = pl.BlockSpec(memory_space=pltpu.VMEM)
    shape = jax.ShapeDtypeStruct((2, SUB, LANE), jnp.float32)
    return pl.pallas_call(
        edges_kernel, out_shape=[shape, shape], in_specs=[vmem] * 2, out_specs=[vmem] * 2
    )(first, second)


def operator_rows(floors, behind, ahead, low_ref, high_ref, diag_ref, outs, edges):
    lane = lax.broadcasted_iota(jnp.int32, (SUB, LANE), 1)
    vecs = floors[0].shape[0]
    per_comp = vecs // diag_ref.shape[0]
    width = 2

    def step(index, carry):
        base = index * width
        rows = []
        for unit in range(width):
            vec = base + unit
            for z in range(4):
                mid = floors[z][vec]
                left = pltpu.roll(behind[z], LANE - vec, axis=1)
                left = jnp.where(lane == 0, left, pltpu.roll(mid, 1, axis=1))
                right = pltpu.roll(ahead[z], LANE - 1 - vec, axis=1)
                right = jnp.where(lane == LANE - 1, right, pltpu.roll(mid, LANE - 1, axis=1))
                rows.append((left, mid, right))
        new = list(carry)
        comp = base // per_comp
        for floor, stencil_ref in ((0, low_ref), (1, high_ref)):
            weight = diag_ref[comp, floor]
            sums = [[None] * 3 for _ in range(width)]
            for offset in range(27):
                taps = stencil_ref[offset]
                dx, dy, dz = offset % 3, offset // 3 % 3, offset // 9
                for unit in range(width):
                    term = taps * rows[4 * unit + floor + dz][dy]
                    old = sums[unit][dx]
                    sums[unit][dx] = term if old is None else old + term
            for unit in range(width):
                vec = base + unit
                total = weight * rows[4 * unit + floor + 1][1] + sums[unit][1]
                total = total + pltpu.roll(sums[unit][0], 1, axis=0)
                total = total + pltpu.roll(sums[unit][2], SUB - 1, axis=0)
                outs[floor][vec] = total
                if edges is not None:
                    new[2 * floor] = jnp.where(
                        lane == vec, pltpu.roll(total, vec, axis=1), new[2 * floor]
                    )
                    new[2 * floor + 1] = jnp.where(
                        lane == vec, pltpu.roll(total, vec + 1, axis=1), new[2 * floor + 1]
                    )
        return tuple(new)

    zero = jnp.zeros((SUB, LANE), jnp.float32)
    done = lax.fori_loop(0, vecs // width, step, (zero,) * (0 if edges is None else 4))
    if edges is not None:
        for floor in range(2):
            edges[0][floor] = done[2 * floor]
            edges[1][floor] = done[2 * floor + 1]


def first_operator_kernel(
    under_ref, first_ref, second_ref, over_ref, behind_ref, ahead_ref, low_ref, top_ref, below_ref,
    diag_ref, out_0_ref, out_1_ref, left_ref, right_ref, high_ref,
):
    high_ref[0:18] = top_ref[...]
    high_ref[18:27] = below_ref[9:18]
    high_ref[9:18] = high_ref[9:18] + below_ref[0:9]
    operator_rows(
        (under_ref, first_ref, second_ref, over_ref),
        [behind_ref[z] for z in range(4)],
        [ahead_ref[z] for z in range(4)],
        low_ref, high_ref, diag_ref, (out_0_ref, out_1_ref), (left_ref, right_ref),
    )


def second_operator_kernel(
    under_ref, first_ref, second_ref, over_ref, behind_ref, ahead_ref, low_ref, high_ref, diag_ref,
    start_0_ref, start_1_ref, out_0_ref, out_1_ref, gram_ref,
):
    operator_rows(
        (under_ref, first_ref, second_ref, over_ref),
        [behind_ref[z] for z in range(4)],
        [ahead_ref[z] for z in range(4)],
        low_ref, high_ref, diag_ref, (out_0_ref, out_1_ref), None,
    )
    blocks = ((start_0_ref, first_ref, out_0_ref), (start_1_ref, second_ref, out_1_ref))
    vecs = first_ref.shape[0] // diag_ref.shape[0]
    gram = None
    for comp in range(diag_ref.shape[0]):
        for floor in range(2):
            for across in range(0, SUB, 2):
                rows = []
                for ref in blocks[floor]:
                    span = pl.ds(comp * vecs, vecs)
                    rows.append(
                        jnp.concatenate([ref[span, across, :], ref[span, across + 1, :]], axis=1)
                    )
                rows = jnp.concatenate(rows, axis=0)
                term = lax.dot_general(
                    rows, rows, (((1,), (1,)), ((), ())), precision=highest,
                    preferred_element_type=jnp.float32,
                )
                gram = term if gram is None else gram + term
    gram_ref[...] = gram


def call_whole(kernel, out_shape, *operands, scratch_shapes=()):
    vmem = pl.BlockSpec(memory_space=pltpu.VMEM)
    return pl.pallas_call(
        kernel,
        out_shape=out_shape,
        in_specs=[vmem] * len(operands),
        out_specs=[vmem] * len(out_shape),
        scratch_shapes=scratch_shapes,
        compiler_params=pltpu.CompilerParams(vmem_limit_bytes=32 * 1024 * 1024),
    )(*operands)


def apply_first(under, first, second, over, behind, ahead, low, top, below, diagonal):
    floor = jax.ShapeDtypeStruct(first.shape, jnp.float32)
    edge = jax.ShapeDtypeStruct((2, SUB, LANE), jnp.float32)
    taps = jax.ShapeDtypeStruct((27, SUB, LANE), jnp.float32)
    return call_whole(
        first_operator_kernel, [floor, floor, edge, edge, taps],
        under, first, second, over, behind, ahead, low, top, below, diagonal,
    )


def apply_second(under, first, second, over, behind, ahead, low, high, diagonal, start_0, start_1):
    floor = jax.ShapeDtypeStruct(first.shape, jnp.float32)
    size = 3 * first.shape[0] // diagonal.shape[0]
    gram = jax.ShapeDtypeStruct((size, size), jnp.float32)
    return call_whole(
        second_operator_kernel, [floor, floor, gram],
        under, first, second, over, behind, ahead, low, high, diagonal, start_0, start_1,
    )


def dot_rows(left, right):
    return lax.dot_general(
        left, right, (((1,), (0,)), ((), ())), precision=highest, preferred_element_type=jnp.float32
    )


def dot_both(left, right):
    return lax.dot_general(
        left, right, (((1,), (1,)), ((), ())), precision=highest, preferred_element_type=jnp.float32
    )


def eliminate(gram):
    size = gram.shape[0]
    row_id = lax.broadcasted_iota(jnp.int32, (size, 2 * size), 0)
    lane_id = lax.broadcasted_iota(jnp.int32, (size, 2 * size), 1)
    identity = (row_id[:, :size] == lane_id[:, :size]).astype(jnp.float32)
    work = jnp.concatenate([gram, identity], axis=1)
    for k in range(size):
        inverse = 1.0 / jnp.sqrt(work[k : k + 1, k : k + 1])
        row = work[k : k + 1, :] * inverse
        column = work[:, k : k + 1] * inverse
        work = jnp.where(row_id == k, row, jnp.where(row_id > k, work - column * row, work))
    upper = jnp.where(row_id[:, :size] <= lane_id[:, :size], work[:, :size], 0.0)
    return upper, work[:, size:]


def finish_kernel(gram_ref, *refs):
    blocks = (refs[0:5:2], refs[1:6:2])
    next_ref, diag_ref, offdiag_ref = refs[6:]
    vecs = diag_ref.shape[1]
    comps = next_ref.shape[0]
    zero = jnp.zeros((vecs, vecs), jnp.float32)
    eye = (
        lax.broadcasted_iota(jnp.int32, (vecs, vecs), 0)
        == lax.broadcasted_iota(jnp.int32, (vecs, vecs), 1)
    ).astype(jnp.float32)

    def grid(rows):
        return jnp.concatenate([jnp.concatenate(row, axis=1) for row in rows], axis=0)

    def block(matrix, row, column):
        return matrix[row * vecs : (row + 1) * vecs, column * vecs : (column + 1) * vecs]

    gram = gram_ref[...]
    upper_0, inverse_0 = eliminate(block(gram, 0, 0))
    spread = grid([[inverse_0, zero, zero], [zero, inverse_0, zero], [zero, zero, inverse_0]])
    krylov = dot_both(dot_rows(spread, gram), spread)
    alpha_1, alpha_1_t = block(krylov, 0, 1), block(krylov, 1, 0)
    change = grid([[eye, zero, zero], [-alpha_1_t, eye, zero], [zero, -alpha_1_t, eye]])
    moved = dot_both(dot_rows(change, krylov), change)
    upper_1, inverse_1 = eliminate(block(moved, 1, 1))
    second = grid([[zero, inverse_1, zero], [-upper_1, zero, inverse_1]])
    products = dot_both(dot_rows(second, moved), second)
    alpha_2, alpha_2_t = block(products, 0, 1), block(products, 1, 0)
    upper_2, inverse_2 = eliminate(block(products, 1, 1) - dot_rows(alpha_2_t, alpha_2))
    residual = jnp.concatenate([-upper_1, -dot_rows(alpha_2_t, inverse_1), inverse_1], axis=1)
    coefs = dot_rows(dot_rows(dot_rows(inverse_2, residual), change), spread)
    diag_ref[0] = alpha_1
    diag_ref[1] = alpha_2
    offdiag_ref[0] = upper_0
    offdiag_ref[1] = upper_1
    offdiag_ref[2] = upper_2
    for comp in range(comps):
        for floor in range(2):
            span = pl.ds(comp * vecs, vecs)
            for across in range(0, SUB, 2):
                rows = jnp.concatenate(
                    [
                        jnp.concatenate([ref[span, across, :], ref[span, across + 1, :]], axis=1)
                        for ref in blocks[floor]
                    ],
                    axis=0,
                )
                mixed = dot_rows(coefs, rows)
                next_ref[comp, :, floor, across, :] = mixed[:, :LANE]
                next_ref[comp, :, floor, across + 1, :] = mixed[:, LANE:]


def finish(gram, blocks, out_shape, vecs):
    return call_whole(
        finish_kernel,
        [
            jax.ShapeDtypeStruct(out_shape, jnp.float32),
            jax.ShapeDtypeStruct((2, vecs, vecs), jnp.float32),
            jax.ShapeDtypeStruct((3, vecs, vecs), jnp.float32),
        ],
        gram, *blocks,
    )


def exchange(value, axis, route):
    size = lax.axis_size(axis)
    return lax.ppermute(value, axis, [(i, route(i)) for i in range(size)])


def ring_pairs(stride, size, odd_first):
    def route(i):
        digit = i // stride % size
        if odd_first:
            partner = (digit + 1) % size if digit % 2 == 0 else (digit - 1) % size
        else:
            partner = (digit + 1) % size if digit % 2 == 1 else (digit - 1) % size
        return i + (partner - digit) * stride

    return route


def far_pairs(stride):
    partners = (3, 6, 5, 0, 7, 2, 1, 4)

    def route(i):
        digit = i // stride % 8
        return i + (partners[digit] - digit) * stride

    return route


def mesh_sum(value):
    steps = [
        ("slab", ring_pairs(1, 2, True)),
        ("dom", ring_pairs(1, 4, True)),
        ("dom", ring_pairs(1, 4, False)),
        ("slab", ring_pairs(2, 4, True)),
        ("slab", ring_pairs(2, 4, False)),
        ("slab", ring_pairs(8, 8, True)),
        ("slab", ring_pairs(8, 8, False)),
        ("slab", far_pairs(8)),
    ]
    for axis, route in steps:
        value = value + exchange(value, axis, route)
    return value


def shifted(value, axis, steps, wrap):
    size = lax.axis_size(axis)
    route = [(i, (i + steps) % size) for i in range(size) if wrap or 0 <= i + steps < size]
    return lax.ppermute(value, axis, route)


def beside(first, second, left, right):
    from_left = shifted(right, "dom", 1, True)
    from_right = shifted(left, "dom", -1, True)
    under = shifted(second, "slab", 1, False)
    over = shifted(first, "slab", -1, False)
    up = shifted(jnp.stack([from_left[1], from_right[1]]), "slab", 1, False)
    down = shifted(jnp.stack([from_left[0], from_right[0]]), "slab", -1, False)
    behind = jnp.concatenate([up[0:1], from_left, down[0:1]], axis=0)
    ahead = jnp.concatenate([up[1:2], from_right, down[1:2]], axis=0)
    return under, over, behind, ahead


def gathered(elem_grad, elem_stress, elem_grade):
    capacity = elem_grad.shape[2]
    packed = jnp.concatenate(
        [
            elem_grad.reshape(24, capacity),
            elem_stress,
            elem_grade.astype(jnp.float32)[None],
            jnp.zeros((1, capacity), jnp.float32),
        ],
        axis=0,
    )
    low, high = packed[:16], packed[16:]
    low_1, high_1 = shifted(low, "dom", 1, True), shifted(high, "dom", 1, True)
    low_3, high_3 = shifted(low, "dom", -1, True), shifted(high, "dom", -1, True)
    low_2, high_2 = shifted(low_1, "dom", 1, True), shifted(high_3, "dom", -1, True)
    return [low, high, low_1, high_1, low_2, high_2, low_3, high_3]


def per_device(
    elem_grad,
    elem_stress,
    elem_grade,
    grade_scale,
    part_counts,
    node_lists,
    stiff_diag,
    start_block,
):
    comps, vecs = start_block.shape[:2]
    floor_shape = (comps * vecs,) + start_block.shape[3:]
    sources = gathered(elem_grad, elem_stress, elem_grade)
    counts = part_counts[0]
    starts = jnp.cumsum(counts) - counts
    parts = lax.axis_size("dom")
    order = (lax.axis_index("dom") - jnp.arange(parts, dtype=jnp.int32)) % parts
    ranges = jnp.stack([starts[order], counts[order]], axis=1).astype(jnp.int32)
    start_0 = start_block[:, :, 0].reshape(floor_shape)
    start_1 = start_block[:, :, 1].reshape(floor_shape)
    under, over, behind, ahead = beside(start_0, start_1, *edge_columns(start_0, start_1))
    low, top, below = local_stencils(ranges, grade_scale, node_lists, sources)
    below = shifted(below, "slab", -1, False)
    image_0, image_1, left, right, high = apply_first(
        under, start_0, start_1, over, behind, ahead, low, top, below, stiff_diag
    )
    under, over, behind, ahead = beside(image_0, image_1, left, right)
    second_0, second_1, gram = apply_second(
        under, image_0, image_1, over, behind, ahead, low, high, stiff_diag, start_0, start_1
    )
    dof_count = (
        start_block.size // vecs * lax.axis_size("slab") * lax.axis_size("dom")
    )
    gram = mesh_sum(gram) / dof_count
    blocks = (start_0, start_1, image_0, image_1, second_0, second_1)
    return finish(gram, blocks, start_block.shape, vecs)


def solution(mesh):
    in_specs = (
        P(None, None, ("slab", "dom")),
        P(None, ("slab", "dom")),
        P(("slab", "dom")),
        P(),
        P("slab", None),
        P(None, "slab", None, "dom"),
        P(None, "slab", None, "dom"),
        P(None, None, "slab", None, "dom"),
    )
    out_specs = (P(None, None, "slab", None, "dom"), P(), P())
    return jax.shard_map(
        per_device, mesh=mesh, in_specs=in_specs, out_specs=out_specs, check_vma=False
    )
```

time: 713 us -> 150 us (0.21)
  blocking collectives: 398 us -> 0 us
  matrix products: 118 us -> 0 us
  local copies, waits for them, and re-layouts: 112 us -> 4.36 us
  starting transfers between devices: 12.5 us -> 67.2 us
  Pallas kernels: 0 us -> 42 us
  other arithmetic: 37.7 us -> 1.38 us
  waiting for transfers between devices: 9.83 us -> 31.8 us
  between operations: 15.9 us -> 0.97 us
    psum x5 -> x0, blocking collectives: 398 us -> none  [the longest x2 172 us: advance(): lax.psum(local_inner(basis_block, image_block), ('slab', 'dom')) / dof_count]
    dot_general x22 -> x0, matrix products: 117 us -> none  [the longest x1 57.7 us: element_matrices(): jnp.einsum('ia...,ib...->ab...', gradients, pushed, precision=highest)]
    ppermute x9 -> x27, starting transfers between devices: 12.4 us -> 67.2 us  [the longest x19 34.5 us: shifted(): return lax.ppermute(value, axis, route)]
    pallas_call x0 -> x5, Pallas kernels: none -> 42 us  [the longest x3 31.3 us: call_whole(): pl.pallas_call(kernel, out_shape=out_shape, in_specs=[vmem] * len(operand...]
    gather x2, local copies, waits for them, and re-layouts: 35.7 us -> 1.28 us  [per_device(): ranges = jnp.stack([starts[order], counts[order]], axis=1).astype(jnp.int32)]
    another operation x22 -> x6, other arithmetic: 22.4 us -> 0.27 us  [the longest x9 10.8 us: normalize(): factor = jnp.linalg.cholesky(gram_matrix)]
    ppermute x9 -> x27, waiting for transfers between devices: 9.81 us -> 31.8 us  [the longest x8 16.8 us: exchange(): return lax.ppermute(value, axis, [(i, route(i)) for i in range(size)])]
    reshape x9 -> x0, local copies, waits for them, and re-layouts: 19.3 us -> none  [the longest x4 9.76 us: apply_operator(): from_right = from_behind(first_column, 'dom', -1).reshape(edge_shape + (1,))]
  transfers between devices with their start and end apart: 10 -> 27, of which waited for: 3 -> 14; matrix products, arithmetic and copies ran while one was open for 6% -> 3% of each run, Pallas kernels for 0% -> 7%
where the time goes in v1:
time: 150 us; the launch traced here: 148 us
  starting transfers between devices  67.2 us (45%)
  Pallas kernels  42 us (28%)
  waiting for transfers between devices  31.8 us (21%)
  local copies, waits for them, and re-layouts  4.36 us (3%)
    ppermute x19, starting transfers between devices, shifted(): return lax.ppermute(value, axis, route)  34.5 us
    ppermute x8, starting transfers between devices, exchange(): return lax.ppermute(value, axis, [(i, route(i)) for i in range(size)])  32.7 us
    pallas_call x3, Pallas kernels, call_whole(): pl.pallas_call(kernel, out_shape=out_shape, in_specs=[vmem] * len(operand...  31.3 us
    ppermute x8, waiting for transfers between devices, exchange(): return lax.ppermute(value, axis, [(i, route(i)) for i in range(size)])  16.8 us
    ppermute x19, waiting for transfers between devices, shifted(): return lax.ppermute(value, axis, route)  15 us
    pallas_call x1, Pallas kernels, local_stencils(): pl.pallas_call(stencil_kernel, out_shape=[jax.ShapeDtypeStruct((27, SUB,...  6.93 us
    pallas_call x1, Pallas kernels, edge_columns(): pl.pallas_call(edges_kernel, out_shape=[shape, shape], in_specs=[vmem] *...  3.76 us
  transfers between devices with their start and end apart: 27, of which 14 were waited for; matrix products, arithmetic and copies ran while one was open for 3% of the time, Pallas kernels for 7%

profile of v1, /device:TPU:8, one launch (start us, length us, event | category | flops | bytes accessed | tf_op | source)
XLA Modules:
  0.0 147.7 jit_solution(272440400214351847)
XLA Ops:
  0.7 1.1 slice_bitcast_fusion.refs_0_
  1.8 2.3 %collective-permute-start.11 = (f32[16,5376]{1,0:T(8,128)S(1)}, f32[16,5376]{1,0:T(8,128)S(1)}, u32[]{:S(2)}, u32[]{:S(2)}) collective-permute-start(f32[16,5376]{1,0:T(8,128)S(1)} %slice_bitcast_fusion.refs_0_), channel_id=1, source_target_pairs={{0,3},{1,0},{2,1},{3,2},{4,7},{5,4},{6,5},{7,6},{8,11},{9,8},{10,9... | collective-permute-start | bytes 1032200 | tf_op jit(solution)/shard_map/ppermute | solution.py:419
  4.2 1.0 fusion.refs_1_
  5.2 2.1 %collective-permute-start.9 = (f32[16,5376]{1,0:T(8,128)S(1)}, f32[16,5376]{1,0:T(8,128)S(1)}, u32[]{:S(2)}, u32[]{:S(2)}) collective-permute-start(f32[16,5376]{1,0:T(8,128)S(1)} %fusion.refs_1_), channel_id=1, source_target_pairs={{0,3},{1,0},{2,1},{3,2},{4,7},{5,4},{6,5},{7,6},{8,11},{9,8},{10,9... | collective-permute-start | bytes 1032200 | tf_op jit(solution)/shard_map/ppermute | solution.py:419
  7.3 0.9 fusion.3
  8.3 3.8 %shard_map.103 = (f32[2,8,128]{2,1,0:T(8,128)}, f32[2,8,128]{2,1,0:T(8,128)}) custom-call(f32[96,8,128]{2,1,0:T(8,128)} %bitcast.15, f32[96,8,128]{2,1,0:T(8,128)} %bitcast.20), custom_call_target="tpu_custom_call" | custom-call | tf_op jit(solution)/shard_map/pallas_call | solution.py:146
  12.0 2.5 %collective-permute-start.3 = (f32[2,8,128]{2,1,0:T(8,128)}, f32[2,8,128]{2,1,0:T(8,128)S(1)}, u32[]{:S(2)}, u32[]{:S(2)}) collective-permute-start(f32[2,8,128]{2,1,0:T(8,128)} %get-tuple-element.17), channel_id=1, source_target_pairs={{0,3},{1,0},{2,1},{3,2},{4,7},{5,4},{6,5},{7,6},{8,11},{9,8},{10,9... | collective-permute-start | bytes 24584 | tf_op jit(solution)/shard_map/ppermute | solution.py:419
  14.5 0.6 copy-done.5
  15.4 0.6 gather_fusion
  16.0 0.6 gather_fusion.1
  16.9 2.3 %collective-permute-done.3 = f32[2,8,128]{2,1,0:T(8,128)S(1)} collective-permute-done((f32[2,8,128]{2,1,0:T(8,128)}, f32[2,8,128]{2,1,0:T(8,128)S(1)}, u32[]{:S(2)}, u32[]{:S(2)}) %collective-permute-start.3) | collective-permute-done | bytes 8224 | tf_op jit(solution)/shard_map/ppermute | solution.py:419
  19.2 1.4 collective-permute-start.5
  20.6 3.0 %collective-permute-start.4 = (f32[2,8,128]{2,1,0:T(8,128)S(1)}, f32[2,8,128]{2,1,0:T(8,128)S(1)}, u32[]{:S(2)}, u32[]{:S(2)}) collective-permute-start(f32[2,8,128]{2,1,0:T(8,128)S(1)} %pad_maximum_fusion.6), channel_id=1, source_target_pairs={{0,4},{4,8},{8,12},{12,16},{16,20},{20,24},{24,28},{28,32},{32,36}... | collective-permute-start | bytes 24584 | tf_op jit(solution)/shard_map/ppermute | solution.py:419
  23.8 1.6 %collective-permute-start.7 = (f32[16,5376]{1,0:T(8,128)S(1)}, f32[16,5376]{1,0:T(8,128)S(1)}, u32[]{:S(2)}, u32[]{:S(2)}) collective-permute-start(f32[16,5376]{1,0:T(8,128)S(1)} %fusion.refs_1_), channel_id=1, source_target_pairs={{0,1},{1,2},{2,3},{3,0},{4,5},{5,6},{6,7},{7,4},{8,9},{9,10},{10,1... | collective-permute-start | bytes 1032200 | tf_op jit(solution)/shard_map/ppermute | solution.py:419
  25.4 2.8 %collective-permute-start = (f32[96,8,128]{2,1,0:T(8,128)S(1)}, f32[96,8,128]{2,1,0:T(8,128)S(1)}, u32[]{:S(2)}, u32[]{:S(2)}) collective-permute-start(f32[96,8,128]{2,1,0:T(8,128)S(1)} %bitcast.21), channel_id=1, source_target_pairs={{0,4},{4,8},{8,12},{12,16},{16,20},{20,24},{24,28},{28,32},{32,36}... | collective-permute-start | bytes 1179656 | tf_op jit(solution)/shard_map/ppermute | solution.py:419
  28.1 1.3 collective-permute-start.1
  29.4 2.6 %collective-permute-start.8 = (f32[16,5376]{1,0:T(8,128)S(1)}, f32[16,5376]{1,0:T(8,128)S(1)}, u32[]{:S(2)}, u32[]{:S(2)}) collective-permute-start(f32[16,5376]{1,0:T(8,128)S(1)} %collective-permute-done.6.refs_2_), channel_id=1, source_target_pairs={{0,1},{1,2},{2,3},{3,0},{4,5},{5,6},{6,7},{7,4},{8,9},{9,10},{10,1... | collective-permute-start | bytes 1032200 | tf_op jit(solution)/shard_map/ppermute | solution.py:419
  32.1 2.5 %collective-permute-done.7.refs_3_ = f32[16,5376]{1,0:T(8,128)S(1)} collective-permute-done((f32[16,5376]{1,0:T(8,128)S(1)}, f32[16,5376]{1,0:T(8,128)S(1)}, u32[]{:S(2)}, u32[]{:S(2)}) %collective-permute-start.7) | collective-permute-done | bytes 344096 | tf_op jit(solution)/shard_map/ppermute | solution.py:419
  34.6 7.4 %collective-permute-done.8.refs_4_ = f32[16,5376]{1,0:T(8,128)S(1)} collective-permute-done((f32[16,5376]{1,0:T(8,128)S(1)}, f32[16,5376]{1,0:T(8,128)S(1)}, u32[]{:S(2)}, u32[]{:S(2)}) %collective-permute-start.8) | collective-permute-done | bytes 344096 | tf_op jit(solution)/shard_map/ppermute | solution.py:419
  42.1 6.9 %shard_map.104 = (f32[27,8,128]{2,1,0:T(8,128)S(1)}, f32[18,8,128]{2,1,0:T(8,128)S(1)}, f32[18,8,128]{2,1,0:T(8,128)S(1)}) custom-call(s32[4,2]{1,0:T(4,128)S(1)} %pad_add_fusion.ranges_ref, f32[16]{0:T(128)S(1)} %copy-done.4, s32[4,2,8,128]{3,2,1,0:T(8,128)S(1)} %copy-done.3, f32[16,5376]{1,0:T(8,128)S(1)} %slice_bitcast_fusion.refs_0_, ...), custom_call_target="tpu_custom_call" | custom-call | tf_op jit(solution)/shard_map/pallas_call | solution.py:105
  49.1 1.3 collective-permute-start.12
  50.4 2.0 %collective-permute-done.12.below_ref = f32[18,8,128]{2,1,0:T(8,128)S(1)} collective-permute-done((f32[18,8,128]{2,1,0:T(8,128)S(1)}, f32[18,8,128]{2,1,0:T(8,128)S(1)}, u32[]{:S(2)}, u32[]{:S(2)}) %collective-permute-start.12) | collective-permute-done | bytes 73760 | tf_op jit(solution)/shard_map/ppermute | solution.py:419
  52.4 8.6 %shard_map.105 = (f32[96,8,128]{2,1,0:T(8,128)S(1)}, f32[96,8,128]{2,1,0:T(8,128)S(1)}, f32[2,8,128]{2,1,0:T(8,128)S(1)}, f32[2,8,128]{2,1,0:T(8,128)S(1)}, f32[27,8,128]{2,1,0:T(8,128)S(1)}) custom-call(f32[96,8,128]{2,1,0:T(8,128)S(1)} %collective-permute-done.under_ref, f32[96,8,128]{2,1,0:T(8,128)S(1)} %bitcast.17, f32[96,8,128]{2,1,0:T(8,128)S(1)} %bitcast.22, ...), custom_call_target="tpu_custom_call" | custom-call | tf_op jit(solution)/shard_map/pallas_call | solution.py:252
  61.0 1.3 collective-permute-start.15
  62.3 1.0 collective-permute-start.16
  63.3 5.1 %collective-permute-start.13 = (f32[96,8,128]{2,1,0:T(8,128)S(1)}, f32[96,8,128]{2,1,0:T(8,128)S(1)}, u32[]{:S(2)}, u32[]{:S(2)}) collective-permute-start(f32[96,8,128]{2,1,0:T(8,128)S(1)} %get-tuple-element.21.second_ref.refs_3_), channel_id=1, source_target_pairs={{0,4},{4,8},{8,12},{12,16},{16,20},{20,24},{24,28},{28,32},{32,36}... | collective-permute-start | bytes 1179656 | tf_op jit(solution)/shard_map/ppermute | solution.py:419
  68.3 1.3 collective-permute-start.14
  69.7 1.3 collective-permute-start.18
  71.0 3.8 %collective-permute-start.17 = (f32[2,8,128]{2,1,0:T(8,128)S(1)}, f32[2,8,128]{2,1,0:T(8,128)S(1)}, u32[]{:S(2)}, u32[]{:S(2)}) collective-permute-start(f32[2,8,128]{2,1,0:T(8,128)S(1)} %pad_maximum_fusion.8), channel_id=1, source_target_pairs={{0,4},{4,8},{8,12},{12,16},{16,20},{20,24},{24,28},{28,32},{32,36}... | collective-permute-start | bytes 24584 | tf_op jit(solution)/shard_map/ppermute | solution.py:419
  74.9 0.6 collective-permute-done.17
  75.5 7.9 %shard_map.106 = (f32[96,8,128]{2,1,0:T(8,128)S(1)}, f32[96,8,128]{2,1,0:T(8,128)S(1)}, f32[96,96]{1,0:T(8,128)S(1)}) custom-call(f32[96,8,128]{2,1,0:T(8,128)S(1)} %collective-permute-done.13.under_ref, f32[96,8,128]{2,1,0:T(8,128)S(1)} %get-tuple-element.22.first_ref.refs_2_, f32[96,8,128]{2,1,0:T(8,128)S(1)} %get-tuple-element.21.second_ref.refs_3_, ...), custom_call_target="tpu_custom_call" | custom-call | tf_op jit(solution)/shard_map/pallas_call | solution.py:252
  83.4 2.6 %collective-permute-start.19 = (f32[96,96]{1,0:T(8,128)S(1)}, f32[96,96]{1,0:T(8,128)S(1)}, u32[]{:S(2)}, u32[]{:S(2)}) collective-permute-start(f32[96,96]{1,0:T(8,128)S(1)} %get-tuple-element.26), channel_id=1, source_target_pairs={{0,4},{4,0},{8,12},{12,8},{16,20},{20,16},{24,28},{28,24},{32,36},... | collective-permute-start | bytes 110600 | tf_op jit(solution)/shard_map/ppermute | solution.py:375
  86.0 0.9 collective-permute-done.19
  86.9 2.2 %collective-permute-start.20 = (f32[96,96]{1,0:T(8,128)S(1)}, f32[96,96]{1,0:T(8,128)S(1)}, u32[]{:S(2)}, u32[]{:S(2)}) collective-permute-start(f32[96,96]{1,0:T(8,128)S(1)} %add.50), channel_id=1, source_target_pairs={{0,1},{1,0},{2,3},{3,2},{4,5},{5,4},{6,7},{7,6},{8,9},{9,8},{10,11... | collective-permute-start | bytes 110600 | tf_op jit(solution)/shard_map/ppermute | solution.py:375
  89.1 2.3 %collective-permute-done.20 = f32[96,96]{1,0:T(8,128)S(1)} collective-permute-done((f32[96,96]{1,0:T(8,128)S(1)}, f32[96,96]{1,0:T(8,128)S(1)}, u32[]{:S(2)}, u32[]{:S(2)}) %collective-permute-start.20) | collective-permute-done | bytes 36896 | tf_op jit(solution)/shard_map/ppermute | solution.py:375
  91.4 1.4 collective-permute-start.21
  92.9 2.7 %collective-permute-done.21 = f32[96,96]{1,0:T(8,128)S(1)} collective-permute-done((f32[96,96]{1,0:T(8,128)S(1)}, f32[96,96]{1,0:T(8,128)S(1)}, u32[]{:S(2)}, u32[]{:S(2)}) %collective-permute-start.21) | collective-permute-done | bytes 36896 | tf_op jit(solution)/shard_map/ppermute | solution.py:375
  95.6 1.7 %collective-permute-start.22 = (f32[96,96]{1,0:T(8,128)S(1)}, f32[96,96]{1,0:T(8,128)S(1)}, u32[]{:S(2)}, u32[]{:S(2)}) collective-permute-start(f32[96,96]{1,0:T(8,128)S(1)} %add.52), channel_id=1, source_target_pairs={{0,8},{4,12},{8,0},{12,4},{16,24},{20,28},{24,16},{28,20},{32,40},... | collective-permute-start | bytes 110600 | tf_op jit(solution)/shard_map/ppermute | solution.py:375
  97.3 2.5 %collective-permute-done.22 = f32[96,96]{1,0:T(8,128)S(1)} collective-permute-done((f32[96,96]{1,0:T(8,128)S(1)}, f32[96,96]{1,0:T(8,128)S(1)}, u32[]{:S(2)}, u32[]{:S(2)}) %collective-permute-start.22) | collective-permute-done | bytes 36896 | tf_op jit(solution)/shard_map/ppermute | solution.py:375
  99.8 7.9 %collective-permute-start.23 = (f32[96,96]{1,0:T(8,128)S(1)}, f32[96,96]{1,0:T(8,128)S(1)}, u32[]{:S(2)}, u32[]{:S(2)}) collective-permute-start(f32[96,96]{1,0:T(8,128)S(1)} %add.53), channel_id=1, source_target_pairs={{0,24},{4,28},{8,16},{12,20},{16,8},{20,12},{24,0},{28,4},{32,56},... | collective-permute-start | bytes 110600 | tf_op jit(solution)/shard_map/ppermute | solution.py:375
  107.7 2.1 %collective-permute-done.23 = f32[96,96]{1,0:T(8,128)S(1)} collective-permute-done((f32[96,96]{1,0:T(8,128)S(1)}, f32[96,96]{1,0:T(8,128)S(1)}, u32[]{:S(2)}, u32[]{:S(2)}) %collective-permute-start.23) | collective-permute-done | bytes 36896 | tf_op jit(solution)/shard_map/ppermute | solution.py:375
  109.8 4.5 %collective-permute-start.24 = (f32[96,96]{1,0:T(8,128)S(1)}, f32[96,96]{1,0:T(8,128)S(1)}, u32[]{:S(2)}, u32[]{:S(2)}) collective-permute-start(f32[96,96]{1,0:T(8,128)S(1)} %add.54), channel_id=1, source_target_pairs={{0,32},{4,36},{8,40},{12,44},{16,48},{20,52},{24,56},{28,60},{32,0... | collective-permute-start | bytes 110600 | tf_op jit(solution)/shard_map/ppermute | solution.py:375
  114.3 2.1 %collective-permute-done.24 = f32[96,96]{1,0:T(8,128)S(1)} collective-permute-done((f32[96,96]{1,0:T(8,128)S(1)}, f32[96,96]{1,0:T(8,128)S(1)}, u32[]{:S(2)}, u32[]{:S(2)}) %collective-permute-start.24) | collective-permute-done | bytes 36896 | tf_op jit(solution)/shard_map/ppermute | solution.py:375
  116.4 7.2 %collective-permute-start.25 = (f32[96,96]{1,0:T(8,128)S(1)}, f32[96,96]{1,0:T(8,128)S(1)}, u32[]{:S(2)}, u32[]{:S(2)}) collective-permute-start(f32[96,96]{1,0:T(8,128)S(1)} %add.55), channel_id=1, source_target_pairs={{0,224},{4,228},{8,232},{12,236},{16,240},{20,244},{24,248},{28,25... | collective-permute-start | bytes 110600 | tf_op jit(solution)/shard_map/ppermute | solution.py:375
  123.5 2.1 %collective-permute-done.25 = f32[96,96]{1,0:T(8,128)S(1)} collective-permute-done((f32[96,96]{1,0:T(8,128)S(1)}, f32[96,96]{1,0:T(8,128)S(1)}, u32[]{:S(2)}, u32[]{:S(2)}) %collective-permute-start.25) | collective-permute-done | bytes 36896 | tf_op jit(solution)/shard_map/ppermute | solution.py:375
  125.6 5.2 %collective-permute-start.26 = (f32[96,96]{1,0:T(8,128)S(1)}, f32[96,96]{1,0:T(8,128)S(1)}, u32[]{:S(2)}, u32[]{:S(2)}) collective-permute-start(f32[96,96]{1,0:T(8,128)S(1)} %add.56), channel_id=1, source_target_pairs={{0,96},{4,100},{8,104},{12,108},{16,112},{20,116},{24,120},{28,124... | collective-permute-start | bytes 110600 | tf_op jit(solution)/shard_map/ppermute | solution.py:375
  130.8 2.1 %collective-permute-done.26 = f32[96,96]{1,0:T(8,128)S(1)} collective-permute-done((f32[96,96]{1,0:T(8,128)S(1)}, f32[96,96]{1,0:T(8,128)S(1)}, u32[]{:S(2)}, u32[]{:S(2)}) %collective-permute-start.26) | collective-permute-done | bytes 36896 | tf_op jit(solution)/shard_map/ppermute | solution.py:375
  132.9 14.8 %shard_map.107 = (f32[3,32,2,8,128]{4,3,2,1,0:T(8,128)}, f32[2,32,32]{2,1,0:T(8,128)}, f32[3,32,32]{2,1,0:T(8,128)}) custom-call(f32[96,96]{1,0:T(8,128)S(1)} %add_multiply_fusion.gram_ref, f32[96,8,128]{2,1,0:T(8,128)S(1)} %bitcast.19, f32[96,8,128]{2,1,0:T(8,128)S(1)} %bitcast.24, f32[96,8,128]{2,1,0:T(8,128)S(1)} %get-tuple-element.22.first_ref.refs_2_, ...), custom_call_target="tpu_custom_call" | custom-call | tf_op jit(solution)/shard_map/pallas_call | solution.py:252
  (68 shorter events, 1.0 us)
Async XLA Ops:
  0.6 3.6 %copy-start.6 = (f32[3,8,5376]{2,1,0:T(8,128)S(1)}, f32[3,8,5376]{2,1,0:T(8,128)}, u32[]{:S(2)}) copy-start(f32[3,8,5376]{2,1,0:T(8,128)} %param.8) | copy-start | bytes 1548292
  0.6 3.5 %copy-start.8 = (s32[5376]{0:T(1024)S(1)}, s32[5376]{0:T(1024)}, u32[]{:S(2)}) copy-start(s32[5376]{0:T(1024)} %param.10) | copy-start | bytes 64516
  0.7 6.7 %copy-start.7 = (f32[3,32,2,8,128]{4,3,2,1,0:T(8,128)S(1)}, f32[3,32,2,8,128]{4,3,2,1,0:T(8,128)}, u32[]{:S(2)}) copy-start(f32[3,32,2,8,128]{4,3,2,1,0:T(8,128)} %param.15) | copy-start | bytes 2359300
  1.8 26.4 %collective-permute-start.11 = (f32[16,5376]{1,0:T(8,128)S(1)}, f32[16,5376]{1,0:T(8,128)S(1)}, u32[]{:S(2)}, u32[]{:S(2)}) collective-permute-start(f32[16,5376]{1,0:T(8,128)S(1)} %slice_bitcast_fusion.refs_0_), channel_id=1, source_target_pairs={{0,3},{1,0},{2,1},{3,2},{4,7},{5,4},{6,5},{7,6},{8,11},{9,8},{10,9... | collective-permute-start | bytes 1032200 | tf_op jit(solution)/shard_map/ppermute | solution.py:419
  4.0 25.4 %collective-permute-start.6 = (f32[16,5376]{1,0:T(8,128)S(1)}, f32[16,5376]{1,0:T(8,128)S(1)}, u32[]{:S(2)}, u32[]{:S(2)}) collective-permute-start(f32[16,5376]{1,0:T(8,128)S(1)} %slice_bitcast_fusion.refs_0_), channel_id=1, source_target_pairs={{0,1},{1,2},{2,3},{3,0},{4,5},{5,6},{6,7},{7,4},{8,9},{9,10},{10,1... | collective-permute-start | bytes 1032200 | tf_op jit(solution)/shard_map/ppermute | solution.py:419
  5.2 26.8 %collective-permute-start.9 = (f32[16,5376]{1,0:T(8,128)S(1)}, f32[16,5376]{1,0:T(8,128)S(1)}, u32[]{:S(2)}, u32[]{:S(2)}) collective-permute-start(f32[16,5376]{1,0:T(8,128)S(1)} %fusion.refs_1_), channel_id=1, source_target_pairs={{0,3},{1,0},{2,1},{3,2},{4,7},{5,4},{6,5},{7,6},{8,11},{9,8},{10,9... | collective-permute-start | bytes 1032200 | tf_op jit(solution)/shard_map/ppermute | solution.py:419
  12.0 4.8 %collective-permute-start.2 = (f32[2,8,128]{2,1,0:T(8,128)}, f32[2,8,128]{2,1,0:T(8,128)S(1)}, u32[]{:S(2)}, u32[]{:S(2)}) collective-permute-start(f32[2,8,128]{2,1,0:T(8,128)} %get-tuple-element.16), channel_id=1, source_target_pairs={{0,1},{1,2},{2,3},{3,0},{4,5},{5,6},{6,7},{7,4},{8,9},{9,10},{10,1... | collective-permute-start | bytes 24584 | tf_op jit(solution)/shard_map/ppermute | solution.py:419
  12.0 7.2 %collective-permute-start.3 = (f32[2,8,128]{2,1,0:T(8,128)}, f32[2,8,128]{2,1,0:T(8,128)S(1)}, u32[]{:S(2)}, u32[]{:S(2)}) collective-permute-start(f32[2,8,128]{2,1,0:T(8,128)} %get-tuple-element.17), channel_id=1, source_target_pairs={{0,3},{1,0},{2,1},{3,2},{4,7},{5,4},{6,5},{7,6},{8,11},{9,8},{10,9... | collective-permute-start | bytes 24584 | tf_op jit(solution)/shard_map/ppermute | solution.py:419
  14.5 0.7 copy-start.5
  15.4 10.0 %copy-start.1 = (f32[3,32,1,8,128]{4,3,2,1,0:T(8,128)S(1)}, f32[3,32,1,8,128]{4,3,2,1,0:T(8,128)}, u32[]{:S(2)}) copy-start(f32[3,32,1,8,128]{4,3,2,1,0:T(8,128)} %get-tuple-element.30) | copy-start | bytes 1179652
  16.0 12.1 %copy-start = (f32[3,32,1,8,128]{4,3,2,1,0:T(8,128)S(1)}, f32[3,32,1,8,128]{4,3,2,1,0:T(8,128)}, u32[]{:S(2)}) copy-start(f32[3,32,1,8,128]{4,3,2,1,0:T(8,128)} %get-tuple-element.29) | copy-start | bytes 1179652
  19.2 22.9 %copy-start.3 = (s32[4,2,8,128]{3,2,1,0:T(8,128)S(1)}, s32[4,2,8,128]{3,2,1,0:T(8,128)}, u32[]{:S(2)}) copy-start(s32[4,2,8,128]{3,2,1,0:T(8,128)} %lists_ref.1) | copy-start | bytes 98308
  19.2 4.5 %collective-permute-start.5 = (f32[2,8,128]{2,1,0:T(8,128)S(1)}, f32[2,8,128]{2,1,0:T(8,128)S(1)}, u32[]{:S(2)}, u32[]{:S(2)}) collective-permute-start(f32[2,8,128]{2,1,0:T(8,128)S(1)} %pad_maximum_fusion.7), channel_id=1, source_target_pairs={{4,0},{8,4},{12,8},{16,12},{20,16},{24,20},{28,24},{32,28},{36,32}... | collective-permute-start | bytes 24584 | tf_op jit(solution)/shard_map/ppermute | solution.py:419
  20.6 4.7 %collective-permute-start.4 = (f32[2,8,128]{2,1,0:T(8,128)S(1)}, f32[2,8,128]{2,1,0:T(8,128)S(1)}, u32[]{:S(2)}, u32[]{:S(2)}) collective-permute-start(f32[2,8,128]{2,1,0:T(8,128)S(1)} %pad_maximum_fusion.6), channel_id=1, source_target_pairs={{0,4},{4,8},{8,12},{12,16},{16,20},{20,24},{24,28},{28,32},{32,36}... | collective-permute-start | bytes 24584 | tf_op jit(solution)/shard_map/ppermute | solution.py:419
  23.8 10.8 %collective-permute-start.7 = (f32[16,5376]{1,0:T(8,128)S(1)}, f32[16,5376]{1,0:T(8,128)S(1)}, u32[]{:S(2)}, u32[]{:S(2)}) collective-permute-start(f32[16,5376]{1,0:T(8,128)S(1)} %fusion.refs_1_), channel_id=1, source_target_pairs={{0,1},{1,2},{2,3},{3,0},{4,5},{5,6},{6,7},{7,4},{8,9},{9,10},{10,1... | collective-permute-start | bytes 1032200 | tf_op jit(solution)/shard_map/ppermute | solution.py:419
  25.4 25.1 %collective-permute-start = (f32[96,8,128]{2,1,0:T(8,128)S(1)}, f32[96,8,128]{2,1,0:T(8,128)S(1)}, u32[]{:S(2)}, u32[]{:S(2)}) collective-permute-start(f32[96,8,128]{2,1,0:T(8,128)S(1)} %bitcast.21), channel_id=1, source_target_pairs={{0,4},{4,8},{8,12},{12,16},{16,20},{20,24},{24,28},{28,32},{32,36}... | collective-permute-start | bytes 1179656 | tf_op jit(solution)/shard_map/ppermute | solution.py:419
  28.1 22.3 %collective-permute-start.1 = (f32[96,8,128]{2,1,0:T(8,128)S(1)}, f32[96,8,128]{2,1,0:T(8,128)S(1)}, u32[]{:S(2)}, u32[]{:S(2)}) collective-permute-start(f32[96,8,128]{2,1,0:T(8,128)S(1)} %bitcast.16), channel_id=1, source_target_pairs={{4,0},{8,4},{12,8},{16,12},{20,16},{24,20},{28,24},{32,28},{36,32}... | collective-permute-start | bytes 1179656 | tf_op jit(solution)/shard_map/ppermute | solution.py:419
  29.4 12.5 %collective-permute-start.8 = (f32[16,5376]{1,0:T(8,128)S(1)}, f32[16,5376]{1,0:T(8,128)S(1)}, u32[]{:S(2)}, u32[]{:S(2)}) collective-permute-start(f32[16,5376]{1,0:T(8,128)S(1)} %collective-permute-done.6.refs_2_), channel_id=1, source_target_pairs={{0,1},{1,2},{2,3},{3,0},{4,5},{5,6},{6,7},{7,4},{8,9},{9,10},{10,1... | collective-permute-start | bytes 1032200 | tf_op jit(solution)/shard_map/ppermute | solution.py:419
  32.0 10.1 %collective-permute-start.10 = (f32[16,5376]{1,0:T(8,128)S(1)}, f32[16,5376]{1,0:T(8,128)S(1)}, u32[]{:S(2)}, u32[]{:S(2)}) collective-permute-start(f32[16,5376]{1,0:T(8,128)S(1)} %collective-permute-done.9.refs_7_), channel_id=1, source_target_pairs={{0,3},{1,0},{2,1},{3,2},{4,7},{5,4},{6,5},{7,6},{8,11},{9,8},{10,9... | collective-permute-start | bytes 1032200 | tf_op jit(solution)/shard_map/ppermute | solution.py:419
  32.0 10.1 %copy-start.4 = (f32[16]{0:T(128)S(1)}, f32[16]{0:T(128)}, u32[]{:S(2)}) copy-start(f32[16]{0:T(128)} %table_ref.1) | copy-start | bytes 196
  49.1 3.3 %collective-permute-start.12 = (f32[18,8,128]{2,1,0:T(8,128)S(1)}, f32[18,8,128]{2,1,0:T(8,128)S(1)}, u32[]{:S(2)}, u32[]{:S(2)}) collective-permute-start(f32[18,8,128]{2,1,0:T(8,128)S(1)} %get-tuple-element.20), channel_id=1, source_target_pairs={{4,0},{8,4},{12,8},{16,12},{20,16},{24,20},{28,24},{32,28},{36,32}... | collective-permute-start | bytes 221192 | tf_op jit(solution)/shard_map/ppermute | solution.py:419
  50.4 2.0 %copy-start.2 = (f32[3,2,8,128]{3,2,1,0:T(8,128)S(1)}, f32[3,2,8,128]{3,2,1,0:T(8,128)}, u32[]{:S(2)}) copy-start(f32[3,2,8,128]{3,2,1,0:T(8,128)} %diag_ref.3) | copy-start | bytes 73732
  61.0 8.6 %collective-permute-start.15 = (f32[2,8,128]{2,1,0:T(8,128)S(1)}, f32[2,8,128]{2,1,0:T(8,128)S(1)}, u32[]{:S(2)}, u32[]{:S(2)}) collective-permute-start(f32[2,8,128]{2,1,0:T(8,128)S(1)} %get-tuple-element.23), channel_id=1, source_target_pairs={{0,1},{1,2},{2,3},{3,0},{4,5},{5,6},{6,7},{7,4},{8,9},{9,10},{10,1... | collective-permute-start | bytes 24584 | tf_op jit(solution)/shard_map/ppermute | solution.py:419
  62.3 7.4 %collective-permute-start.16 = (f32[2,8,128]{2,1,0:T(8,128)S(1)}, f32[2,8,128]{2,1,0:T(8,128)S(1)}, u32[]{:S(2)}, u32[]{:S(2)}) collective-permute-start(f32[2,8,128]{2,1,0:T(8,128)S(1)} %get-tuple-element.24), channel_id=1, source_target_pairs={{0,3},{1,0},{2,1},{3,2},{4,7},{5,4},{6,5},{7,6},{8,11},{9,8},{10,9... | collective-permute-start | bytes 24584 | tf_op jit(solution)/shard_map/ppermute | solution.py:419
  63.3 12.2 %collective-permute-start.13 = (f32[96,8,128]{2,1,0:T(8,128)S(1)}, f32[96,8,128]{2,1,0:T(8,128)S(1)}, u32[]{:S(2)}, u32[]{:S(2)}) collective-permute-start(f32[96,8,128]{2,1,0:T(8,128)S(1)} %get-tuple-element.21.second_ref.refs_3_), channel_id=1, source_target_pairs={{0,4},{4,8},{8,12},{12,16},{16,20},{20,24},{24,28},{28,32},{32,36}... | collective-permute-start | bytes 1179656 | tf_op jit(solution)/shard_map/ppermute | solution.py:419
  68.3 7.2 %collective-permute-start.14 = (f32[96,8,128]{2,1,0:T(8,128)S(1)}, f32[96,8,128]{2,1,0:T(8,128)S(1)}, u32[]{:S(2)}, u32[]{:S(2)}) collective-permute-start(f32[96,8,128]{2,1,0:T(8,128)S(1)} %get-tuple-element.22.first_ref.refs_2_), channel_id=1, source_target_pairs={{4,0},{8,4},{12,8},{16,12},{20,16},{24,20},{28,24},{32,28},{36,32}... | collective-permute-start | bytes 1179656 | tf_op jit(solution)/shard_map/ppermute | solution.py:419
  69.7 5.2 %collective-permute-start.18 = (f32[2,8,128]{2,1,0:T(8,128)S(1)}, f32[2,8,128]{2,1,0:T(8,128)S(1)}, u32[]{:S(2)}, u32[]{:S(2)}) collective-permute-start(f32[2,8,128]{2,1,0:T(8,128)S(1)} %pad_maximum_fusion.9), channel_id=1, source_target_pairs={{4,0},{8,4},{12,8},{16,12},{20,16},{24,20},{28,24},{32,28},{36,32}... | collective-permute-start | bytes 24584 | tf_op jit(solution)/shard_map/ppermute | solution.py:419
  71.0 4.5 %collective-permute-start.17 = (f32[2,8,128]{2,1,0:T(8,128)S(1)}, f32[2,8,128]{2,1,0:T(8,128)S(1)}, u32[]{:S(2)}, u32[]{:S(2)}) collective-permute-start(f32[2,8,128]{2,1,0:T(8,128)S(1)} %pad_maximum_fusion.8), channel_id=1, source_target_pairs={{0,4},{4,8},{8,12},{12,16},{16,20},{20,24},{24,28},{28,32},{32,36}... | collective-permute-start | bytes 24584 | tf_op jit(solution)/shard_map/ppermute | solution.py:419
  83.4 3.5 %collective-permute-start.19 = (f32[96,96]{1,0:T(8,128)S(1)}, f32[96,96]{1,0:T(8,128)S(1)}, u32[]{:S(2)}, u32[]{:S(2)}) collective-permute-start(f32[96,96]{1,0:T(8,128)S(1)} %get-tuple-element.26), channel_id=1, source_target_pairs={{0,4},{4,0},{8,12},{12,8},{16,20},{20,16},{24,28},{28,24},{32,36},... | collective-permute-start | bytes 110600 | tf_op jit(solution)/shard_map/ppermute | solution.py:375
  86.9 4.5 %collective-permute-start.20 = (f32[96,96]{1,0:T(8,128)S(1)}, f32[96,96]{1,0:T(8,128)S(1)}, u32[]{:S(2)}, u32[]{:S(2)}) collective-permute-start(f32[96,96]{1,0:T(8,128)S(1)} %add.50), channel_id=1, source_target_pairs={{0,1},{1,0},{2,3},{3,2},{4,5},{5,4},{6,7},{7,6},{8,9},{9,8},{10,11... | collective-permute-start | bytes 110600 | tf_op jit(solution)/shard_map/ppermute | solution.py:375
  91.4 4.2 %collective-permute-start.21 = (f32[96,96]{1,0:T(8,128)S(1)}, f32[96,96]{1,0:T(8,128)S(1)}, u32[]{:S(2)}, u32[]{:S(2)}) collective-permute-start(f32[96,96]{1,0:T(8,128)S(1)} %add.51), channel_id=1, source_target_pairs={{0,3},{1,2},{2,1},{3,0},{4,7},{5,6},{6,5},{7,4},{8,11},{9,10},{10,... | collective-permute-start | bytes 110600 | tf_op jit(solution)/shard_map/ppermute | solution.py:375
  95.6 4.2 %collective-permute-start.22 = (f32[96,96]{1,0:T(8,128)S(1)}, f32[96,96]{1,0:T(8,128)S(1)}, u32[]{:S(2)}, u32[]{:S(2)}) collective-permute-start(f32[96,96]{1,0:T(8,128)S(1)} %add.52), channel_id=1, source_target_pairs={{0,8},{4,12},{8,0},{12,4},{16,24},{20,28},{24,16},{28,20},{32,40},... | collective-permute-start | bytes 110600 | tf_op jit(solution)/shard_map/ppermute | solution.py:375
  99.8 10.0 %collective-permute-start.23 = (f32[96,96]{1,0:T(8,128)S(1)}, f32[96,96]{1,0:T(8,128)S(1)}, u32[]{:S(2)}, u32[]{:S(2)}) collective-permute-start(f32[96,96]{1,0:T(8,128)S(1)} %add.53), channel_id=1, source_target_pairs={{0,24},{4,28},{8,16},{12,20},{16,8},{20,12},{24,0},{28,4},{32,56},... | collective-permute-start | bytes 110600 | tf_op jit(solution)/shard_map/ppermute | solution.py:375
  109.8 6.6 %collective-permute-start.24 = (f32[96,96]{1,0:T(8,128)S(1)}, f32[96,96]{1,0:T(8,128)S(1)}, u32[]{:S(2)}, u32[]{:S(2)}) collective-permute-start(f32[96,96]{1,0:T(8,128)S(1)} %add.54), channel_id=1, source_target_pairs={{0,32},{4,36},{8,40},{12,44},{16,48},{20,52},{24,56},{28,60},{32,0... | collective-permute-start | bytes 110600 | tf_op jit(solution)/shard_map/ppermute | solution.py:375
  116.4 9.2 %collective-permute-start.25 = (f32[96,96]{1,0:T(8,128)S(1)}, f32[96,96]{1,0:T(8,128)S(1)}, u32[]{:S(2)}, u32[]{:S(2)}) collective-permute-start(f32[96,96]{1,0:T(8,128)S(1)} %add.55), channel_id=1, source_target_pairs={{0,224},{4,228},{8,232},{12,236},{16,240},{20,244},{24,248},{28,25... | collective-permute-start | bytes 110600 | tf_op jit(solution)/shard_map/ppermute | solution.py:375
  125.6 7.3 %collective-permute-start.26 = (f32[96,96]{1,0:T(8,128)S(1)}, f32[96,96]{1,0:T(8,128)S(1)}, u32[]{:S(2)}, u32[]{:S(2)}) collective-permute-start(f32[96,96]{1,0:T(8,128)S(1)} %add.56), channel_id=1, source_target_pairs={{0,96},{4,100},{8,104},{12,108},{16,112},{20,116},{24,120},{28,124... | collective-permute-start | bytes 110600 | tf_op jit(solution)/shard_map/ppermute | solution.py:375

commit v2 on v1

v2 whole, which is shorter than its diff:
```python
import jax
import jax.numpy as jnp
from jax import lax
from jax.experimental import pallas as pl
from jax.experimental.pallas import tpu as pltpu
from jax.sharding import PartitionSpec as P

highest = lax.Precision.HIGHEST
SUB, LANE = 8, 128
ROWS = 31


def lane_pick(values, index):
    return jnp.take_along_axis(values, index, axis=1, mode="promise_in_bounds")


def stencil_kernel(counts_ref, table_ref, lists_ref, *refs):
    sources, (low_ref, top_ref, below_ref, picked_ref) = refs[:-4], refs[-4:]
    sub = lax.broadcasted_iota(jnp.int32, (SUB, LANE), 0)
    lane = lax.broadcasted_iota(jnp.int32, (SUB, LANE), 1)
    inner = sub < SUB - 1
    ids = []
    for layer in range(2):
        behind = jnp.broadcast_to(lists_ref[2, layer, :, 0:1], (SUB, LANE))
        behind = jnp.max(jnp.where(lane == sub, behind, -1), axis=0, keepdims=True)
        behind = jnp.broadcast_to(behind, (SUB, LANE))
        behind = jnp.where(lane < SUB - 1, behind, -1)
        ids.append(jnp.where(inner, lists_ref[0, layer], behind))
    picked_ref[...] = jnp.zeros(picked_ref.shape, jnp.float32)
    parts = 4
    for part in range(parts):
        owner = lax.rem(lax.axis_index("dom") + (parts - part), parts)
        count = counts_ref[0, owner]
        start = jnp.int32(0)
        for other in range(parts):
            start = start + jnp.where(owner > other, counts_ref[0, other], 0)
        group_of, lane_of = [], []
        for layer in range(2):
            place = ids[layer] - start
            held = (place >= 0) & (place < count)
            group_of.append(jnp.where(held, place >> 7, -1))
            lane_of.append(jnp.where(held, place & (LANE - 1), 0))
        halves = ((0,), (1,), (2, 3), (4,))[part]

        def pick_groups(step, carry):
            for unit in range(2):
                group = step * 2 + unit
                span = pl.ds(pl.multiple_of(group * LANE, LANE), LANE)
                here = [group_of[layer] == group for layer in range(2)]
                for row in range(ROWS):
                    half, line = divmod(row, 16) if len(halves) == 2 else (0, row)
                    source = sources[halves[half]]
                    line = jnp.broadcast_to(source[line : line + 1, span], (SUB, LANE))
                    for layer in range(2):
                        got = lane_pick(line, lane_of[layer])
                        picked_ref[layer, row] = jnp.where(here[layer], got, picked_ref[layer, row])
            return carry

        lax.fori_loop(0, (count + 2 * LANE - 1) // (2 * LANE), pick_groups, 0)
    low_ref[...] = jnp.zeros(low_ref.shape, jnp.float32)
    top_ref[...] = jnp.zeros(top_ref.shape, jnp.float32)
    below_ref[...] = jnp.zeros(below_ref.shape, jnp.float32)
    first_lane = lane == 0

    def from_behind(rows):
        edge = lane_pick(jnp.broadcast_to(rows[SUB - 1 : SUB], (SUB, LANE)), sub)
        return jnp.where(first_lane, edge, pltpu.roll(rows, 1, axis=1))

    for layer in range(2):
        grade = picked_ref[layer, 30]
        scale = jnp.zeros((SUB, LANE), jnp.float32)
        for level in range(table_ref.shape[0]):
            scale = jnp.where(grade == float(level), table_ref[level], scale)
        own = [picked_ref[layer, row] for row in range(24)]
        own += [picked_ref[layer, 24 + row] * scale for row in range(6)]
        behind = [from_behind(rows) for rows in own]
        for slot in range(4):
            data = own if slot < 2 else behind
            stress = [jnp.where(inner, data[24 + row], 0.0) for row in range(6)]
            grad = data[:24]
            if slot % 2 == 1:
                stress = [pltpu.roll(rows, 1, axis=0) for rows in stress]
                grad = [pltpu.roll(rows, 1, axis=0) for rows in grad]
            order = ((0, 5, 4), (5, 1, 3), (4, 3, 2))
            for corner in range(8):
                pushed = [
                    stress[order[i][0]] * grad[corner]
                    + stress[order[i][1]] * grad[8 + corner]
                    + stress[order[i][2]] * grad[16 + corner]
                    for i in range(3)
                ]
                offset = (corner % 2 - slot % 2 + 1) + 3 * (corner // 2 % 2 - slot // 2 + 1)
                offset += 9 * (corner // 4)
                upper = sum(grad[8 * i + slot + 4] * pushed[i] for i in range(3))
                lower = sum(grad[8 * i + slot] * pushed[i] for i in range(3))
                if layer == 0:
                    low_ref[offset] += upper
                    below_ref[offset] += lower
                else:
                    top_ref[offset] += upper
                    low_ref[offset + 9] += lower
    for ref in (low_ref, top_ref, below_ref):
        for offset in range(ref.shape[0]):
            if offset % 3 != 1:
                ref[offset] = pltpu.roll(ref[offset], (offset % 3 - 1) % SUB, axis=0)


def local_stencils(counts, table, lists, sources):
    vmem = pl.BlockSpec(memory_space=pltpu.VMEM)
    smem = pl.BlockSpec(memory_space=pltpu.SMEM)
    return pl.pallas_call(
        stencil_kernel,
        out_shape=[
            jax.ShapeDtypeStruct((27, SUB, LANE), jnp.float32),
            jax.ShapeDtypeStruct((18, SUB, LANE), jnp.float32),
            jax.ShapeDtypeStruct((18, SUB, LANE), jnp.float32),
        ],
        in_specs=[smem, smem] + [vmem] * (1 + len(sources)),
        out_specs=[vmem, vmem, vmem],
        scratch_shapes=[pltpu.VMEM((2, ROWS, SUB, LANE), jnp.float32)],
        compiler_params=pltpu.CompilerParams(vmem_limit_bytes=24 * 1024 * 1024),
    )(counts, table, lists, *sources)


def split_kernel(start_ref, diag_ref, slab_ref, edges_ref):
    comps, vecs = start_ref.shape[:2]
    total = comps * vecs
    lane = lax.broadcasted_iota(jnp.int32, (SUB, LANE), 1)
    found = [jnp.zeros((SUB, LANE), jnp.float32)] * 4
    for comp in range(comps):
        for floor in range(2):
            slab_ref[2 * total + 2 * comp + floor] = diag_ref[comp, floor]

        def step(vec, carry):
            out = []
            place = comp * vecs + vec
            for floor in range(2):
                rows = start_ref[comp, vec, floor]
                slab_ref[floor * total + place] = rows
                out.append(jnp.where(lane == place, pltpu.roll(rows, place, axis=1), carry[floor]))
            for floor in range(2):
                rows = start_ref[comp, vec, floor]
                turned = pltpu.roll(rows, place + 1, axis=1)
                out.append(jnp.where(lane == place, turned, carry[2 + floor]))
            return tuple(out)

        found = lax.fori_loop(0, vecs, step, tuple(found), unroll=16)
    for k in range(4):
        edges_ref[k] = found[k]


def split_slab(start_block, diagonal):
    total = start_block.shape[0] * start_block.shape[1]
    return call_whole(
        split_kernel,
        [
            jax.ShapeDtypeStruct((2 * total + 2 * start_block.shape[0], SUB, LANE), jnp.float32),
            jax.ShapeDtypeStruct((4, SUB, LANE), jnp.float32),
        ],
        start_block, diagonal,
    )


def operator_rows(floors, behind, ahead, taps, weights, outs, edges, total, vecs, width):
    lane = lax.broadcasted_iota(jnp.int32, (SUB, LANE), 1)

    def step(index, carry):
        first = index * width
        rows = []
        for unit in range(width):
            vec = first + unit
            for z, (ref, base) in enumerate(floors):
                mid = ref[base + vec]
                left = pltpu.roll(behind[z], LANE - vec, axis=1)
                left = jnp.where(lane == 0, left, pltpu.roll(mid, 1, axis=1))
                right = pltpu.roll(ahead[z], LANE - 1 - vec, axis=1)
                right = jnp.where(lane == LANE - 1, right, pltpu.roll(mid, LANE - 1, axis=1))
                rows.append((left, mid, right))
        new = list(carry)
        comp = first // vecs
        for floor, (out_ref, base) in enumerate(outs):
            weight = weights[floor](comp)
            sums = [[None] * 3 for _ in range(width)]
            for offset in range(27):
                tap = taps[floor][offset]
                dx, dy, dz = offset % 3, offset // 3 % 3, offset // 9
                for unit in range(width):
                    term = tap * rows[len(floors) * unit + floor + dz][dy]
                    old = sums[unit][dx]
                    sums[unit][dx] = term if old is None else old + term
            for unit in range(width):
                vec = first + unit
                result = weight * rows[len(floors) * unit + floor + 1][1] + sums[unit][1]
                result = result + pltpu.roll(sums[unit][0], 1, axis=0)
                result = result + pltpu.roll(sums[unit][2], SUB - 1, axis=0)
                out_ref[base + vec] = result
                if edges is not None:
                    for side in range(2):
                        turned = pltpu.roll(result, vec + side, axis=1)
                        spot = 2 * floor + side
                        new[spot] = jnp.where(lane == vec, turned, new[spot])
        return tuple(new)

    zero = jnp.zeros((SUB, LANE), jnp.float32)
    count = 0 if edges is None else 2 * len(outs)
    done = lax.fori_loop(0, total // width, step, (zero,) * count)
    if edges is not None:
        for floor in range(len(outs)):
            edges[0][floor] = done[2 * floor]
            edges[1][floor] = done[2 * floor + 1]


def first_operator_kernel(
    under_ref, own_ref, over_ref, low_ref, top_ref, below_ref, from_above_ref, from_below_ref,
    columns_ref, image_ref, left_ref, right_ref, high_ref, under_taps_ref,
):
    total = image_ref.shape[0] // 4
    comps = (own_ref.shape[0] - 2 * total) // 2
    diag_row = 2 * total
    inside = jnp.where(lax.axis_index("slab") > 0, 1.0, 0.0)
    cols_refs = ((from_below_ref, 18), (columns_ref, 0), (from_above_ref, 45))
    high_ref[0:18] = top_ref[...]
    high_ref[18:27] = from_above_ref[36:45]
    high_ref[9:18] = high_ref[9:18] + from_above_ref[27:36]
    under_taps_ref[0:9] = from_below_ref[0:9] * inside
    under_taps_ref[9:18] = (from_below_ref[9:18] + below_ref[0:9]) * inside
    under_taps_ref[18:27] = below_ref[9:18] * inside
    slabs = (under_ref, own_ref, over_ref)
    floors = [(ref, floor * total) for ref in slabs for floor in range(2)]
    behind = [ref[row + floor] for ref, row in cols_refs for floor in range(2)]
    ahead = [ref[row + 2 + floor] for ref, row in cols_refs for floor in range(2)]

    def weight(ref, floor):
        return lambda comp: ref[diag_row + 2 * comp + floor]

    operator_rows(
        floors, behind, ahead, (under_taps_ref, low_ref, high_ref, from_above_ref),
        (weight(under_ref, 1), weight(own_ref, 0), weight(own_ref, 1), weight(over_ref, 0)),
        [(image_ref, floor * total) for floor in range(4)],
        (left_ref, right_ref), total, total // comps, 8,
    )


def second_operator_kernel(
    image_ref, from_left_ref, from_right_ref, low_ref, high_ref, diag_ref, out_ref, gram_ref
):
    total = out_ref.shape[0] // 2
    comps = diag_ref.shape[0]
    vecs = total // comps

    def weight(floor):
        return lambda comp: diag_ref[comp, floor]

    operator_rows(
        [(image_ref, floor * total) for floor in range(4)],
        [from_left_ref[floor] for floor in range(4)],
        [from_right_ref[floor] for floor in range(4)],
        (low_ref, high_ref), (weight(0), weight(1)),
        [(out_ref, floor * total) for floor in range(2)],
        None, total, vecs, 16,
    )
    blocks = [
        ((image_ref, (1 + floor) * total), (out_ref, floor * total)) for floor in range(2)
    ]
    gram_ref[...] = local_gram(blocks, comps, vecs, vecs)


def paired_rows(parts, start, vecs, across):
    rows = []
    for ref, base in parts:
        span = pl.ds(base + start, vecs)
        rows.append(jnp.concatenate([ref[span, across, :], ref[span, across + 1, :]], axis=1))
    return jnp.concatenate(rows, axis=0)


def local_gram(blocks, comps, vecs, skipped):
    gram = None
    for comp in range(comps):
        for parts in blocks:
            for across in range(0, SUB, 2):
                rows = paired_rows(parts, comp * vecs, vecs, across)
                term = dot_both(rows, rows[skipped:])
                gram = term if gram is None else gram + term
    return gram


def first_gram_kernel(own_ref, image_ref, gram_ref):
    vecs = gram_ref.shape[0] // 2
    total = image_ref.shape[0] // 4
    blocks = [
        ((own_ref, floor * total), (image_ref, (1 + floor) * total)) for floor in range(2)
    ]
    gram_ref[...] = local_gram(blocks, total // vecs, vecs, 0)


def call_whole(kernel, out_shape, *operands, scratch_shapes=()):
    vmem = pl.BlockSpec(memory_space=pltpu.VMEM)
    return pl.pallas_call(
        kernel,
        out_shape=out_shape,
        in_specs=[vmem] * len(operands),
        out_specs=[vmem] * len(out_shape),
        scratch_shapes=scratch_shapes,
        compiler_params=pltpu.CompilerParams(vmem_limit_bytes=32 * 1024 * 1024),
    )(*operands)


def apply_first(under, own, over, low, top, below, from_above, from_below, columns, total):
    edge = jax.ShapeDtypeStruct((4, SUB, LANE), jnp.float32)
    taps = jax.ShapeDtypeStruct((27, SUB, LANE), jnp.float32)
    return call_whole(
        first_operator_kernel,
        [jax.ShapeDtypeStruct((4 * total, SUB, LANE), jnp.float32), edge, edge, taps],
        under, own, over, low, top, below, from_above, from_below, columns,
        scratch_shapes=[pltpu.VMEM((27, SUB, LANE), jnp.float32)],
    )


def apply_second(image, from_left, from_right, low, high, diagonal):
    total = image.shape[0] // 4
    vecs = total // diagonal.shape[0]
    return call_whole(
        second_operator_kernel,
        [
            jax.ShapeDtypeStruct((2 * total, SUB, LANE), jnp.float32),
            jax.ShapeDtypeStruct((2 * vecs, vecs), jnp.float32),
        ],
        image, from_left, from_right, low, high, diagonal,
    )


def first_gram(own, image, vecs):
    shape = jax.ShapeDtypeStruct((2 * vecs, 2 * vecs), jnp.float32)
    return call_whole(first_gram_kernel, [shape], own, image)[0]


def dot_rows(left, right):
    return lax.dot_general(
        left, right, (((1,), (0,)), ((), ())), precision=highest, preferred_element_type=jnp.float32
    )


def dot_both(left, right):
    return lax.dot_general(
        left, right, (((1,), (1,)), ((), ())), precision=highest, preferred_element_type=jnp.float32
    )


def eliminate(gram):
    size = gram.shape[0]
    row_id = lax.broadcasted_iota(jnp.int32, (size, 2 * size), 0)
    lane_id = lax.broadcasted_iota(jnp.int32, (size, 2 * size), 1)
    identity = (row_id[:, :size] == lane_id[:, :size]).astype(jnp.float32)
    work = jnp.concatenate([gram, identity], axis=1)
    panel = 8
    for first in range(0, size, panel):
        spots = range(first, first + panel)
        columns = [jnp.broadcast_to(work[:, k : k + 1], (size, 2 * size)) for k in spots]
        rows = [work[k : k + 1, :] for k in spots]
        for j, k in enumerate(spots):
            pivot = columns[j][k : k + 1, :]
            inverse = lax.rsqrt(pivot)
            inverse = inverse * (1.5 - 0.5 * pivot * inverse * inverse)
            rows[j] = rows[j] * inverse
            columns[j] = columns[j] * inverse
            for later in range(j + 1, panel):
                weight = columns[j][first + later : first + later + 1, :]
                columns[later] = columns[later] - columns[j] * weight
                rows[later] = rows[later] - rows[j] * weight
        reduced = work
        for j in range(panel):
            reduced = reduced - columns[j] * rows[j]
        work = jnp.where(row_id >= first + panel, reduced, work)
        for j, k in enumerate(spots):
            work = jnp.where(row_id == k, rows[j], work)
    upper = jnp.where(row_id[:, :size] <= lane_id[:, :size], work[:, :size], 0.0)
    return upper, work[:, size:]


def finish_kernel(gram_ref, own_ref, image_ref, second_ref, next_ref, diag_ref, offdiag_ref):
    total = image_ref.shape[0] // 4
    vecs = diag_ref.shape[1]
    comps = next_ref.shape[0]
    zero = jnp.zeros((vecs, vecs), jnp.float32)
    eye = (
        lax.broadcasted_iota(jnp.int32, (vecs, vecs), 0)
        == lax.broadcasted_iota(jnp.int32, (vecs, vecs), 1)
    ).astype(jnp.float32)

    def grid(rows):
        return jnp.concatenate([jnp.concatenate(row, axis=1) for row in rows], axis=0)

    def block(matrix, row, column):
        return matrix[row * vecs : (row + 1) * vecs, column * vecs : (column + 1) * vecs]

    packed = gram_ref[...]
    moments = [packed[:vecs, k * vecs : (k + 1) * vecs] for k in range(4)]
    moments.append(
        jnp.concatenate([packed[vecs:, k * vecs : (k + 1) * vecs] for k in range(4)], axis=0)
    )
    gram = grid([moments[k : k + 3] for k in range(3)])
    upper_0, inverse_0 = eliminate(block(gram, 0, 0))
    spread = grid([[inverse_0, zero, zero], [zero, inverse_0, zero], [zero, zero, inverse_0]])
    krylov = dot_both(dot_rows(spread, gram), spread)
    alpha_1, alpha_1_t = block(krylov, 0, 1), block(krylov, 1, 0)
    change = grid([[eye, zero, zero], [-alpha_1_t, eye, zero], [zero, -alpha_1_t, eye]])
    moved = dot_both(dot_rows(change, krylov), change)
    upper_1, inverse_1 = eliminate(block(moved, 1, 1))
    second = grid([[zero, inverse_1, zero], [-upper_1, zero, inverse_1]])
    products = dot_both(dot_rows(second, moved), second)
    alpha_2, alpha_2_t = block(products, 0, 1), block(products, 1, 0)
    upper_2, inverse_2 = eliminate(block(products, 1, 1) - dot_rows(alpha_2_t, alpha_2))
    residual = jnp.concatenate([-upper_1, -dot_rows(alpha_2_t, inverse_1), inverse_1], axis=1)
    coefs = dot_rows(dot_rows(dot_rows(inverse_2, residual), change), spread)
    diag_ref[0] = alpha_1
    diag_ref[1] = alpha_2
    offdiag_ref[0] = upper_0
    offdiag_ref[1] = upper_1
    offdiag_ref[2] = upper_2
    for comp in range(comps):
        for floor in range(2):
            parts = (
                (own_ref, floor * total),
                (image_ref, (1 + floor) * total),
                (second_ref, floor * total),
            )
            for across in range(0, SUB, 2):
                mixed = dot_rows(coefs, paired_rows(parts, comp * vecs, vecs, across))
                next_ref[comp, :, floor, across, :] = mixed[:, :LANE]
                next_ref[comp, :, floor, across + 1, :] = mixed[:, LANE:]


def finish(gram, blocks, out_shape, vecs):
    return call_whole(
        finish_kernel,
        [
            jax.ShapeDtypeStruct(out_shape, jnp.float32),
            jax.ShapeDtypeStruct((2, vecs, vecs), jnp.float32),
            jax.ShapeDtypeStruct((3, vecs, vecs), jnp.float32),
        ],
        gram, *blocks,
    )


def exchange(value, axis, route):
    size = lax.axis_size(axis)
    return lax.ppermute(value, axis, [(i, route(i)) for i in range(size)])


def ring_pairs(stride, size, odd_first):
    def route(i):
        digit = i // stride % size
        if odd_first:
            partner = (digit + 1) % size if digit % 2 == 0 else (digit - 1) % size
        else:
            partner = (digit + 1) % size if digit % 2 == 1 else (digit - 1) % size
        return i + (partner - digit) * stride

    return route


def far_pairs(stride):
    partners = (3, 6, 5, 0, 7, 2, 1, 4)

    def route(i):
        digit = i // stride % 8
        return i + (partners[digit] - digit) * stride

    return route


def mesh_sum(value):
    steps = [
        ("slab", ring_pairs(1, 2, True)),
        ("dom", ring_pairs(1, 4, True)),
        ("dom", ring_pairs(1, 4, False)),
        ("slab", ring_pairs(2, 4, True)),
        ("slab", ring_pairs(2, 4, False)),
        ("slab", ring_pairs(8, 8, True)),
        ("slab", ring_pairs(8, 8, False)),
        ("slab", far_pairs(8)),
    ]
    for axis, route in steps:
        value = value + exchange(value, axis, route)
    return value


def shifted(value, axis, steps, wrap):
    size = lax.axis_size(axis)
    route = [(i, (i + steps) % size) for i in range(size) if wrap or 0 <= i + steps < size]
    return lax.ppermute(value, axis, route)


def gathered(elem_grad, elem_stress, elem_grade):
    capacity = elem_grad.shape[2]
    packed = jnp.concatenate(
        [
            elem_grad.reshape(24, capacity),
            elem_stress,
            elem_grade.astype(jnp.float32)[None],
            jnp.zeros((1, capacity), jnp.float32),
        ],
        axis=0,
    )
    ahead, behind = shifted(packed, "dom", 1, True), shifted(packed, "dom", -1, True)
    low, high = shifted(ahead[:16], "dom", 1, True), shifted(behind[16:], "dom", -1, True)
    return [packed, ahead, low, high, behind]


def per_device(
    elem_grad,
    elem_stress,
    elem_grade,
    grade_scale,
    part_counts,
    node_lists,
    stiff_diag,
    start_block,
):
    comps, vecs = start_block.shape[:2]
    total = comps * vecs
    own, edges = split_slab(start_block, stiff_diag)
    sources = gathered(elem_grad, elem_stress, elem_grade)
    from_left = shifted(edges[2:], "dom", 1, True)
    from_right = shifted(edges[:2], "dom", -1, True)
    columns = jnp.concatenate([from_left, from_right], axis=0)
    under = shifted(own, "slab", 1, False)
    over = shifted(own, "slab", -1, False)
    sources, under, over = lax.optimization_barrier((sources, under, over))
    low, top, below = local_stencils(part_counts, grade_scale, node_lists, sources)
    from_above = shifted(jnp.concatenate([low, below, columns], axis=0), "slab", -1, False)
    from_below = shifted(jnp.concatenate([top, columns], axis=0), "slab", 1, False)
    image, left, right, high = apply_first(
        under, own, over, low, top, below, from_above, from_below, columns, total
    )
    from_left = shifted(right, "dom", 1, True)
    from_right = shifted(left, "dom", -1, True)
    outer = first_gram(own, image, vecs)
    second, inner = apply_second(image, from_left, from_right, low, high, stiff_diag)
    last = inner[vecs:]
    packed = jnp.concatenate(
        [
            jnp.concatenate([outer[:vecs], outer[vecs:, vecs:], inner[:vecs]], axis=1),
            jnp.concatenate([last[k * 8 : k * 8 + 8] for k in range(vecs // 8)], axis=1),
        ],
        axis=0,
    )
    dof_count = (
        start_block.size // vecs * lax.axis_size("slab") * lax.axis_size("dom")
    )
    packed = mesh_sum(packed) / dof_count
    return finish(packed, (own, image, second), start_block.shape, vecs)


def solution(mesh):
    in_specs = (
        P(None, None, ("slab", "dom")),
        P(None, ("slab", "dom")),
        P(("slab", "dom")),
        P(),
        P("slab", None),
        P(None, "slab", None, "dom"),
        P(None, "slab", None, "dom"),
        P(None, None, "slab", None, "dom"),
    )
    out_specs = (P(None, None, "slab", None, "dom"), P(), P())
    return jax.shard_map(
        per_device, mesh=mesh, in_specs=in_specs, out_specs=out_specs, check_vma=False
    )
```

time: 150 us -> 109 us (0.73)
  starting transfers between devices: 67.2 us -> 42.3 us
  Pallas kernels: 42 us -> 27.6 us
  local copies, waits for them, and re-layouts: 4.36 us -> 0.98 us
    ppermute x19 -> x12, starting transfers between devices: 34.5 us -> 16.5 us  [shifted(): return lax.ppermute(value, axis, route)]
    pallas_call x3 -> x5, Pallas kernels: 31.3 us -> 20.5 us  [call_whole(): pl.pallas_call(kernel, out_shape=out_shape, in_specs=[vmem] * len(operand...]
    ppermute x8, starting transfers between devices: 32.7 us -> 25.8 us  [exchange(): return lax.ppermute(value, axis, [(i, route(i)) for i in range(size)])]
    pallas_call x1 -> x0, Pallas kernels: 3.76 us -> none  [edge_columns(): pl.pallas_call(edges_kernel, out_shape=[shape, shape], in_specs=[vmem] *...]
    ppermute x19 -> x12, waiting for transfers between devices: 15 us -> 18 us  [shifted(): return lax.ppermute(value, axis, route)]
    slice x11 -> x7, local copies, waits for them, and re-layouts: 2.12 us -> 0.13 us  [the longest x1 0.07 us: per_device(): outer[vecs:, vecs:]]
    ppermute x8, waiting for transfers between devices: 16.8 us -> 15 us  [exchange(): return lax.ppermute(value, axis, [(i, route(i)) for i in range(size)])]
  transfers between devices with their start and end apart: 27 -> 20, of which waited for: 14 -> 13; matrix products, arithmetic and copies ran while one was open for 3% -> 0% of each run, Pallas kernels for 7% -> 9%
where the time goes in v2:
time: 109 us; the launch traced here: 107 us
  starting transfers between devices  42.3 us (39%)
  waiting for transfers between devices  33 us (30%)
  Pallas kernels  27.6 us (25%)
  other arithmetic  2.24 us (2%)
    ppermute x8, starting transfers between devices, exchange(): return lax.ppermute(value, axis, [(i, route(i)) for i in range(size)])  25.8 us
    pallas_call x5, Pallas kernels, call_whole(): pl.pallas_call(kernel, out_shape=out_shape, in_specs=[vmem] * len(operand...  20.5 us
    ppermute x12, waiting for transfers between devices, shifted(): return lax.ppermute(value, axis, route)  18 us
    ppermute x12, starting transfers between devices, shifted(): return lax.ppermute(value, axis, route)  16.5 us
    ppermute x8, waiting for transfers between devices, exchange(): return lax.ppermute(value, axis, [(i, route(i)) for i in range(size)])  15 us
    pallas_call x1, Pallas kernels, local_stencils(): pl.pallas_call(stencil_kernel, out_shape=[jax.ShapeDtypeStruct((27, SUB,...  7.12 us
  transfers between devices with their start and end apart: 20, of which 13 were waited for; matrix products, arithmetic and copies ran while one was open for 0% of the time, Pallas kernels for 9%

profile of v2, /device:TPU:8, one launch (start us, length us, event | category | flops | bytes accessed | tf_op | source)
XLA Modules:
  0.0 106.9 jit_solution(15065143568605545874)
XLA Ops:
  0.6 0.8 convert_element_type.3
  1.5 0.1 pad.19.clone
  1.6 1.3 %maximum_maximum_fusion.refs_0_ = f32[32,5376]{1,0:T(8,128)S(1)} fusion(f32[1,5376]{1,0:T(1,128)S(1)} %broadcast_in_dim.6, f32[6,5376]{1,0:T(8,128)} %param.9, f32[24,5376]{1,0:T(8,128)} %bitcast.2, f32[32]{0:T(128)S(1)} %pad.19.clone), kind=kLoop, calls=%fused_computation | loop fusion | flops 516096 | bytes 1354880 | tf_op jit(solution)/shard_map/concatenate | solution.py:496
  2.8 1.7 %collective-permute-start = (f32[32,5376]{1,0:T(8,128)S(1)}, f32[32,5376]{1,0:T(8,128)S(1)}, u32[]{:S(2)}, u32[]{:S(2)}) collective-permute-start(f32[32,5376]{1,0:T(8,128)S(1)} %maximum_maximum_fusion.refs_0_), channel_id=1, source_target_pairs={{0,1},{1,2},{2,3},{3,0},{4,5},{5,6},{6,7},{7,4},{8,9},{9,10},{10,1... | collective-permute-start | bytes 2064392 | tf_op jit(solution)/shard_map/ppermute | solution.py:491
  4.5 0.7 collective-permute-start.2
  5.2 0.7 copy-done.1
  5.9 0.8 shard_map.103
  6.8 1.3 %collective-permute-start.4 = (f32[198,8,128]{2,1,0:T(8,128)S(1)}, f32[198,8,128]{2,1,0:T(8,128)S(1)}, u32[]{:S(2)}, u32[]{:S(2)}) collective-permute-start(f32[198,8,128]{2,1,0:T(8,128)S(1)} %get-tuple-element.21.own_ref), channel_id=1, source_target_pairs={{0,4},{4,8},{8,12},{12,16},{16,20},{20,24},{24,28},{28,32},{32,36}... | collective-permute-start | bytes 2433032 | tf_op jit(solution)/shard_map/ppermute | solution.py:491
  8.1 1.3 %collective-permute-start.5 = (f32[198,8,128]{2,1,0:T(8,128)S(1)}, f32[198,8,128]{2,1,0:T(8,128)S(1)}, u32[]{:S(2)}, u32[]{:S(2)}) collective-permute-start(f32[198,8,128]{2,1,0:T(8,128)S(1)} %get-tuple-element.21.own_ref), channel_id=1, source_target_pairs={{4,0},{8,4},{12,8},{16,12},{20,16},{24,20},{28,24},{32,28},{36,32}... | collective-permute-start | bytes 2433032 | tf_op jit(solution)/shard_map/ppermute | solution.py:491
  9.4 10.7 %collective-permute-done.refs_1_ = f32[32,5376]{1,0:T(8,128)S(1)} collective-permute-done((f32[32,5376]{1,0:T(8,128)S(1)}, f32[32,5376]{1,0:T(8,128)S(1)}, u32[]{:S(2)}, u32[]{:S(2)}) %collective-permute-start) | collective-permute-done | bytes 688160 | tf_op jit(solution)/shard_map/ppermute | solution.py:491
  20.1 1.7 %collective-permute-start.1 = (f32[16,5376]{1,0:T(8,128)S(1)}, f32[16,5376]{1,0:T(8,128)S(1)}, u32[]{:S(2)}, u32[]{:S(2)}) collective-permute-start(f32[16,5376]{1,0:T(8,128)S(1)} %slice.49), channel_id=1, source_target_pairs={{0,1},{1,2},{2,3},{3,0},{4,5},{5,6},{6,7},{7,4},{8,9},{9,10},{10,1... | collective-permute-start | bytes 1032200 | tf_op jit(solution)/shard_map/ppermute | solution.py:491
  21.8 0.0 collective-permute-done.2.refs_4_
  21.8 0.5 collective-permute-start.3
  22.3 2.9 %collective-permute-start.7 = (f32[2,8,128]{2,1,0:T(8,128)S(1)}, f32[2,8,128]{2,1,0:T(8,128)S(1)}, u32[]{:S(2)}, u32[]{:S(2)}) collective-permute-start(f32[2,8,128]{2,1,0:T(8,128)S(1)} %get-tuple-element.44), channel_id=1, source_target_pairs={{0,3},{1,0},{2,1},{3,2},{4,7},{5,4},{6,5},{7,6},{8,11},{9,8},{10,9... | collective-permute-start | bytes 24584 | tf_op jit(solution)/shard_map/ppermute | solution.py:491
  25.3 0.0 collective-permute-done.4.under_ref
  25.3 0.0 collective-permute-start.6
  25.3 3.7 %collective-permute-done.1.refs_2_ = f32[16,5376]{1,0:T(8,128)S(1)} collective-permute-done((f32[16,5376]{1,0:T(8,128)S(1)}, f32[16,5376]{1,0:T(8,128)S(1)}, u32[]{:S(2)}, u32[]{:S(2)}) %collective-permute-start.1) | collective-permute-done | bytes 344096 | tf_op jit(solution)/shard_map/ppermute | solution.py:491
  29.0 1.6 %collective-permute-done.3.refs_3_ = f32[16,5376]{1,0:T(8,128)S(1)} collective-permute-done((f32[16,5376]{1,0:T(8,128)S(1)}, f32[16,5376]{1,0:T(8,128)S(1)}, u32[]{:S(2)}, u32[]{:S(2)}) %collective-permute-start.3) | collective-permute-done | bytes 344096 | tf_op jit(solution)/shard_map/ppermute | solution.py:491
  30.6 7.1 %shard_map.104 = (f32[27,8,128]{2,1,0:T(8,128)S(1)}, f32[18,8,128]{2,1,0:T(8,128)S(1)}, f32[18,8,128]{2,1,0:T(8,128)S(1)}) custom-call(s32[1,4]{1,0:T(1,128)S(1)} %copy-done.4, f32[16]{0:T(128)S(1)} %copy-done.5, s32[4,2,8,128]{3,2,1,0:T(8,128)S(1)} %copy-done.3, f32[32,5376]{1,0:T(8,128)S(1)} %maximum_maximum_fusion.refs_0_, ...), custom_call_target="tpu_custom_call" | custom-call | tf_op jit(solution)/shard_map/pallas_call | solution.py:111
  37.8 1.3 %collective-permute-start.8 = (f32[49,8,128]{2,1,0:T(8,128)S(1)}, f32[49,8,128]{2,1,0:T(8,128)S(1)}, u32[]{:S(2)}, u32[]{:S(2)}) collective-permute-start(f32[49,8,128]{2,1,0:T(8,128)S(1)} %pad_maximum_fusion), channel_id=1, source_target_pairs={{4,0},{8,4},{12,8},{16,12},{20,16},{24,20},{28,24},{32,28},{36,32}... | collective-permute-start | bytes 602120 | tf_op jit(solution)/shard_map/ppermute | solution.py:491
  39.1 3.0 %collective-permute-start.9 = (f32[22,8,128]{2,1,0:T(8,128)S(1)}, f32[22,8,128]{2,1,0:T(8,128)S(1)}, u32[]{:S(2)}, u32[]{:S(2)}) collective-permute-start(f32[22,8,128]{2,1,0:T(8,128)S(1)} %pad_maximum_fusion.1), channel_id=1, source_target_pairs={{0,4},{4,8},{8,12},{12,16},{16,20},{20,24},{24,28},{28,32},{32,36}... | collective-permute-start | bytes 270344 | tf_op jit(solution)/shard_map/ppermute | solution.py:491
  42.2 0.9 collective-permute-done.9.from_below_ref
  43.1 5.5 %shard_map.105 = (f32[384,8,128]{2,1,0:T(8,128)S(1)}, f32[4,8,128]{2,1,0:T(8,128)S(1)}, f32[4,8,128]{2,1,0:T(8,128)S(1)}, f32[27,8,128]{2,1,0:T(8,128)S(1)}) custom-call(f32[198,8,128]{2,1,0:T(8,128)S(1)} %collective-permute-done.4.under_ref, f32[198,8,128]{2,1,0:T(8,128)S(1)} %get-tuple-element.21.own_ref, ...), custom_call_target="tpu_custom_call" | custom-call | tf_op jit(solution)/shard_map/pallas_call | solution.py:298
  48.6 0.0 copy-start.2
  48.6 1.4 %collective-permute-start.10 = (f32[4,8,128]{2,1,0:T(8,128)S(1)}, f32[4,8,128]{2,1,0:T(8,128)S(1)}, u32[]{:S(2)}, u32[]{:S(2)}) collective-permute-start(f32[4,8,128]{2,1,0:T(8,128)S(1)} %get-tuple-element.34), channel_id=1, source_target_pairs={{0,1},{1,2},{2,3},{3,0},{4,5},{5,6},{6,7},{7,4},{8,9},{9,10},{10,1... | collective-permute-start | bytes 49160 | tf_op jit(solution)/shard_map/ppermute | solution.py:491
  49.9 0.7 collective-permute-start.11
  50.7 1.9 %shard_map.106 = f32[64,64]{1,0:T(8,128)S(1)} custom-call(f32[198,8,128]{2,1,0:T(8,128)S(1)} %get-tuple-element.21.own_ref, f32[384,8,128]{2,1,0:T(8,128)S(1)} %get-tuple-element.33.image_ref), custom_call_target="tpu_custom_call" | custom-call | tf_op jit(solution)/shard_map/pallas_call | solution.py:298
  52.6 0.1 slice.52
  52.7 1.0 collective-permute-done.11.from_right_ref
  53.7 3.8 %shard_map.107 = (f32[192,8,128]{2,1,0:T(8,128)S(1)}, f32[64,32]{1,0:T(8,128)S(1)}) custom-call(f32[384,8,128]{2,1,0:T(8,128)S(1)} %get-tuple-element.33.image_ref, f32[4,8,128]{2,1,0:T(8,128)S(1)} %collective-permute-done.10.from_left_ref, f32[4,8,128]{2,1,0:T(8,128)S(1)} %collective-permute-done.11.from_right_ref, ...), custom_call_target="tpu_custom_call" | custom-call | tf_op jit(solution)/shard_map/pallas_call | solution.py:298
  57.6 0.1 maximum_maximum_fusion.1
  57.6 1.4 %collective-permute-start.12 = (f32[40,128]{1,0:T(8,128)S(1)}, f32[40,128]{1,0:T(8,128)S(1)}, u32[]{:S(2)}, u32[]{:S(2)}) collective-permute-start(f32[40,128]{1,0:T(8,128)S(1)} %maximum_maximum_fusion.1), channel_id=1, source_target_pairs={{0,4},{4,0},{8,12},{12,8},{16,20},{20,16},{24,28},{28,24},{32,36},... | collective-permute-start | bytes 61448 | tf_op jit(solution)/shard_map/ppermute | solution.py:447
  59.0 0.8 collective-permute-done.12
  59.9 1.8 %collective-permute-start.13 = (f32[40,128]{1,0:T(8,128)S(1)}, f32[40,128]{1,0:T(8,128)S(1)}, u32[]{:S(2)}, u32[]{:S(2)}) collective-permute-start(f32[40,128]{1,0:T(8,128)S(1)} %add.24), channel_id=1, source_target_pairs={{0,1},{1,0},{2,3},{3,2},{4,5},{5,4},{6,7},{7,6},{8,9},{9,8},{10,11... | collective-permute-start | bytes 61448 | tf_op jit(solution)/shard_map/ppermute | solution.py:447
  61.7 2.0 %collective-permute-done.13 = f32[40,128]{1,0:T(8,128)S(1)} collective-permute-done((f32[40,128]{1,0:T(8,128)S(1)}, f32[40,128]{1,0:T(8,128)S(1)}, u32[]{:S(2)}, u32[]{:S(2)}) %collective-permute-start.13) | collective-permute-done | bytes 20512 | tf_op jit(solution)/shard_map/ppermute | solution.py:447
  63.6 1.7 %collective-permute-start.14 = (f32[40,128]{1,0:T(8,128)S(1)}, f32[40,128]{1,0:T(8,128)S(1)}, u32[]{:S(2)}, u32[]{:S(2)}) collective-permute-start(f32[40,128]{1,0:T(8,128)S(1)} %add.25), channel_id=1, source_target_pairs={{0,3},{1,2},{2,1},{3,0},{4,7},{5,6},{6,5},{7,4},{8,11},{9,10},{10,... | collective-permute-start | bytes 61448 | tf_op jit(solution)/shard_map/ppermute | solution.py:447
  65.4 2.0 %collective-permute-done.14 = f32[40,128]{1,0:T(8,128)S(1)} collective-permute-done((f32[40,128]{1,0:T(8,128)S(1)}, f32[40,128]{1,0:T(8,128)S(1)}, u32[]{:S(2)}, u32[]{:S(2)}) %collective-permute-start.14) | collective-permute-done | bytes 20512 | tf_op jit(solution)/shard_map/ppermute | solution.py:447
  67.4 3.8 %collective-permute-start.15 = (f32[40,128]{1,0:T(8,128)S(1)}, f32[40,128]{1,0:T(8,128)S(1)}, u32[]{:S(2)}, u32[]{:S(2)}) collective-permute-start(f32[40,128]{1,0:T(8,128)S(1)} %add.26), channel_id=1, source_target_pairs={{0,8},{4,12},{8,0},{12,4},{16,24},{20,28},{24,16},{28,20},{32,40},... | collective-permute-start | bytes 61448 | tf_op jit(solution)/shard_map/ppermute | solution.py:447
  71.2 1.8 %collective-permute-done.15 = f32[40,128]{1,0:T(8,128)S(1)} collective-permute-done((f32[40,128]{1,0:T(8,128)S(1)}, f32[40,128]{1,0:T(8,128)S(1)}, u32[]{:S(2)}, u32[]{:S(2)}) %collective-permute-start.15) | collective-permute-done | bytes 20512 | tf_op jit(solution)/shard_map/ppermute | solution.py:447
  73.0 3.5 %collective-permute-start.16 = (f32[40,128]{1,0:T(8,128)S(1)}, f32[40,128]{1,0:T(8,128)S(1)}, u32[]{:S(2)}, u32[]{:S(2)}) collective-permute-start(f32[40,128]{1,0:T(8,128)S(1)} %add.27), channel_id=1, source_target_pairs={{0,24},{4,28},{8,16},{12,20},{16,8},{20,12},{24,0},{28,4},{32,56},... | collective-permute-start | bytes 61448 | tf_op jit(solution)/shard_map/ppermute | solution.py:447
  76.5 1.8 %collective-permute-done.16 = f32[40,128]{1,0:T(8,128)S(1)} collective-permute-done((f32[40,128]{1,0:T(8,128)S(1)}, f32[40,128]{1,0:T(8,128)S(1)}, u32[]{:S(2)}, u32[]{:S(2)}) %collective-permute-start.16) | collective-permute-done | bytes 20512 | tf_op jit(solution)/shard_map/ppermute | solution.py:447
  78.2 4.5 %collective-permute-start.17 = (f32[40,128]{1,0:T(8,128)S(1)}, f32[40,128]{1,0:T(8,128)S(1)}, u32[]{:S(2)}, u32[]{:S(2)}) collective-permute-start(f32[40,128]{1,0:T(8,128)S(1)} %add.28), channel_id=1, source_target_pairs={{0,32},{4,36},{8,40},{12,44},{16,48},{20,52},{24,56},{28,60},{32,0... | collective-permute-start | bytes 61448 | tf_op jit(solution)/shard_map/ppermute | solution.py:447
  82.7 1.8 %collective-permute-done.17 = f32[40,128]{1,0:T(8,128)S(1)} collective-permute-done((f32[40,128]{1,0:T(8,128)S(1)}, f32[40,128]{1,0:T(8,128)S(1)}, u32[]{:S(2)}, u32[]{:S(2)}) %collective-permute-start.17) | collective-permute-done | bytes 20512 | tf_op jit(solution)/shard_map/ppermute | solution.py:447
  84.5 6.3 %collective-permute-start.18 = (f32[40,128]{1,0:T(8,128)S(1)}, f32[40,128]{1,0:T(8,128)S(1)}, u32[]{:S(2)}, u32[]{:S(2)}) collective-permute-start(f32[40,128]{1,0:T(8,128)S(1)} %add.29), channel_id=1, source_target_pairs={{0,224},{4,228},{8,232},{12,236},{16,240},{20,244},{24,248},{28,25... | collective-permute-start | bytes 61448 | tf_op jit(solution)/shard_map/ppermute | solution.py:447
  90.8 1.8 %collective-permute-done.18 = f32[40,128]{1,0:T(8,128)S(1)} collective-permute-done((f32[40,128]{1,0:T(8,128)S(1)}, f32[40,128]{1,0:T(8,128)S(1)}, u32[]{:S(2)}, u32[]{:S(2)}) %collective-permute-start.18) | collective-permute-done | bytes 20512 | tf_op jit(solution)/shard_map/ppermute | solution.py:447
  92.6 2.8 %collective-permute-start.19 = (f32[40,128]{1,0:T(8,128)S(1)}, f32[40,128]{1,0:T(8,128)S(1)}, u32[]{:S(2)}, u32[]{:S(2)}) collective-permute-start(f32[40,128]{1,0:T(8,128)S(1)} %add.30), channel_id=1, source_target_pairs={{0,96},{4,100},{8,104},{12,108},{16,112},{20,116},{24,120},{28,124... | collective-permute-start | bytes 61448 | tf_op jit(solution)/shard_map/ppermute | solution.py:447
  95.3 3.1 %collective-permute-done.19 = f32[40,128]{1,0:T(8,128)S(1)} collective-permute-done((f32[40,128]{1,0:T(8,128)S(1)}, f32[40,128]{1,0:T(8,128)S(1)}, u32[]{:S(2)}, u32[]{:S(2)}) %collective-permute-start.19) | collective-permute-done | bytes 20512 | tf_op jit(solution)/shard_map/ppermute | solution.py:447
  98.5 8.4 %shard_map.108 = (f32[3,32,2,8,128]{4,3,2,1,0:T(8,128)}, f32[2,32,32]{2,1,0:T(8,128)}, f32[3,32,32]{2,1,0:T(8,128)}) custom-call(f32[40,128]{1,0:T(8,128)S(1)} %add_multiply_fusion.gram_ref, f32[198,8,128]{2,1,0:T(8,128)S(1)} %get-tuple-element.21.own_ref, f32[384,8,128]{2,1,0:T(8,128)S(1)} %get-tuple-element.33.image_ref, ...), custom_call_target="tpu_custom_call" | custom-call | tf_op jit(solution)/shard_map/pallas_call | solution.py:298
  (33 shorter events, 0.2 us)
Async XLA Ops:
  0.6 4.6 %copy-start = (f32[3,32,2,8,128]{4,3,2,1,0:T(8,128)S(1)}, f32[3,32,2,8,128]{4,3,2,1,0:T(8,128)}, u32[]{:S(2)}) copy-start(f32[3,32,2,8,128]{4,3,2,1,0:T(8,128)} %start_ref.1) | copy-start | bytes 2359300
  1.6 29.1 %copy-start.3 = (s32[4,2,8,128]{3,2,1,0:T(8,128)S(1)}, s32[4,2,8,128]{3,2,1,0:T(8,128)}, u32[]{:S(2)}) copy-start(s32[4,2,8,128]{3,2,1,0:T(8,128)} %lists_ref.1) | copy-start | bytes 98308
  1.6 29.1 %copy-start.4 = (s32[1,4]{1,0:T(1,128)S(1)}, s32[1,4]{1,0:T(1,128)}, u32[]{:S(2)}) copy-start(s32[1,4]{1,0:T(1,128)} %counts_ref.1) | copy-start | bytes 52
  1.6 29.1 %copy-start.5 = (f32[16]{0:T(128)S(1)}, f32[16]{0:T(128)}, u32[]{:S(2)}) copy-start(f32[16]{0:T(128)} %table_ref.1) | copy-start | bytes 196
  2.8 17.3 %collective-permute-start = (f32[32,5376]{1,0:T(8,128)S(1)}, f32[32,5376]{1,0:T(8,128)S(1)}, u32[]{:S(2)}, u32[]{:S(2)}) collective-permute-start(f32[32,5376]{1,0:T(8,128)S(1)} %maximum_maximum_fusion.refs_0_), channel_id=1, source_target_pairs={{0,1},{1,2},{2,3},{3,0},{4,5},{5,6},{6,7},{7,4},{8,9},{9,10},{10,1... | collective-permute-start | bytes 2064392 | tf_op jit(solution)/shard_map/ppermute | solution.py:491
  4.5 17.3 %collective-permute-start.2 = (f32[32,5376]{1,0:T(8,128)S(1)}, f32[32,5376]{1,0:T(8,128)S(1)}, u32[]{:S(2)}, u32[]{:S(2)}) collective-permute-start(f32[32,5376]{1,0:T(8,128)S(1)} %maximum_maximum_fusion.refs_0_), channel_id=1, source_target_pairs={{0,3},{1,0},{2,1},{3,2},{4,7},{5,4},{6,5},{7,6},{8,11},{9,8},{10,9... | collective-permute-start | bytes 2064392 | tf_op jit(solution)/shard_map/ppermute | solution.py:491
  5.2 0.7 copy-start.1
  6.8 18.5 %collective-permute-start.4 = (f32[198,8,128]{2,1,0:T(8,128)S(1)}, f32[198,8,128]{2,1,0:T(8,128)S(1)}, u32[]{:S(2)}, u32[]{:S(2)}) collective-permute-start(f32[198,8,128]{2,1,0:T(8,128)S(1)} %get-tuple-element.21.own_ref), channel_id=1, source_target_pairs={{0,4},{4,8},{8,12},{12,16},{16,20},{20,24},{24,28},{28,32},{32,36}... | collective-permute-start | bytes 2433032 | tf_op jit(solution)/shard_map/ppermute | solution.py:491
  8.1 17.2 %collective-permute-start.5 = (f32[198,8,128]{2,1,0:T(8,128)S(1)}, f32[198,8,128]{2,1,0:T(8,128)S(1)}, u32[]{:S(2)}, u32[]{:S(2)}) collective-permute-start(f32[198,8,128]{2,1,0:T(8,128)S(1)} %get-tuple-element.21.own_ref), channel_id=1, source_target_pairs={{4,0},{8,4},{12,8},{16,12},{20,16},{24,20},{28,24},{32,28},{36,32}... | collective-permute-start | bytes 2433032 | tf_op jit(solution)/shard_map/ppermute | solution.py:491
  20.1 8.9 %collective-permute-start.1 = (f32[16,5376]{1,0:T(8,128)S(1)}, f32[16,5376]{1,0:T(8,128)S(1)}, u32[]{:S(2)}, u32[]{:S(2)}) collective-permute-start(f32[16,5376]{1,0:T(8,128)S(1)} %slice.49), channel_id=1, source_target_pairs={{0,1},{1,2},{2,3},{3,0},{4,5},{5,6},{6,7},{7,4},{8,9},{9,10},{10,1... | collective-permute-start | bytes 1032200 | tf_op jit(solution)/shard_map/ppermute | solution.py:491
  21.8 8.8 %collective-permute-start.3 = (f32[16,5376]{1,0:T(8,128)S(1)}, f32[16,5376]{1,0:T(8,128)S(1)}, u32[]{:S(2)}, u32[]{:S(2)}) collective-permute-start(f32[16,5376]{1,0:T(8,128)S(1)} %slice.50), channel_id=1, source_target_pairs={{0,3},{1,0},{2,1},{3,2},{4,7},{5,4},{6,5},{7,6},{8,11},{9,8},{10,9... | collective-permute-start | bytes 1032200 | tf_op jit(solution)/shard_map/ppermute | solution.py:491
  22.3 15.4 %collective-permute-start.7 = (f32[2,8,128]{2,1,0:T(8,128)S(1)}, f32[2,8,128]{2,1,0:T(8,128)S(1)}, u32[]{:S(2)}, u32[]{:S(2)}) collective-permute-start(f32[2,8,128]{2,1,0:T(8,128)S(1)} %get-tuple-element.44), channel_id=1, source_target_pairs={{0,3},{1,0},{2,1},{3,2},{4,7},{5,4},{6,5},{7,6},{8,11},{9,8},{10,9... | collective-permute-start | bytes 24584 | tf_op jit(solution)/shard_map/ppermute | solution.py:491
  25.3 12.5 %collective-permute-start.6 = (f32[2,8,128]{2,1,0:T(8,128)S(1)}, f32[2,8,128]{2,1,0:T(8,128)S(1)}, u32[]{:S(2)}, u32[]{:S(2)}) collective-permute-start(f32[2,8,128]{2,1,0:T(8,128)S(1)} %get-tuple-element.43), channel_id=1, source_target_pairs={{0,1},{1,2},{2,3},{3,0},{4,5},{5,6},{6,7},{7,4},{8,9},{9,10},{10,1... | collective-permute-start | bytes 24584 | tf_op jit(solution)/shard_map/ppermute | solution.py:491
  37.8 5.3 %collective-permute-start.8 = (f32[49,8,128]{2,1,0:T(8,128)S(1)}, f32[49,8,128]{2,1,0:T(8,128)S(1)}, u32[]{:S(2)}, u32[]{:S(2)}) collective-permute-start(f32[49,8,128]{2,1,0:T(8,128)S(1)} %pad_maximum_fusion), channel_id=1, source_target_pairs={{4,0},{8,4},{12,8},{16,12},{20,16},{24,20},{28,24},{32,28},{36,32}... | collective-permute-start | bytes 602120 | tf_op jit(solution)/shard_map/ppermute | solution.py:491
  39.1 4.0 %collective-permute-start.9 = (f32[22,8,128]{2,1,0:T(8,128)S(1)}, f32[22,8,128]{2,1,0:T(8,128)S(1)}, u32[]{:S(2)}, u32[]{:S(2)}) collective-permute-start(f32[22,8,128]{2,1,0:T(8,128)S(1)} %pad_maximum_fusion.1), channel_id=1, source_target_pairs={{0,4},{4,8},{8,12},{12,16},{16,20},{20,24},{24,28},{28,32},{32,36}... | collective-permute-start | bytes 270344 | tf_op jit(solution)/shard_map/ppermute | solution.py:491
  48.6 5.1 %copy-start.2 = (f32[3,2,8,128]{3,2,1,0:T(8,128)S(1)}, f32[3,2,8,128]{3,2,1,0:T(8,128)}, u32[]{:S(2)}) copy-start(f32[3,2,8,128]{3,2,1,0:T(8,128)} %diag_ref.3) | copy-start | bytes 73732
  48.6 4.1 %collective-permute-start.10 = (f32[4,8,128]{2,1,0:T(8,128)S(1)}, f32[4,8,128]{2,1,0:T(8,128)S(1)}, u32[]{:S(2)}, u32[]{:S(2)}) collective-permute-start(f32[4,8,128]{2,1,0:T(8,128)S(1)} %get-tuple-element.34), channel_id=1, source_target_pairs={{0,1},{1,2},{2,3},{3,0},{4,5},{5,6},{6,7},{7,4},{8,9},{9,10},{10,1... | collective-permute-start | bytes 49160 | tf_op jit(solution)/shard_map/ppermute | solution.py:491
  49.9 3.7 %collective-permute-start.11 = (f32[4,8,128]{2,1,0:T(8,128)S(1)}, f32[4,8,128]{2,1,0:T(8,128)S(1)}, u32[]{:S(2)}, u32[]{:S(2)}) collective-permute-start(f32[4,8,128]{2,1,0:T(8,128)S(1)} %get-tuple-element.35), channel_id=1, source_target_pairs={{0,3},{1,0},{2,1},{3,2},{4,7},{5,4},{6,5},{7,6},{8,11},{9,8},{10,9... | collective-permute-start | bytes 49160 | tf_op jit(solution)/shard_map/ppermute | solution.py:491
  57.6 2.2 %collective-permute-start.12 = (f32[40,128]{1,0:T(8,128)S(1)}, f32[40,128]{1,0:T(8,128)S(1)}, u32[]{:S(2)}, u32[]{:S(2)}) collective-permute-start(f32[40,128]{1,0:T(8,128)S(1)} %maximum_maximum_fusion.1), channel_id=1, source_target_pairs={{0,4},{4,0},{8,12},{12,8},{16,20},{20,16},{24,28},{28,24},{32,36},... | collective-permute-start | bytes 61448 | tf_op jit(solution)/shard_map/ppermute | solution.py:447
  59.9 3.8 %collective-permute-start.13 = (f32[40,128]{1,0:T(8,128)S(1)}, f32[40,128]{1,0:T(8,128)S(1)}, u32[]{:S(2)}, u32[]{:S(2)}) collective-permute-start(f32[40,128]{1,0:T(8,128)S(1)} %add.24), channel_id=1, source_target_pairs={{0,1},{1,0},{2,3},{3,2},{4,5},{5,4},{6,7},{7,6},{8,9},{9,8},{10,11... | collective-permute-start | bytes 61448 | tf_op jit(solution)/shard_map/ppermute | solution.py:447
  63.6 3.8 %collective-permute-start.14 = (f32[40,128]{1,0:T(8,128)S(1)}, f32[40,128]{1,0:T(8,128)S(1)}, u32[]{:S(2)}, u32[]{:S(2)}) collective-permute-start(f32[40,128]{1,0:T(8,128)S(1)} %add.25), channel_id=1, source_target_pairs={{0,3},{1,2},{2,1},{3,0},{4,7},{5,6},{6,5},{7,4},{8,11},{9,10},{10,... | collective-permute-start | bytes 61448 | tf_op jit(solution)/shard_map/ppermute | solution.py:447
  67.4 5.5 %collective-permute-start.15 = (f32[40,128]{1,0:T(8,128)S(1)}, f32[40,128]{1,0:T(8,128)S(1)}, u32[]{:S(2)}, u32[]{:S(2)}) collective-permute-start(f32[40,128]{1,0:T(8,128)S(1)} %add.26), channel_id=1, source_target_pairs={{0,8},{4,12},{8,0},{12,4},{16,24},{20,28},{24,16},{28,20},{32,40},... | collective-permute-start | bytes 61448 | tf_op jit(solution)/shard_map/ppermute | solution.py:447
  73.0 5.2 %collective-permute-start.16 = (f32[40,128]{1,0:T(8,128)S(1)}, f32[40,128]{1,0:T(8,128)S(1)}, u32[]{:S(2)}, u32[]{:S(2)}) collective-permute-start(f32[40,128]{1,0:T(8,128)S(1)} %add.27), channel_id=1, source_target_pairs={{0,24},{4,28},{8,16},{12,20},{16,8},{20,12},{24,0},{28,4},{32,56},... | collective-permute-start | bytes 61448 | tf_op jit(solution)/shard_map/ppermute | solution.py:447
  78.2 6.3 %collective-permute-start.17 = (f32[40,128]{1,0:T(8,128)S(1)}, f32[40,128]{1,0:T(8,128)S(1)}, u32[]{:S(2)}, u32[]{:S(2)}) collective-permute-start(f32[40,128]{1,0:T(8,128)S(1)} %add.28), channel_id=1, source_target_pairs={{0,32},{4,36},{8,40},{12,44},{16,48},{20,52},{24,56},{28,60},{32,0... | collective-permute-start | bytes 61448 | tf_op jit(solution)/shard_map/ppermute | solution.py:447
  84.5 8.1 %collective-permute-start.18 = (f32[40,128]{1,0:T(8,128)S(1)}, f32[40,128]{1,0:T(8,128)S(1)}, u32[]{:S(2)}, u32[]{:S(2)}) collective-permute-start(f32[40,128]{1,0:T(8,128)S(1)} %add.29), channel_id=1, source_target_pairs={{0,224},{4,228},{8,232},{12,236},{16,240},{20,244},{24,248},{28,25... | collective-permute-start | bytes 61448 | tf_op jit(solution)/shard_map/ppermute | solution.py:447
  92.6 5.9 %collective-permute-start.19 = (f32[40,128]{1,0:T(8,128)S(1)}, f32[40,128]{1,0:T(8,128)S(1)}, u32[]{:S(2)}, u32[]{:S(2)}) collective-permute-start(f32[40,128]{1,0:T(8,128)S(1)} %add.30), channel_id=1, source_target_pairs={{0,96},{4,100},{8,104},{12,108},{16,112},{20,116},{24,120},{28,124... | collective-permute-start | bytes 61448 | tf_op jit(solution)/shard_map/ppermute | solution.py:447

commit v3 on v2

--- a/solution.py
+++ b/solution.py
@@ -3,11 +3,14 @@
 from jax import lax
 from jax.experimental import pallas as pl
 from jax.experimental.pallas import tpu as pltpu
+from jax.sharding import Mesh
 from jax.sharding import PartitionSpec as P
 
 highest = lax.Precision.HIGHEST
 SUB, LANE = 8, 128
 ROWS = 31
+UNITS = 3
+SLAB = ("z", "x", "core")
 
 
 def lane_pick(values, index):
@@ -43,20 +46,26 @@
         halves = ((0,), (1,), (2, 3), (4,))[part]
 
         def pick_groups(step, carry):
-            for unit in range(2):
-                group = step * 2 + unit
-                span = pl.ds(pl.multiple_of(group * LANE, LANE), LANE)
-                here = [group_of[layer] == group for layer in range(2)]
-                for row in range(ROWS):
-                    half, line = divmod(row, 16) if len(halves) == 2 else (0, row)
-                    source = sources[halves[half]]
-                    line = jnp.broadcast_to(source[line : line + 1, span], (SUB, LANE))
+            spans, here = [], []
+            for unit in range(UNITS):
+                group = step * UNITS + unit
+                spans.append(pl.ds(pl.multiple_of(group * LANE, LANE), LANE))
+                here.append([group_of[layer] == group for layer in range(2)])
+            for row in range(ROWS):
+                half, line = divmod(row, 16) if len(halves) == 2 else (0, row)
+                source = sources[halves[half]]
+                found = [picked_ref[layer, row] for layer in range(2)]
+                for unit in range(UNITS):
+                    values = jnp.broadcast_to(source[line : line + 1, spans[unit]], (SUB, LANE))
                     for layer in range(2):
-                        got = lane_pick(line, lane_of[layer])
-                        picked_ref[layer, row] = jnp.where(here[layer], got, picked_ref[layer, row])
+                        got = lane_pick(values, lane_of[layer])
+                        found[layer] = jnp.where(here[unit][layer], got, found[layer])
+                for layer in range(2):
+                    picked_ref[layer, row] = found[layer]
             return carry
 
-        lax.fori_loop(0, (count + 2 * LANE - 1) // (2 * LANE), pick_groups, 0)
+        width = UNITS * LANE
+        lax.fori_loop(0, (count + width - 1) // width, pick_groups, 0)
     low_ref[...] = jnp.zeros(low_ref.shape, jnp.float32)
     top_ref[...] = jnp.zeros(top_ref.shape, jnp.float32)
     below_ref[...] = jnp.zeros(below_ref.shape, jnp.float32)
@@ -217,7 +226,7 @@
     total = image_ref.shape[0] // 4
     comps = (own_ref.shape[0] - 2 * total) // 2
     diag_row = 2 * total
-    inside = jnp.where(lax.axis_index("slab") > 0, 1.0, 0.0)
+    inside = jnp.where(sum(lax.axis_index(name) for name in SLAB) > 0, 1.0, 0.0)
     cols_refs = ((from_below_ref, 18), (columns_ref, 0), (from_above_ref, 45))
     high_ref[0:18] = top_ref[...]
     high_ref[18:27] = from_above_ref[36:45]
@@ -242,7 +251,8 @@
 
 
 def second_operator_kernel(
-    image_ref, from_left_ref, from_right_ref, low_ref, high_ref, diag_ref, out_ref, gram_ref
+    image_ref, from_left_ref, from_right_ref, low_ref, high_ref, diag_ref, moment_ref, outer_ref,
+    out_ref, packed_ref,
 ):
     total = out_ref.shape[0] // 2
     comps = diag_ref.shape[0]
@@ -262,7 +272,68 @@
     blocks = [
         ((image_ref, (1 + floor) * total), (out_ref, floor * total)) for floor in range(2)
     ]
-    gram_ref[...] = local_gram(blocks, comps, vecs, vecs)
+    inner = local_gram(blocks, comps, vecs, vecs)
+    outer = outer_ref[...]
+    pack_moments(
+        packed_ref, moment_ref[...], outer[:vecs], outer[vecs:], inner[:vecs], inner[vecs:]
+    )
+
+
+def square_ids(size):
+    return (
+        lax.broadcasted_iota(jnp.int32, (size, size), 0),
+        lax.broadcasted_iota(jnp.int32, (size, size), 1),
+    )
+
+
+def pack_moments(packed_ref, *moments):
+    size = moments[0].shape[0]
+    half = size // 2
+    row, column = square_ids(size)
+    squares = [
+        jnp.where(row <= column, moments[0], moments[1]),
+        jnp.where(row <= column, moments[2], moments[3]),
+    ]
+    extra = jnp.zeros((size, size), jnp.float32)
+    for k in range(2):
+        line = jnp.sum(jnp.where(row == column, moments[2 * k + 1], 0.0), axis=0, keepdims=True)
+        turned = jnp.concatenate([line[:, half:], line[:, :half]], axis=1)
+        extra = jnp.where(row == half + 2 * k, line, extra)
+        extra = jnp.where(row == half + 2 * k + 1, turned, extra)
+    squares.append(jnp.where(row <= column, moments[4], extra))
+    for k, square in enumerate(squares):
+        packed_ref[SUB * k : SUB * (k + 1)] = jnp.concatenate(
+            [square[SUB * part : SUB * (part + 1)] for part in range(size // SUB)], axis=1
+        )
+
+
+def unpack_moments(packed, size):
+    half = size // 2
+    row, column = square_ids(size)
+    squares = [
+        jnp.concatenate(
+            [
+                packed[SUB * k : SUB * (k + 1), size * part : size * (part + 1)]
+                for part in range(size // SUB)
+            ],
+            axis=0,
+        )
+        for k in range(3)
+    ]
+    flipped = dot_both((row == column).astype(jnp.float32), jnp.concatenate(squares, axis=0))
+    moments = []
+    for k, square in enumerate(squares):
+        mirror = flipped[:, size * k : size * (k + 1)]
+        moments.append(jnp.where(row <= column, square, mirror))
+        if k < 2:
+            spot = half + 2 * k
+            line = jnp.concatenate(
+                [squares[2][spot : spot + 1, :half], squares[2][spot + 1 : spot + 2, :half]],
+                axis=1,
+            )
+            lower = jnp.where(row > column, square, mirror)
+            moments.append(jnp.where(row == column, line, lower))
+    return moments
 
 
 def paired_rows(parts, start, vecs, across):
@@ -284,13 +355,20 @@
     return gram
 
 
+def start_gram_kernel(own_ref, gram_ref):
+    vecs = gram_ref.shape[0]
+    total = own_ref.shape[0] * vecs // (2 * vecs + 2)
+    blocks = [((own_ref, floor * total),) for floor in range(2)]
+    gram_ref[...] = local_gram(blocks, total // vecs, vecs, 0)
+
+
 def first_gram_kernel(own_ref, image_ref, gram_ref):
-    vecs = gram_ref.shape[0] // 2
+    vecs = gram_ref.shape[1]
     total = image_ref.shape[0] // 4
     blocks = [
         ((own_ref, floor * total), (image_ref, (1 + floor) * total)) for floor in range(2)
     ]
-    gram_ref[...] = local_gram(blocks, total // vecs, vecs, 0)
+    gram_ref[...] = local_gram(blocks, total // vecs, vecs, vecs)
 
 
 def call_whole(kernel, out_shape, *operands, scratch_shapes=()):
@@ -316,21 +394,25 @@
     )
 
 
-def apply_second(image, from_left, from_right, low, high, diagonal):
+def apply_second(image, from_left, from_right, low, high, diagonal, moment, outer):
     total = image.shape[0] // 4
     vecs = total // diagonal.shape[0]
     return call_whole(
         second_operator_kernel,
         [
             jax.ShapeDtypeStruct((2 * total, SUB, LANE), jnp.float32),
-            jax.ShapeDtypeStruct((2 * vecs, vecs), jnp.float32),
+            jax.ShapeDtypeStruct((3 * SUB, SUB * vecs // 2), jnp.float32),
         ],
-        image, from_left, from_right, low, high, diagonal,
-    )
+        image, from_left, from_right, low, high, diagonal, moment, outer,
+    )
+
+
+def start_gram(own, vecs):
+    return call_whole(start_gram_kernel, [jax.ShapeDtypeStruct((vecs, vecs), jnp.float32)], own)[0]
 
 
 def first_gram(own, image, vecs):
-    shape = jax.ShapeDtypeStruct((2 * vecs, 2 * vecs), jnp.float32)
+    shape = jax.ShapeDtypeStruct((2 * vecs, vecs), jnp.float32)
     return call_whole(first_gram_kernel, [shape], own, image)[0]
 
 
@@ -352,7 +434,7 @@
     lane_id = lax.broadcasted_iota(jnp.int32, (size, 2 * size), 1)
     identity = (row_id[:, :size] == lane_id[:, :size]).astype(jnp.float32)
     work = jnp.concatenate([gram, identity], axis=1)
-    panel = 8
+    panel = 16
     for first in range(0, size, panel):
         spots = range(first, first + panel)
         columns = [jnp.broadcast_to(work[:, k : k + 1], (size, 2 * size)) for k in spots]
@@ -393,11 +475,7 @@
     def block(matrix, row, column):
         return matrix[row * vecs : (row + 1) * vecs, column * vecs : (column + 1) * vecs]
 
-    packed = gram_ref[...]
-    moments = [packed[:vecs, k * vecs : (k + 1) * vecs] for k in range(4)]
-    moments.append(
-        jnp.concatenate([packed[vecs:, k * vecs : (k + 1) * vecs] for k in range(4)], axis=0)
-    )
+    moments = unpack_moments(gram_ref[...], vecs)
     gram = grid([moments[k : k + 3] for k in range(3)])
     upper_0, inverse_0 = eliminate(block(gram, 0, 0))
     spread = grid([[inverse_0, zero, zero], [zero, inverse_0, zero], [zero, zero, inverse_0]])
@@ -442,47 +520,15 @@
     )
 
 
-def exchange(value, axis, route):
-    size = lax.axis_size(axis)
-    return lax.ppermute(value, axis, [(i, route(i)) for i in range(size)])
-
-
-def ring_pairs(stride, size, odd_first):
-    def route(i):
-        digit = i // stride % size
-        if odd_first:
-            partner = (digit + 1) % size if digit % 2 == 0 else (digit - 1) % size
-        else:
-            partner = (digit + 1) % size if digit % 2 == 1 else (digit - 1) % size
-        return i + (partner - digit) * stride
-
-    return route
-
-
-def far_pairs(stride):
-    partners = (3, 6, 5, 0, 7, 2, 1, 4)
-
-    def route(i):
-        digit = i // stride % 8
-        return i + (partners[digit] - digit) * stride
-
-    return route
+def spread_sum(value, axes):
+    copies = jnp.broadcast_to(value, (lax.axis_size(axes),) + value.shape)
+    return jnp.sum(lax.all_to_all(copies, axes, 0, 0), axis=0)
 
 
 def mesh_sum(value):
-    steps = [
-        ("slab", ring_pairs(1, 2, True)),
-        ("dom", ring_pairs(1, 4, True)),
-        ("dom", ring_pairs(1, 4, False)),
-        ("slab", ring_pairs(2, 4, True)),
-        ("slab", ring_pairs(2, 4, False)),
-        ("slab", ring_pairs(8, 8, True)),
-        ("slab", ring_pairs(8, 8, False)),
-        ("slab", far_pairs(8)),
-    ]
-    for axis, route in steps:
-        value = value + exchange(value, axis, route)
-    return value
+    value = value + lax.ppermute(value, "core", [(0, 1), (1, 0)])
+    value = spread_sum(value, ("x", "dom"))
+    return spread_sum(value, ("z",))
 
 
 def shifted(value, axis, steps, wrap):
@@ -524,46 +570,42 @@
     from_left = shifted(edges[2:], "dom", 1, True)
     from_right = shifted(edges[:2], "dom", -1, True)
     columns = jnp.concatenate([from_left, from_right], axis=0)
-    under = shifted(own, "slab", 1, False)
-    over = shifted(own, "slab", -1, False)
-    sources, under, over = lax.optimization_barrier((sources, under, over))
+    under = shifted(own, SLAB, 1, False)
+    over = shifted(own, SLAB, -1, False)
+    moment = start_gram(own, vecs)
+    sources, under, over, moment = lax.optimization_barrier((sources, under, over, moment))
     low, top, below = local_stencils(part_counts, grade_scale, node_lists, sources)
-    from_above = shifted(jnp.concatenate([low, below, columns], axis=0), "slab", -1, False)
-    from_below = shifted(jnp.concatenate([top, columns], axis=0), "slab", 1, False)
+    from_above = shifted(jnp.concatenate([low, below, columns], axis=0), SLAB, -1, False)
+    from_below = shifted(jnp.concatenate([top, columns], axis=0), SLAB, 1, False)
     image, left, right, high = apply_first(
         under, own, over, low, top, below, from_above, from_below, columns, total
     )
     from_left = shifted(right, "dom", 1, True)
     from_right = shifted(left, "dom", -1, True)
     outer = first_gram(own, image, vecs)
-    second, inner = apply_second(image, from_left, from_right, low, high, stiff_diag)
-    last = inner[vecs:]
-    packed = jnp.concatenate(
-        [
-            jnp.concatenate([outer[:vecs], outer[vecs:, vecs:], inner[:vecs]], axis=1),
-            jnp.concatenate([last[k * 8 : k * 8 + 8] for k in range(vecs // 8)], axis=1),
-        ],
-        axis=0,
+    second, packed = apply_second(
+        image, from_left, from_right, low, high, stiff_diag, moment, outer
     )
     dof_count = (
-        start_block.size // vecs * lax.axis_size("slab") * lax.axis_size("dom")
+        start_block.size // vecs * lax.axis_size(SLAB + ("dom",))
     )
     packed = mesh_sum(packed) / dof_count
     return finish(packed, (own, image, second), start_block.shape, vecs)
 
 
 def solution(mesh):
+    torus = Mesh(mesh.devices.reshape(8, 4, 2, 4), SLAB + ("dom",))
     in_specs = (
-        P(None, None, ("slab", "dom")),
-        P(None, ("slab", "dom")),
-        P(("slab", "dom")),
+        P(None, None, SLAB + ("dom",)),
+        P(None, SLAB + ("dom",)),
+        P(SLAB + ("dom",)),
         P(),
-        P("slab", None),
-        P(None, "slab", None, "dom"),
-        P(None, "slab", None, "dom"),
-        P(None, None, "slab", None, "dom"),
-    )
-    out_specs = (P(None, None, "slab", None, "dom"), P(), P())
+        P(SLAB, None),
+        P(None, SLAB, None, "dom"),
+        P(None, SLAB, None, "dom"),
+        P(None, None, SLAB, None, "dom"),
+    )
+    out_specs = (P(None, None, SLAB, None, "dom"), P(), P())
     return jax.shard_map(
-        per_device, mesh=mesh, in_specs=in_specs, out_specs=out_specs, check_vma=False
-    )
+        per_device, mesh=torus, in_specs=in_specs, out_specs=out_specs, check_vma=False
+    )

time: 109 us -> 103 us (0.945); the launches traced: 107 us -> 103 us
  blocking collectives: 0 us -> 34.9 us
  starting transfers between devices: 42.3 us -> 17.9 us
  waiting for transfers between devices: 33 us -> 18.4 us
    all_to_all x0 -> x2, blocking collectives: none -> 34.9 us  [spread_sum(): return jnp.sum(lax.all_to_all(copies, axes, 0, 0), axis=0)]
    ppermute x8 -> x1, starting transfers between devices: 25.8 us -> 1.38 us  [mesh_sum(): value = value + lax.ppermute(value, 'core', [(0, 1), (1, 0)])]
    ppermute x8 -> x1, waiting for transfers between devices: 15 us -> 0.83 us  [mesh_sum(): value = value + lax.ppermute(value, 'core', [(0, 1), (1, 0)])]
    pallas_call x5 -> x6, Pallas kernels: 20.5 us -> 21.2 us  [call_whole(): pl.pallas_call(kernel, out_shape=out_shape, in_specs=[vmem] * len(operand...]
  transfers between devices with their start and end apart: 20 -> 13, of which waited for: 13 -> 7; matrix products, arithmetic and copies ran while one was open for 0% -> 0% of each run, Pallas kernels for 9% -> 9%
where the time goes in v3:
time: 103 us
  blocking collectives  34.9 us (34%)
  Pallas kernels  27.5 us (27%)
  waiting for transfers between devices  18.4 us (18%)
  starting transfers between devices  17.9 us (17%)
  other arithmetic  2.16 us (2%)
    all_to_all x2, blocking collectives, spread_sum(): return jnp.sum(lax.all_to_all(copies, axes, 0, 0), axis=0)  34.9 us
    pallas_call x6, Pallas kernels, call_whole(): pl.pallas_call(kernel, out_shape=out_shape, in_specs=[vmem] * len(operand...  21.2 us
    ppermute x12, waiting for transfers between devices, shifted(): return lax.ppermute(value, axis, route)  17.6 us
    ppermute x12, starting transfers between devices, shifted(): return lax.ppermute(value, axis, route)  16.5 us
    pallas_call x1, Pallas kernels, local_stencils(): pl.pallas_call(stencil_kernel, out_shape=[jax.ShapeDtypeStruct((27, SUB,...  6.35 us
  transfers between devices with their start and end apart: 13, of which 7 were waited for; matrix products, arithmetic and copies ran while one was open for 0% of the time, Pallas kernels for 9%

profile of v3, /device:TPU:8, one launch (start us, length us, event | category | flops | bytes accessed | tf_op | source)
XLA Modules:
  0.0 102.6 jit_solution(9020111762297967693)
XLA Ops:
  0.6 0.0 copy-start
  0.6 0.8 convert_element_type.3
  1.5 0.1 pad.12.clone
  1.6 0.0 copy-start.2
  1.6 0.0 copy-start.3
  1.6 0.0 copy-start.4
  1.6 1.3 %maximum_maximum_fusion.refs_0_ = f32[32,5376]{1,0:T(8,128)S(1)} fusion(f32[1,5376]{1,0:T(1,128)S(1)} %broadcast_in_dim.12, f32[6,5376]{1,0:T(8,128)} %param.9, f32[24,5376]{1,0:T(8,128)} %bitcast.2, f32[32]{0:T(128)S(1)} %pad.12.clone), kind=kLoop, calls=%fused_computation | loop fusion | flops 516096 | bytes 1354880 | tf_op jit(solution)/shard_map/concatenate | solution.py:542
  2.8 1.7 %collective-permute-start = (f32[32,5376]{1,0:T(8,128)S(1)}, f32[32,5376]{1,0:T(8,128)S(1)}, u32[]{:S(2)}, u32[]{:S(2)}) collective-permute-start(f32[32,5376]{1,0:T(8,128)S(1)} %maximum_maximum_fusion.refs_0_), channel_id=1, source_target_pairs={{0,1},{1,2},{2,3},{3,0},{4,5},{5,6},{6,7},{7,4},{8,9},{9,10},{10,1... | collective-permute-start | bytes 2064392 | tf_op jit(solution)/shard_map/ppermute | solution.py:537
  4.5 0.7 collective-permute-start.2
  5.2 0.0 copy-done
  5.2 0.0 copy-start.1
  5.2 0.7 copy-done.1
  5.9 0.8 shard_map.103
  6.8 1.3 %collective-permute-start.4 = (f32[198,8,128]{2,1,0:T(8,128)S(1)}, f32[198,8,128]{2,1,0:T(8,128)S(1)}, u32[]{:S(2)}, u32[]{:S(2)}) collective-permute-start(f32[198,8,128]{2,1,0:T(8,128)S(1)} %get-tuple-element.22.own_ref), channel_id=1, source_target_pairs={{0,4},{4,8},{8,12},{12,16},{16,20},{20,24},{24,28},{28,32},{32,36}... | collective-permute-start | bytes 2433032 | tf_op jit(solution)/shard_map/ppermute | solution.py:537
  8.1 1.3 %collective-permute-start.5 = (f32[198,8,128]{2,1,0:T(8,128)S(1)}, f32[198,8,128]{2,1,0:T(8,128)S(1)}, u32[]{:S(2)}, u32[]{:S(2)}) collective-permute-start(f32[198,8,128]{2,1,0:T(8,128)S(1)} %get-tuple-element.22.own_ref), channel_id=1, source_target_pairs={{4,0},{8,4},{12,8},{16,12},{20,16},{24,20},{28,24},{32,28},{36,32}... | collective-permute-start | bytes 2433032 | tf_op jit(solution)/shard_map/ppermute | solution.py:537
  9.4 10.7 %collective-permute-done.refs_1_ = f32[32,5376]{1,0:T(8,128)S(1)} collective-permute-done((f32[32,5376]{1,0:T(8,128)S(1)}, f32[32,5376]{1,0:T(8,128)S(1)}, u32[]{:S(2)}, u32[]{:S(2)}) %collective-permute-start) | collective-permute-done | bytes 688160 | tf_op jit(solution)/shard_map/ppermute | solution.py:537
  20.1 1.7 %collective-permute-start.1 = (f32[16,5376]{1,0:T(8,128)S(1)}, f32[16,5376]{1,0:T(8,128)S(1)}, u32[]{:S(2)}, u32[]{:S(2)}) collective-permute-start(f32[16,5376]{1,0:T(8,128)S(1)} %slice.16), channel_id=1, source_target_pairs={{0,1},{1,2},{2,3},{3,0},{4,5},{5,6},{6,7},{7,4},{8,9},{9,10},{10,1... | collective-permute-start | bytes 1032200 | tf_op jit(solution)/shard_map/ppermute | solution.py:537
  21.8 0.0 collective-permute-done.2.refs_4_
  21.8 0.5 collective-permute-start.3
  22.3 2.9 %collective-permute-start.7 = (f32[2,8,128]{2,1,0:T(8,128)S(1)}, f32[2,8,128]{2,1,0:T(8,128)S(1)}, u32[]{:S(2)}, u32[]{:S(2)}) collective-permute-start(f32[2,8,128]{2,1,0:T(8,128)S(1)} %get-tuple-element.42), channel_id=1, source_target_pairs={{0,3},{1,0},{2,1},{3,2},{4,7},{5,4},{6,5},{7,6},{8,11},{9,8},{10,9... | collective-permute-start | bytes 24584 | tf_op jit(solution)/shard_map/ppermute | solution.py:537
  25.3 0.0 collective-permute-done.4.under_ref
  25.3 0.0 collective-permute-start.6
  25.3 0.8 shard_map.104.moment_ref
  26.1 0.0 collective-permute-done.5.over_ref
  26.1 2.9 %collective-permute-done.1.refs_2_ = f32[16,5376]{1,0:T(8,128)S(1)} collective-permute-done((f32[16,5376]{1,0:T(8,128)S(1)}, f32[16,5376]{1,0:T(8,128)S(1)}, u32[]{:S(2)}, u32[]{:S(2)}) %collective-permute-start.1) | collective-permute-done | bytes 344096 | tf_op jit(solution)/shard_map/ppermute | solution.py:537
  29.0 1.6 %collective-permute-done.3.refs_3_ = f32[16,5376]{1,0:T(8,128)S(1)} collective-permute-done((f32[16,5376]{1,0:T(8,128)S(1)}, f32[16,5376]{1,0:T(8,128)S(1)}, u32[]{:S(2)}, u32[]{:S(2)}) %collective-permute-start.3) | collective-permute-done | bytes 344096 | tf_op jit(solution)/shard_map/ppermute | solution.py:537
  30.6 0.0 copy-done.2
  30.6 0.0 copy-done.3
  30.6 0.0 copy-done.4
  30.6 6.4 %shard_map.105 = (f32[27,8,128]{2,1,0:T(8,128)S(1)}, f32[18,8,128]{2,1,0:T(8,128)S(1)}, f32[18,8,128]{2,1,0:T(8,128)S(1)}) custom-call(s32[1,4]{1,0:T(1,128)S(1)} %copy-done.3, f32[16]{0:T(128)S(1)} %copy-done.4, s32[4,2,8,128]{3,2,1,0:T(8,128)S(1)} %copy-done.2, f32[32,5376]{1,0:T(8,128)S(1)} %maximum_maximum_fusion.refs_0_, ...), custom_call_target="tpu_custom_call" | custom-call | tf_op jit(solution)/shard_map/pallas_call | solution.py:120
  37.0 0.0 collective-permute-done.7
  37.0 0.0 collective-permute-done.6
  37.0 1.3 %collective-permute-start.8 = (f32[49,8,128]{2,1,0:T(8,128)S(1)}, f32[49,8,128]{2,1,0:T(8,128)S(1)}, u32[]{:S(2)}, u32[]{:S(2)}) collective-permute-start(f32[49,8,128]{2,1,0:T(8,128)S(1)} %pad_maximum_fusion), channel_id=1, source_target_pairs={{4,0},{8,4},{12,8},{16,12},{20,16},{24,20},{28,24},{32,28},{36,32}... | collective-permute-start | bytes 602120 | tf_op jit(solution)/shard_map/ppermute | solution.py:537
  38.3 3.0 %collective-permute-start.9 = (f32[22,8,128]{2,1,0:T(8,128)S(1)}, f32[22,8,128]{2,1,0:T(8,128)S(1)}, u32[]{:S(2)}, u32[]{:S(2)}) collective-permute-start(f32[22,8,128]{2,1,0:T(8,128)S(1)} %pad_maximum_fusion.1), channel_id=1, source_target_pairs={{0,4},{4,8},{8,12},{12,16},{16,20},{20,24},{24,28},{28,32},{32,36}... | collective-permute-start | bytes 270344 | tf_op jit(solution)/shard_map/ppermute | solution.py:537
  41.4 0.9 collective-permute-done.9.from_below_ref
  42.3 0.0 collective-permute-done.8.from_above_ref
  42.3 5.6 %shard_map.106 = (f32[384,8,128]{2,1,0:T(8,128)S(1)}, f32[4,8,128]{2,1,0:T(8,128)S(1)}, f32[4,8,128]{2,1,0:T(8,128)S(1)}, f32[27,8,128]{2,1,0:T(8,128)S(1)}) custom-call(f32[198,8,128]{2,1,0:T(8,128)S(1)} %collective-permute-done.4.under_ref, f32[198,8,128]{2,1,0:T(8,128)S(1)} %get-tuple-element.22.own_ref, ...), custom_call_target="tpu_custom_call" | custom-call | tf_op jit(solution)/shard_map/pallas_call | solution.py:376
  47.9 1.4 %collective-permute-start.10 = (f32[4,8,128]{2,1,0:T(8,128)S(1)}, f32[4,8,128]{2,1,0:T(8,128)S(1)}, u32[]{:S(2)}, u32[]{:S(2)}) collective-permute-start(f32[4,8,128]{2,1,0:T(8,128)S(1)} %get-tuple-element.35), channel_id=1, source_target_pairs={{0,1},{1,2},{2,3},{3,0},{4,5},{5,6},{6,7},{7,4},{8,9},{9,10},{10,1... | collective-permute-start | bytes 49160 | tf_op jit(solution)/shard_map/ppermute | solution.py:537
  49.3 0.7 collective-permute-start.11
  50.1 1.5 %shard_map.107.outer_ref = f32[64,32]{1,0:T(8,128)S(1)} custom-call(f32[198,8,128]{2,1,0:T(8,128)S(1)} %get-tuple-element.22.own_ref, f32[384,8,128]{2,1,0:T(8,128)S(1)} %get-tuple-element.34.image_ref), custom_call_target="tpu_custom_call" | custom-call | tf_op jit(solution)/shard_map/pallas_call | solution.py:376
  51.6 0.2 collective-permute-done.10.from_left_ref
  51.8 1.3 %collective-permute-done.11.from_right_ref = f32[4,8,128]{2,1,0:T(8,128)S(1)} collective-permute-done((f32[4,8,128]{2,1,0:T(8,128)S(1)}, f32[4,8,128]{2,1,0:T(8,128)S(1)}, u32[]{:S(2)}, u32[]{:S(2)}) %collective-permute-start.11) | collective-permute-done | bytes 16416 | tf_op jit(solution)/shard_map/ppermute | solution.py:537
  53.0 3.9 %shard_map.108 = (f32[192,8,128]{2,1,0:T(8,128)S(1)}, f32[24,128]{1,0:T(8,128)S(1)}) custom-call(f32[384,8,128]{2,1,0:T(8,128)S(1)} %get-tuple-element.34.image_ref, f32[4,8,128]{2,1,0:T(8,128)S(1)} %collective-permute-done.10.from_left_ref, f32[4,8,128]{2,1,0:T(8,128)S(1)} %collective-permute-done.11.from_right_ref, ...), custom_call_target="tpu_custom_call" | custom-call | tf_op jit(solution)/shard_map/pallas_call | solution.py:376
  57.0 1.4 %collective-permute-start.12 = (f32[24,128]{1,0:T(8,128)S(1)}, f32[24,128]{1,0:T(8,128)S(1)}, u32[]{:S(2)}, u32[]{:S(2)}) collective-permute-start(f32[24,128]{1,0:T(8,128)S(1)} %get-tuple-element.39), channel_id=1, source_target_pairs={{0,4},{4,0},{1,5},{5,1},{2,6},{6,2},{3,7},{7,3},{8,12},{12,8},{9,1... | collective-permute-start | bytes 36872 | tf_op jit(solution)/shard_map/ppermute | solution.py:529
  58.3 0.8 collective-permute-done.12
  59.2 16.8 %all_to_all.10 = f32[16,24,128]{2,1,0:T(8,128)S(1)} all-to-all(f32[16,24,128]{2,1,0:T(8,128)S(1)} %broadcast_in_dim.14), channel_id=1, replica_groups=mesh['z'=8,'x'=4,'core'=2,'dom'=4] {'x','dom'}, dimensions={0} | all-to-all | bytes 393216 | tf_op jit(solution)/shard_map/all_to_all | solution.py:525
  76.0 18.1 %all_to_all.11 = f32[8,24,128]{2,1,0:T(8,128)S(1)} all-to-all(f32[8,24,128]{2,1,0:T(8,128)S(1)} %broadcast_in_dim.15), channel_id=1, replica_groups=mesh['z'=8,'x'=4,'core'=2,'dom'=4] {'z'}, dimensions={0} | all-to-all | bytes 196608 | tf_op jit(solution)/shard_map/all_to_all | solution.py:525
  94.2 8.5 %shard_map.109 = (f32[3,32,2,8,128]{4,3,2,1,0:T(8,128)}, f32[2,32,32]{2,1,0:T(8,128)}, f32[3,32,32]{2,1,0:T(8,128)}) custom-call(f32[24,128]{1,0:T(8,128)S(1)} %broadcast_multiply_fusion.gram_ref, f32[198,8,128]{2,1,0:T(8,128)S(1)} %get-tuple-element.22.own_ref, f32[384,8,128]{2,1,0:T(8,128)S(1)} %get-tuple-element.34.image_ref, ...), custom_call_target="tpu_custom_call" | custom-call | tf_op jit(solution)/shard_map/pallas_call | solution.py:376
  (13 shorter events, 0.2 us)
Async XLA Ops:
  0.6 4.6 %copy-start = (f32[3,32,2,8,128]{4,3,2,1,0:T(8,128)S(1)}, f32[3,32,2,8,128]{4,3,2,1,0:T(8,128)}, u32[]{:S(2)}) copy-start(f32[3,32,2,8,128]{4,3,2,1,0:T(8,128)} %start_ref.1) | copy-start | bytes 2359300
  1.6 29.1 %copy-start.2 = (s32[4,2,8,128]{3,2,1,0:T(8,128)S(1)}, s32[4,2,8,128]{3,2,1,0:T(8,128)}, u32[]{:S(2)}) copy-start(s32[4,2,8,128]{3,2,1,0:T(8,128)} %lists_ref.1) | copy-start | bytes 98308
  1.6 29.1 %copy-start.3 = (s32[1,4]{1,0:T(1,128)S(1)}, s32[1,4]{1,0:T(1,128)}, u32[]{:S(2)}) copy-start(s32[1,4]{1,0:T(1,128)} %counts_ref.1) | copy-start | bytes 52
  1.6 29.1 %copy-start.4 = (f32[16]{0:T(128)S(1)}, f32[16]{0:T(128)}, u32[]{:S(2)}) copy-start(f32[16]{0:T(128)} %table_ref.1) | copy-start | bytes 196
  2.8 17.3 %collective-permute-start = (f32[32,5376]{1,0:T(8,128)S(1)}, f32[32,5376]{1,0:T(8,128)S(1)}, u32[]{:S(2)}, u32[]{:S(2)}) collective-permute-start(f32[32,5376]{1,0:T(8,128)S(1)} %maximum_maximum_fusion.refs_0_), channel_id=1, source_target_pairs={{0,1},{1,2},{2,3},{3,0},{4,5},{5,6},{6,7},{7,4},{8,9},{9,10},{10,1... | collective-permute-start | bytes 2064392 | tf_op jit(solution)/shard_map/ppermute | solution.py:537
  4.5 17.3 %collective-permute-start.2 = (f32[32,5376]{1,0:T(8,128)S(1)}, f32[32,5376]{1,0:T(8,128)S(1)}, u32[]{:S(2)}, u32[]{:S(2)}) collective-permute-start(f32[32,5376]{1,0:T(8,128)S(1)} %maximum_maximum_fusion.refs_0_), channel_id=1, source_target_pairs={{0,3},{1,0},{2,1},{3,2},{4,7},{5,4},{6,5},{7,6},{8,11},{9,8},{10,9... | collective-permute-start | bytes 2064392 | tf_op jit(solution)/shard_map/ppermute | solution.py:537
  5.2 0.7 copy-start.1
  6.8 18.5 %collective-permute-start.4 = (f32[198,8,128]{2,1,0:T(8,128)S(1)}, f32[198,8,128]{2,1,0:T(8,128)S(1)}, u32[]{:S(2)}, u32[]{:S(2)}) collective-permute-start(f32[198,8,128]{2,1,0:T(8,128)S(1)} %get-tuple-element.22.own_ref), channel_id=1, source_target_pairs={{0,4},{4,8},{8,12},{12,16},{16,20},{20,24},{24,28},{28,32},{32,36}... | collective-permute-start | bytes 2433032 | tf_op jit(solution)/shard_map/ppermute | solution.py:537
  8.1 18.0 %collective-permute-start.5 = (f32[198,8,128]{2,1,0:T(8,128)S(1)}, f32[198,8,128]{2,1,0:T(8,128)S(1)}, u32[]{:S(2)}, u32[]{:S(2)}) collective-permute-start(f32[198,8,128]{2,1,0:T(8,128)S(1)} %get-tuple-element.22.own_ref), channel_id=1, source_target_pairs={{4,0},{8,4},{12,8},{16,12},{20,16},{24,20},{28,24},{32,28},{36,32}... | collective-permute-start | bytes 2433032 | tf_op jit(solution)/shard_map/ppermute | solution.py:537
  20.1 8.9 %collective-permute-start.1 = (f32[16,5376]{1,0:T(8,128)S(1)}, f32[16,5376]{1,0:T(8,128)S(1)}, u32[]{:S(2)}, u32[]{:S(2)}) collective-permute-start(f32[16,5376]{1,0:T(8,128)S(1)} %slice.16), channel_id=1, source_target_pairs={{0,1},{1,2},{2,3},{3,0},{4,5},{5,6},{6,7},{7,4},{8,9},{9,10},{10,1... | collective-permute-start | bytes 1032200 | tf_op jit(solution)/shard_map/ppermute | solution.py:537
  21.8 8.8 %collective-permute-start.3 = (f32[16,5376]{1,0:T(8,128)S(1)}, f32[16,5376]{1,0:T(8,128)S(1)}, u32[]{:S(2)}, u32[]{:S(2)}) collective-permute-start(f32[16,5376]{1,0:T(8,128)S(1)} %slice.17), channel_id=1, source_target_pairs={{0,3},{1,0},{2,1},{3,2},{4,7},{5,4},{6,5},{7,6},{8,11},{9,8},{10,9... | collective-permute-start | bytes 1032200 | tf_op jit(solution)/shard_map/ppermute | solution.py:537
  22.3 14.7 %collective-permute-start.7 = (f32[2,8,128]{2,1,0:T(8,128)S(1)}, f32[2,8,128]{2,1,0:T(8,128)S(1)}, u32[]{:S(2)}, u32[]{:S(2)}) collective-permute-start(f32[2,8,128]{2,1,0:T(8,128)S(1)} %get-tuple-element.42), channel_id=1, source_target_pairs={{0,3},{1,0},{2,1},{3,2},{4,7},{5,4},{6,5},{7,6},{8,11},{9,8},{10,9... | collective-permute-start | bytes 24584 | tf_op jit(solution)/shard_map/ppermute | solution.py:537
  25.3 11.7 %collective-permute-start.6 = (f32[2,8,128]{2,1,0:T(8,128)S(1)}, f32[2,8,128]{2,1,0:T(8,128)S(1)}, u32[]{:S(2)}, u32[]{:S(2)}) collective-permute-start(f32[2,8,128]{2,1,0:T(8,128)S(1)} %get-tuple-element.41), channel_id=1, source_target_pairs={{0,1},{1,2},{2,3},{3,0},{4,5},{5,6},{6,7},{7,4},{8,9},{9,10},{10,1... | collective-permute-start | bytes 24584 | tf_op jit(solution)/shard_map/ppermute | solution.py:537
  37.0 5.3 %collective-permute-start.8 = (f32[49,8,128]{2,1,0:T(8,128)S(1)}, f32[49,8,128]{2,1,0:T(8,128)S(1)}, u32[]{:S(2)}, u32[]{:S(2)}) collective-permute-start(f32[49,8,128]{2,1,0:T(8,128)S(1)} %pad_maximum_fusion), channel_id=1, source_target_pairs={{4,0},{8,4},{12,8},{16,12},{20,16},{24,20},{28,24},{32,28},{36,32}... | collective-permute-start | bytes 602120 | tf_op jit(solution)/shard_map/ppermute | solution.py:537
  38.3 4.0 %collective-permute-start.9 = (f32[22,8,128]{2,1,0:T(8,128)S(1)}, f32[22,8,128]{2,1,0:T(8,128)S(1)}, u32[]{:S(2)}, u32[]{:S(2)}) collective-permute-start(f32[22,8,128]{2,1,0:T(8,128)S(1)} %pad_maximum_fusion.1), channel_id=1, source_target_pairs={{0,4},{4,8},{8,12},{12,16},{16,20},{20,24},{24,28},{28,32},{32,36}... | collective-permute-start | bytes 270344 | tf_op jit(solution)/shard_map/ppermute | solution.py:537
  47.9 3.8 %collective-permute-start.10 = (f32[4,8,128]{2,1,0:T(8,128)S(1)}, f32[4,8,128]{2,1,0:T(8,128)S(1)}, u32[]{:S(2)}, u32[]{:S(2)}) collective-permute-start(f32[4,8,128]{2,1,0:T(8,128)S(1)} %get-tuple-element.35), channel_id=1, source_target_pairs={{0,1},{1,2},{2,3},{3,0},{4,5},{5,6},{6,7},{7,4},{8,9},{9,10},{10,1... | collective-permute-start | bytes 49160 | tf_op jit(solution)/shard_map/ppermute | solution.py:537
  49.3 3.7 %collective-permute-start.11 = (f32[4,8,128]{2,1,0:T(8,128)S(1)}, f32[4,8,128]{2,1,0:T(8,128)S(1)}, u32[]{:S(2)}, u32[]{:S(2)}) collective-permute-start(f32[4,8,128]{2,1,0:T(8,128)S(1)} %get-tuple-element.36), channel_id=1, source_target_pairs={{0,3},{1,0},{2,1},{3,2},{4,7},{5,4},{6,5},{7,6},{8,11},{9,8},{10,9... | collective-permute-start | bytes 49160 | tf_op jit(solution)/shard_map/ppermute | solution.py:537
  57.0 2.2 %collective-permute-start.12 = (f32[24,128]{1,0:T(8,128)S(1)}, f32[24,128]{1,0:T(8,128)S(1)}, u32[]{:S(2)}, u32[]{:S(2)}) collective-permute-start(f32[24,128]{1,0:T(8,128)S(1)} %get-tuple-element.39), channel_id=1, source_target_pairs={{0,4},{4,0},{1,5},{5,1},{2,6},{6,2},{3,7},{7,3},{8,12},{12,8},{9,1... | collective-permute-start | bytes 36872 | tf_op jit(solution)/shard_map/ppermute | solution.py:529

commit v4 on v3

--- a/solution.py
+++ b/solution.py
@@ -489,7 +489,7 @@
     alpha_2, alpha_2_t = block(products, 0, 1), block(products, 1, 0)
     upper_2, inverse_2 = eliminate(block(products, 1, 1) - dot_rows(alpha_2_t, alpha_2))
     residual = jnp.concatenate([-upper_1, -dot_rows(alpha_2_t, inverse_1), inverse_1], axis=1)
-    coefs = dot_rows(dot_rows(dot_rows(inverse_2, residual), change), spread)
+    coefs = dot_rows(inverse_2, dot_rows(residual, dot_rows(change, spread)))
     diag_ref[0] = alpha_1
     diag_ref[1] = alpha_2
     offdiag_ref[0] = upper_0

time: 103 us -> 102 us (level)
  transfers between devices with their start and end apart: 13 -> 13, of which waited for: 7 -> 7; matrix products, arithmetic and copies ran while one was open for 0% -> 0% of each run, Pallas kernels for 9% -> 10%
where the time goes in v4:
time: 102 us
  blocking collectives  34.6 us (34%)
  Pallas kernels  27.4 us (27%)
  waiting for transfers between devices  18.4 us (18%)
  starting transfers between devices  17.6 us (17%)
  other arithmetic  2.16 us (2%)
    all_to_all x2, blocking collectives, spread_sum(): return jnp.sum(lax.all_to_all(copies, axes, 0, 0), axis=0)  34.6 us
    pallas_call x6, Pallas kernels, call_whole(): pl.pallas_call(kernel, out_shape=out_shape, in_specs=[vmem] * len(operand...  20.8 us
    ppermute x12, waiting for transfers between devices, shifted(): return lax.ppermute(value, axis, route)  17.6 us
    ppermute x12, starting transfers between devices, shifted(): return lax.ppermute(value, axis, route)  16.5 us
    pallas_call x1, Pallas kernels, local_stencils(): pl.pallas_call(stencil_kernel, out_shape=[jax.ShapeDtypeStruct((27, SUB,...  6.62 us
  transfers between devices with their start and end apart: 13, of which 7 were waited for; matrix products, arithmetic and copies ran while one was open for 0% of the time, Pallas kernels for 10%

profile of v4, /device:TPU:8, one launch (start us, length us, event | category | flops | bytes accessed | tf_op | source)
XLA Modules:
  0.0 102.0 jit_solution(5394900947813121964)
XLA Ops:
  0.6 0.0 copy-start
  0.6 0.8 convert_element_type.3
  1.5 0.1 pad.12.clone
  1.6 0.0 copy-start.2
  1.6 0.0 copy-start.3
  1.6 0.0 copy-start.4
  1.6 1.3 %maximum_maximum_fusion.refs_0_ = f32[32,5376]{1,0:T(8,128)S(1)} fusion(f32[1,5376]{1,0:T(1,128)S(1)} %broadcast_in_dim.12, f32[6,5376]{1,0:T(8,128)} %param.9, f32[24,5376]{1,0:T(8,128)} %bitcast.2, f32[32]{0:T(128)S(1)} %pad.12.clone), kind=kLoop, calls=%fused_computation | loop fusion | flops 516096 | bytes 1354880 | tf_op jit(solution)/shard_map/concatenate | solution.py:542
  2.8 1.7 %collective-permute-start = (f32[32,5376]{1,0:T(8,128)S(1)}, f32[32,5376]{1,0:T(8,128)S(1)}, u32[]{:S(2)}, u32[]{:S(2)}) collective-permute-start(f32[32,5376]{1,0:T(8,128)S(1)} %maximum_maximum_fusion.refs_0_), channel_id=1, source_target_pairs={{0,1},{1,2},{2,3},{3,0},{4,5},{5,6},{6,7},{7,4},{8,9},{9,10},{10,1... | collective-permute-start | bytes 2064392 | tf_op jit(solution)/shard_map/ppermute | solution.py:537
  4.5 0.7 collective-permute-start.2
  5.2 0.0 copy-done
  5.2 0.0 copy-start.1
  5.2 0.7 copy-done.1
  5.9 0.8 shard_map.103
  6.8 1.3 %collective-permute-start.4 = (f32[198,8,128]{2,1,0:T(8,128)S(1)}, f32[198,8,128]{2,1,0:T(8,128)S(1)}, u32[]{:S(2)}, u32[]{:S(2)}) collective-permute-start(f32[198,8,128]{2,1,0:T(8,128)S(1)} %get-tuple-element.22.own_ref), channel_id=1, source_target_pairs={{0,4},{4,8},{8,12},{12,16},{16,20},{20,24},{24,28},{28,32},{32,36}... | collective-permute-start | bytes 2433032 | tf_op jit(solution)/shard_map/ppermute | solution.py:537
  8.1 1.3 %collective-permute-start.5 = (f32[198,8,128]{2,1,0:T(8,128)S(1)}, f32[198,8,128]{2,1,0:T(8,128)S(1)}, u32[]{:S(2)}, u32[]{:S(2)}) collective-permute-start(f32[198,8,128]{2,1,0:T(8,128)S(1)} %get-tuple-element.22.own_ref), channel_id=1, source_target_pairs={{4,0},{8,4},{12,8},{16,12},{20,16},{24,20},{28,24},{32,28},{36,32}... | collective-permute-start | bytes 2433032 | tf_op jit(solution)/shard_map/ppermute | solution.py:537
  9.4 10.7 %collective-permute-done.refs_1_ = f32[32,5376]{1,0:T(8,128)S(1)} collective-permute-done((f32[32,5376]{1,0:T(8,128)S(1)}, f32[32,5376]{1,0:T(8,128)S(1)}, u32[]{:S(2)}, u32[]{:S(2)}) %collective-permute-start) | collective-permute-done | bytes 688160 | tf_op jit(solution)/shard_map/ppermute | solution.py:537
  20.1 1.7 %collective-permute-start.1 = (f32[16,5376]{1,0:T(8,128)S(1)}, f32[16,5376]{1,0:T(8,128)S(1)}, u32[]{:S(2)}, u32[]{:S(2)}) collective-permute-start(f32[16,5376]{1,0:T(8,128)S(1)} %slice.16), channel_id=1, source_target_pairs={{0,1},{1,2},{2,3},{3,0},{4,5},{5,6},{6,7},{7,4},{8,9},{9,10},{10,1... | collective-permute-start | bytes 1032200 | tf_op jit(solution)/shard_map/ppermute | solution.py:537
  21.8 0.0 collective-permute-done.2.refs_4_
  21.8 0.5 collective-permute-start.3
  22.3 2.9 %collective-permute-start.7 = (f32[2,8,128]{2,1,0:T(8,128)S(1)}, f32[2,8,128]{2,1,0:T(8,128)S(1)}, u32[]{:S(2)}, u32[]{:S(2)}) collective-permute-start(f32[2,8,128]{2,1,0:T(8,128)S(1)} %get-tuple-element.42), channel_id=1, source_target_pairs={{0,3},{1,0},{2,1},{3,2},{4,7},{5,4},{6,5},{7,6},{8,11},{9,8},{10,9... | collective-permute-start | bytes 24584 | tf_op jit(solution)/shard_map/ppermute | solution.py:537
  25.3 0.0 collective-permute-done.4.under_ref
  25.3 0.0 collective-permute-start.6
  25.3 0.8 shard_map.104.moment_ref
  26.1 0.0 collective-permute-done.5.over_ref
  26.1 2.9 %collective-permute-done.1.refs_2_ = f32[16,5376]{1,0:T(8,128)S(1)} collective-permute-done((f32[16,5376]{1,0:T(8,128)S(1)}, f32[16,5376]{1,0:T(8,128)S(1)}, u32[]{:S(2)}, u32[]{:S(2)}) %collective-permute-start.1) | collective-permute-done | bytes 344096 | tf_op jit(solution)/shard_map/ppermute | solution.py:537
  29.0 1.6 %collective-permute-done.3.refs_3_ = f32[16,5376]{1,0:T(8,128)S(1)} collective-permute-done((f32[16,5376]{1,0:T(8,128)S(1)}, f32[16,5376]{1,0:T(8,128)S(1)}, u32[]{:S(2)}, u32[]{:S(2)}) %collective-permute-start.3) | collective-permute-done | bytes 344096 | tf_op jit(solution)/shard_map/ppermute | solution.py:537
  30.6 0.0 copy-done.2
  30.6 0.0 copy-done.3
  30.6 0.0 copy-done.4
  30.6 6.6 %shard_map.105 = (f32[27,8,128]{2,1,0:T(8,128)S(1)}, f32[18,8,128]{2,1,0:T(8,128)S(1)}, f32[18,8,128]{2,1,0:T(8,128)S(1)}) custom-call(s32[1,4]{1,0:T(1,128)S(1)} %copy-done.3, f32[16]{0:T(128)S(1)} %copy-done.4, s32[4,2,8,128]{3,2,1,0:T(8,128)S(1)} %copy-done.2, f32[32,5376]{1,0:T(8,128)S(1)} %maximum_maximum_fusion.refs_0_, ...), custom_call_target="tpu_custom_call" | custom-call | tf_op jit(solution)/shard_map/pallas_call | solution.py:120
  37.3 0.0 collective-permute-done.7
  37.3 0.0 collective-permute-done.6
  37.3 1.3 %collective-permute-start.8 = (f32[49,8,128]{2,1,0:T(8,128)S(1)}, f32[49,8,128]{2,1,0:T(8,128)S(1)}, u32[]{:S(2)}, u32[]{:S(2)}) collective-permute-start(f32[49,8,128]{2,1,0:T(8,128)S(1)} %pad_maximum_fusion), channel_id=1, source_target_pairs={{4,0},{8,4},{12,8},{16,12},{20,16},{24,20},{28,24},{32,28},{36,32}... | collective-permute-start | bytes 602120 | tf_op jit(solution)/shard_map/ppermute | solution.py:537
  38.6 3.0 %collective-permute-start.9 = (f32[22,8,128]{2,1,0:T(8,128)S(1)}, f32[22,8,128]{2,1,0:T(8,128)S(1)}, u32[]{:S(2)}, u32[]{:S(2)}) collective-permute-start(f32[22,8,128]{2,1,0:T(8,128)S(1)} %pad_maximum_fusion.1), channel_id=1, source_target_pairs={{0,4},{4,8},{8,12},{12,16},{16,20},{20,24},{24,28},{28,32},{32,36}... | collective-permute-start | bytes 270344 | tf_op jit(solution)/shard_map/ppermute | solution.py:537
  41.7 0.9 collective-permute-done.9.from_below_ref
  42.6 0.0 collective-permute-done.8.from_above_ref
  42.6 5.6 %shard_map.106 = (f32[384,8,128]{2,1,0:T(8,128)S(1)}, f32[4,8,128]{2,1,0:T(8,128)S(1)}, f32[4,8,128]{2,1,0:T(8,128)S(1)}, f32[27,8,128]{2,1,0:T(8,128)S(1)}) custom-call(f32[198,8,128]{2,1,0:T(8,128)S(1)} %collective-permute-done.4.under_ref, f32[198,8,128]{2,1,0:T(8,128)S(1)} %get-tuple-element.22.own_ref, ...), custom_call_target="tpu_custom_call" | custom-call | tf_op jit(solution)/shard_map/pallas_call | solution.py:376
  48.2 1.4 %collective-permute-start.10 = (f32[4,8,128]{2,1,0:T(8,128)S(1)}, f32[4,8,128]{2,1,0:T(8,128)S(1)}, u32[]{:S(2)}, u32[]{:S(2)}) collective-permute-start(f32[4,8,128]{2,1,0:T(8,128)S(1)} %get-tuple-element.35), channel_id=1, source_target_pairs={{0,1},{1,2},{2,3},{3,0},{4,5},{5,6},{6,7},{7,4},{8,9},{9,10},{10,1... | collective-permute-start | bytes 49160 | tf_op jit(solution)/shard_map/ppermute | solution.py:537
  49.6 0.7 collective-permute-start.11
  50.3 1.5 %shard_map.107.outer_ref = f32[64,32]{1,0:T(8,128)S(1)} custom-call(f32[198,8,128]{2,1,0:T(8,128)S(1)} %get-tuple-element.22.own_ref, f32[384,8,128]{2,1,0:T(8,128)S(1)} %get-tuple-element.34.image_ref), custom_call_target="tpu_custom_call" | custom-call | tf_op jit(solution)/shard_map/pallas_call | solution.py:376
  51.9 0.2 collective-permute-done.10.from_left_ref
  52.0 1.3 %collective-permute-done.11.from_right_ref = f32[4,8,128]{2,1,0:T(8,128)S(1)} collective-permute-done((f32[4,8,128]{2,1,0:T(8,128)S(1)}, f32[4,8,128]{2,1,0:T(8,128)S(1)}, u32[]{:S(2)}, u32[]{:S(2)}) %collective-permute-start.11) | collective-permute-done | bytes 16416 | tf_op jit(solution)/shard_map/ppermute | solution.py:537
  53.3 3.9 %shard_map.108 = (f32[192,8,128]{2,1,0:T(8,128)S(1)}, f32[24,128]{1,0:T(8,128)S(1)}) custom-call(f32[384,8,128]{2,1,0:T(8,128)S(1)} %get-tuple-element.34.image_ref, f32[4,8,128]{2,1,0:T(8,128)S(1)} %collective-permute-done.10.from_left_ref, f32[4,8,128]{2,1,0:T(8,128)S(1)} %collective-permute-done.11.from_right_ref, ...), custom_call_target="tpu_custom_call" | custom-call | tf_op jit(solution)/shard_map/pallas_call | solution.py:376
  57.2 1.1 %collective-permute-start.12 = (f32[24,128]{1,0:T(8,128)S(1)}, f32[24,128]{1,0:T(8,128)S(1)}, u32[]{:S(2)}, u32[]{:S(2)}) collective-permute-start(f32[24,128]{1,0:T(8,128)S(1)} %get-tuple-element.39), channel_id=1, source_target_pairs={{0,4},{4,0},{1,5},{5,1},{2,6},{6,2},{3,7},{7,3},{8,12},{12,8},{9,1... | collective-permute-start | bytes 36872 | tf_op jit(solution)/shard_map/ppermute | solution.py:529
  58.3 0.8 collective-permute-done.12
  59.2 16.8 %all_to_all.10 = f32[16,24,128]{2,1,0:T(8,128)S(1)} all-to-all(f32[16,24,128]{2,1,0:T(8,128)S(1)} %broadcast_in_dim.14), channel_id=1, replica_groups=mesh['z'=8,'x'=4,'core'=2,'dom'=4] {'x','dom'}, dimensions={0} | all-to-all | bytes 393216 | tf_op jit(solution)/shard_map/all_to_all | solution.py:525
  76.0 17.8 %all_to_all.11 = f32[8,24,128]{2,1,0:T(8,128)S(1)} all-to-all(f32[8,24,128]{2,1,0:T(8,128)S(1)} %broadcast_in_dim.15), channel_id=1, replica_groups=mesh['z'=8,'x'=4,'core'=2,'dom'=4] {'z'}, dimensions={0} | all-to-all | bytes 196608 | tf_op jit(solution)/shard_map/all_to_all | solution.py:525
  93.9 8.1 %shard_map.109 = (f32[3,32,2,8,128]{4,3,2,1,0:T(8,128)}, f32[2,32,32]{2,1,0:T(8,128)}, f32[3,32,32]{2,1,0:T(8,128)}) custom-call(f32[24,128]{1,0:T(8,128)S(1)} %broadcast_multiply_fusion.gram_ref, f32[198,8,128]{2,1,0:T(8,128)S(1)} %get-tuple-element.22.own_ref, f32[384,8,128]{2,1,0:T(8,128)S(1)} %get-tuple-element.34.image_ref, ...), custom_call_target="tpu_custom_call" | custom-call | tf_op jit(solution)/shard_map/pallas_call | solution.py:376
  (13 shorter events, 0.2 us)
Async XLA Ops:
  0.6 4.6 %copy-start = (f32[3,32,2,8,128]{4,3,2,1,0:T(8,128)S(1)}, f32[3,32,2,8,128]{4,3,2,1,0:T(8,128)}, u32[]{:S(2)}) copy-start(f32[3,32,2,8,128]{4,3,2,1,0:T(8,128)} %start_ref.1) | copy-start | bytes 2359300
  1.6 29.1 %copy-start.2 = (s32[4,2,8,128]{3,2,1,0:T(8,128)S(1)}, s32[4,2,8,128]{3,2,1,0:T(8,128)}, u32[]{:S(2)}) copy-start(s32[4,2,8,128]{3,2,1,0:T(8,128)} %lists_ref.1) | copy-start | bytes 98308
  1.6 29.1 %copy-start.3 = (s32[1,4]{1,0:T(1,128)S(1)}, s32[1,4]{1,0:T(1,128)}, u32[]{:S(2)}) copy-start(s32[1,4]{1,0:T(1,128)} %counts_ref.1) | copy-start | bytes 52
  1.6 29.1 %copy-start.4 = (f32[16]{0:T(128)S(1)}, f32[16]{0:T(128)}, u32[]{:S(2)}) copy-start(f32[16]{0:T(128)} %table_ref.1) | copy-start | bytes 196
  2.8 17.3 %collective-permute-start = (f32[32,5376]{1,0:T(8,128)S(1)}, f32[32,5376]{1,0:T(8,128)S(1)}, u32[]{:S(2)}, u32[]{:S(2)}) collective-permute-start(f32[32,5376]{1,0:T(8,128)S(1)} %maximum_maximum_fusion.refs_0_), channel_id=1, source_target_pairs={{0,1},{1,2},{2,3},{3,0},{4,5},{5,6},{6,7},{7,4},{8,9},{9,10},{10,1... | collective-permute-start | bytes 2064392 | tf_op jit(solution)/shard_map/ppermute | solution.py:537
  4.5 17.3 %collective-permute-start.2 = (f32[32,5376]{1,0:T(8,128)S(1)}, f32[32,5376]{1,0:T(8,128)S(1)}, u32[]{:S(2)}, u32[]{:S(2)}) collective-permute-start(f32[32,5376]{1,0:T(8,128)S(1)} %maximum_maximum_fusion.refs_0_), channel_id=1, source_target_pairs={{0,3},{1,0},{2,1},{3,2},{4,7},{5,4},{6,5},{7,6},{8,11},{9,8},{10,9... | collective-permute-start | bytes 2064392 | tf_op jit(solution)/shard_map/ppermute | solution.py:537
  5.2 0.7 copy-start.1
  6.8 18.5 %collective-permute-start.4 = (f32[198,8,128]{2,1,0:T(8,128)S(1)}, f32[198,8,128]{2,1,0:T(8,128)S(1)}, u32[]{:S(2)}, u32[]{:S(2)}) collective-permute-start(f32[198,8,128]{2,1,0:T(8,128)S(1)} %get-tuple-element.22.own_ref), channel_id=1, source_target_pairs={{0,4},{4,8},{8,12},{12,16},{16,20},{20,24},{24,28},{28,32},{32,36}... | collective-permute-start | bytes 2433032 | tf_op jit(solution)/shard_map/ppermute | solution.py:537
  8.1 18.0 %collective-permute-start.5 = (f32[198,8,128]{2,1,0:T(8,128)S(1)}, f32[198,8,128]{2,1,0:T(8,128)S(1)}, u32[]{:S(2)}, u32[]{:S(2)}) collective-permute-start(f32[198,8,128]{2,1,0:T(8,128)S(1)} %get-tuple-element.22.own_ref), channel_id=1, source_target_pairs={{4,0},{8,4},{12,8},{16,12},{20,16},{24,20},{28,24},{32,28},{36,32}... | collective-permute-start | bytes 2433032 | tf_op jit(solution)/shard_map/ppermute | solution.py:537
  20.1 8.9 %collective-permute-start.1 = (f32[16,5376]{1,0:T(8,128)S(1)}, f32[16,5376]{1,0:T(8,128)S(1)}, u32[]{:S(2)}, u32[]{:S(2)}) collective-permute-start(f32[16,5376]{1,0:T(8,128)S(1)} %slice.16), channel_id=1, source_target_pairs={{0,1},{1,2},{2,3},{3,0},{4,5},{5,6},{6,7},{7,4},{8,9},{9,10},{10,1... | collective-permute-start | bytes 1032200 | tf_op jit(solution)/shard_map/ppermute | solution.py:537
  21.8 8.8 %collective-permute-start.3 = (f32[16,5376]{1,0:T(8,128)S(1)}, f32[16,5376]{1,0:T(8,128)S(1)}, u32[]{:S(2)}, u32[]{:S(2)}) collective-permute-start(f32[16,5376]{1,0:T(8,128)S(1)} %slice.17), channel_id=1, source_target_pairs={{0,3},{1,0},{2,1},{3,2},{4,7},{5,4},{6,5},{7,6},{8,11},{9,8},{10,9... | collective-permute-start | bytes 1032200 | tf_op jit(solution)/shard_map/ppermute | solution.py:537
  22.3 14.9 %collective-permute-start.7 = (f32[2,8,128]{2,1,0:T(8,128)S(1)}, f32[2,8,128]{2,1,0:T(8,128)S(1)}, u32[]{:S(2)}, u32[]{:S(2)}) collective-permute-start(f32[2,8,128]{2,1,0:T(8,128)S(1)} %get-tuple-element.42), channel_id=1, source_target_pairs={{0,3},{1,0},{2,1},{3,2},{4,7},{5,4},{6,5},{7,6},{8,11},{9,8},{10,9... | collective-permute-start | bytes 24584 | tf_op jit(solution)/shard_map/ppermute | solution.py:537
  25.3 12.0 %collective-permute-start.6 = (f32[2,8,128]{2,1,0:T(8,128)S(1)}, f32[2,8,128]{2,1,0:T(8,128)S(1)}, u32[]{:S(2)}, u32[]{:S(2)}) collective-permute-start(f32[2,8,128]{2,1,0:T(8,128)S(1)} %get-tuple-element.41), channel_id=1, source_target_pairs={{0,1},{1,2},{2,3},{3,0},{4,5},{5,6},{6,7},{7,4},{8,9},{9,10},{10,1... | collective-permute-start | bytes 24584 | tf_op jit(solution)/shard_map/ppermute | solution.py:537
  37.3 5.3 %collective-permute-start.8 = (f32[49,8,128]{2,1,0:T(8,128)S(1)}, f32[49,8,128]{2,1,0:T(8,128)S(1)}, u32[]{:S(2)}, u32[]{:S(2)}) collective-permute-start(f32[49,8,128]{2,1,0:T(8,128)S(1)} %pad_maximum_fusion), channel_id=1, source_target_pairs={{4,0},{8,4},{12,8},{16,12},{20,16},{24,20},{28,24},{32,28},{36,32}... | collective-permute-start | bytes 602120 | tf_op jit(solution)/shard_map/ppermute | solution.py:537
  38.6 4.0 %collective-permute-start.9 = (f32[22,8,128]{2,1,0:T(8,128)S(1)}, f32[22,8,128]{2,1,0:T(8,128)S(1)}, u32[]{:S(2)}, u32[]{:S(2)}) collective-permute-start(f32[22,8,128]{2,1,0:T(8,128)S(1)} %pad_maximum_fusion.1), channel_id=1, source_target_pairs={{0,4},{4,8},{8,12},{12,16},{16,20},{20,24},{24,28},{28,32},{32,36}... | collective-permute-start | bytes 270344 | tf_op jit(solution)/shard_map/ppermute | solution.py:537
  48.2 3.8 %collective-permute-start.10 = (f32[4,8,128]{2,1,0:T(8,128)S(1)}, f32[4,8,128]{2,1,0:T(8,128)S(1)}, u32[]{:S(2)}, u32[]{:S(2)}) collective-permute-start(f32[4,8,128]{2,1,0:T(8,128)S(1)} %get-tuple-element.35), channel_id=1, source_target_pairs={{0,1},{1,2},{2,3},{3,0},{4,5},{5,6},{6,7},{7,4},{8,9},{9,10},{10,1... | collective-permute-start | bytes 49160 | tf_op jit(solution)/shard_map/ppermute | solution.py:537
  49.6 3.7 %collective-permute-start.11 = (f32[4,8,128]{2,1,0:T(8,128)S(1)}, f32[4,8,128]{2,1,0:T(8,128)S(1)}, u32[]{:S(2)}, u32[]{:S(2)}) collective-permute-start(f32[4,8,128]{2,1,0:T(8,128)S(1)} %get-tuple-element.36), channel_id=1, source_target_pairs={{0,3},{1,0},{2,1},{3,2},{4,7},{5,4},{6,5},{7,6},{8,11},{9,8},{10,9... | collective-permute-start | bytes 49160 | tf_op jit(solution)/shard_map/ppermute | solution.py:537
  57.2 1.9 %collective-permute-start.12 = (f32[24,128]{1,0:T(8,128)S(1)}, f32[24,128]{1,0:T(8,128)S(1)}, u32[]{:S(2)}, u32[]{:S(2)}) collective-permute-start(f32[24,128]{1,0:T(8,128)S(1)} %get-tuple-element.39), channel_id=1, source_target_pairs={{0,4},{4,0},{1,5},{5,1},{2,6},{6,2},{3,7},{7,3},{8,12},{12,8},{9,1... | collective-permute-start | bytes 36872 | tf_op jit(solution)/shard_map/ppermute | solution.py:529
